TPU v7x, 128 devices: a whole 4x4x4 slice. The times are simulated.
128 devices in a mesh: row: 8 (over x, core), col: 16 (over y, z).
Axes of the slice: x: 4, y: 4, z: 4, core: 2. Of those that a mesh axis runs over, the one named last changes fastest.
Arguments:
- response_cache: bfloat16 [256, 256, 256], P('col'), may hold values from -128 to 128
- near_cache: bfloat16 [8, 256, 256], replicated, may hold values from -0.0073296421 to 0.0073296421
- lead_diag: float32 [512], replicated, may hold values from 0.25 to 2
- far_offsets: int32 [512, 24], P(('row', 'col')), may hold values from 0 to 255, as said below
- near_first: int32 [512, 24], P(('row', 'col')), may hold values from 0 to 7
- near_second: int32 [512, 24], P(('row', 'col')), may hold values from 0 to 7
- tile_counts: int32 [512], P(('row', 'col')), may hold values from 1 to 24, as said below
Outputs:
- lead_factor: float32 [512, 512], replicated
- far_factor: float32 [131072, 512], P(('row', 'col'))
Inputs may be any that keep to these rules, and one draw needn't show every extreme that they name: Slots at positions tile_counts[f] and above are unused; the last far tile uses all 24 slots. Among the slots of the 4 far tiles of one device, at most 8 have far_offsets // 16 equal to any one value, and exactly 8 for some value.
All inputs are finite; a program needn't handle non-finite values.
Results may differ from a plain program's by a relative error of at most 0.0003.
Values may be sent and summed in bfloat16 or wider, within the bound.
No kernel may reach another device: no remote copies, remote signals or barrier semaphores. Data moves between devices by JAX's collectives and lax.ppermute only.
A program may use at most 192 MiB of HBM per device.

v0:
```python
import functools

import jax
import jax.numpy as jnp
from jax import lax
from jax.experimental import pallas as pl
from jax.experimental.pallas import tpu as pltpu
from jax.sharding import PartitionSpec as P

HIGHEST = lax.Precision.HIGHEST
BLOCK = 128
GROUP = 4


def dot32(left, right):
    return jnp.dot(left, right, precision=HIGHEST, preferred_element_type=jnp.float32)


def spread_rows(value, row):
    return jnp.broadcast_to(value[row : row + 1, :], (8, BLOCK))


def factor_block(block):
    groups = BLOCK // 8
    sub = lax.broadcasted_iota(jnp.int32, (8, BLOCK), 0)
    lane = lax.broadcasted_iota(jnp.int32, (8, BLOCK), 1)
    main = [block[8 * g : 8 * g + 8, :] for g in range(groups)]
    side = [(lane == sub + 8 * g).astype(jnp.float32) for g in range(groups)]
    for panel in range(groups):
        start = 8 * panel
        cols = {
            (g, m): jnp.broadcast_to(main[g][:, start + m : start + m + 1], (8, BLOCK))
            for g in range(panel, groups)
            for m in range(8)
        }
        scale = jnp.ones((8, BLOCK), jnp.float32)
        for j in range(8):
            pivots = {m: spread_rows(cols[panel, m], j) for m in range(j, 8)}
            root = lax.rsqrt(pivots[j])
            root = root * (1.5 - 0.5 * pivots[j] * root * root)
            inverse = root * root
            scale = jnp.where(sub == j, root, scale)
            main_row = spread_rows(main[panel], j)
            side_row = spread_rows(side[panel], j)
            for g in range(panel, groups):
                ratio = cols[g, j] * inverse
                if g == panel:
                    ratio = jnp.where(sub > j, ratio, 0.0)
                for m in range(j + 1, 8):
                    cols[g, m] = cols[g, m] - ratio * pivots[m]
                main[g] = main[g] - ratio * main_row
                side[g] = side[g] - ratio * side_row
        main[panel] = main[panel] * scale
        side[panel] = side[panel] * scale
    for g in range(groups):
        main[g] = jnp.where(lane >= sub + 8 * g, main[g], 0.0)
        side[g] = jnp.where(lane <= sub + 8 * g, side[g], 0.0)
    return jnp.concatenate(main, axis=0), jnp.concatenate(side, axis=0)


def lead_kernel(pairs_ref, near_ref, turned_ref, diag_ref, factor_ref, inverse_ref, work, upper):
    near_total, size, _ = near_ref.shape
    whole = 2 * size
    first_sums = [sum(pairs_ref[j, k] for k in range(near_total)) for j in range(near_total)]
    second_sums = [sum(pairs_ref[j, k] for j in range(near_total)) for k in range(near_total)]
    work[...] = jnp.zeros_like(work)
    for j in range(near_total):
        left = turned_ref[j]
        mixed = jnp.zeros((size, size), jnp.float32)
        for k in range(near_total):
            product = jnp.dot(left, near_ref[k], preferred_element_type=jnp.float32)
            mixed = mixed + pairs_ref[j, k] * product
            if k == j:
                own = product
        work[:size, :size] += first_sums[j] * own
        work[size:, size:whole] += second_sums[j] * own
        work[:size, size:whole] += mixed
    rows = lax.broadcasted_iota(jnp.int32, (whole, whole), 0)
    columns = lax.broadcasted_iota(jnp.int32, (whole, whole), 1)
    same = rows == columns
    work[:, :whole] += jnp.where(same, jnp.broadcast_to(diag_ref[...], (whole, whole)), 0.0)
    work[:, whole:] = same.astype(jnp.float32)

    def step(b, carry):
        base = pl.multiple_of(b * BLOCK, BLOCK)
        own = pl.ds(base, BLOCK)
        _, turned = factor_block(work[own, own])
        solved = dot32(turned, work[own, :])
        at = columns[:BLOCK, :] >= base + rows[:BLOCK, :]
        solved_main = jnp.where(at, solved[:, :whole], 0.0)
        upper[own, :] = solved_main
        work[own, whole:] = solved[:, whole:]
        below = jnp.where(columns[:BLOCK, :] >= base + BLOCK, solved_main, 0.0)
        change = dot32(below.T, jnp.concatenate([below, solved[:, whole:]], axis=1))
        work[...] = work[...] - change
        return carry

    lax.fori_loop(0, whole // BLOCK, step, 0)
    factor_ref[...] = upper[...].T
    inverse_ref[...] = work[:, whole:].T


def lead(pairs, near_cache, turned_near, lead_diag):
    whole = lead_diag.shape[0]
    vmem = pl.BlockSpec(memory_space=pltpu.VMEM)
    return pl.pallas_call(
        lead_kernel,
        out_shape=(
            jax.ShapeDtypeStruct((whole, whole), jnp.float32),
            jax.ShapeDtypeStruct((whole, whole), jnp.float32),
        ),
        in_specs=[pl.BlockSpec(memory_space=pltpu.SMEM), vmem, vmem, vmem],
        out_specs=(vmem, vmem),
        scratch_shapes=[
            pltpu.VMEM((whole, 2 * whole), jnp.float32),
            pltpu.VMEM((whole, whole), jnp.float32),
        ],
        compiler_params=pltpu.CompilerParams(vmem_limit_bytes=40 << 20),
        name="lead",
    )(pairs, near_cache, turned_near, lead_diag.reshape(1, whole))


def far_kernel(
    counts_ref, offsets_ref, first_ref, second_ref, blocks_ref, turned_ref, inverse_ref, out_ref,
    held, total, arrived,
):
    tiles, slots = offsets_ref.shape
    size = turned_ref.shape[1]
    tile = pl.program_id(0)
    rounds = slots // GROUP
    empty = turned_ref.shape[0] - 1

    def fetch(t, s):
        return pltpu.make_async_copy(
            blocks_ref.at[offsets_ref[t, s]],
            held.at[t, pl.ds(pl.multiple_of(s * size, size), size), :],
            arrived.at[t, s],
        )

    def rounds_of(t):
        return (counts_ref[t] + GROUP - 1) // GROUP

    @pl.when(tile == 0)
    def start():
        for t in range(tiles):
            def begin(s, carry):
                fetch(t, s).start()
                return carry

            lax.fori_loop(0, rounds_of(t) * GROUP, begin, 0)

    total[...] = jnp.zeros_like(total)

    def one_round(r, carry):
        for i in range(GROUP):
            fetch(tile, r * GROUP + i).wait()
        firsts = []
        seconds = []
        for i in range(GROUP):
            s = r * GROUP + i
            used = s < counts_ref[tile]
            firsts.append(turned_ref[jnp.where(used, first_ref[tile, s], empty)])
            seconds.append(turned_ref[jnp.where(used, second_ref[tile, s], empty)])
        left = jnp.concatenate(
            [jnp.concatenate(firsts, axis=1), jnp.concatenate(seconds, axis=1)], axis=0
        )
        span = GROUP * size
        right = held[tile, pl.ds(pl.multiple_of(r * span, span), span), :]
        total[...] += jnp.dot(left, right, preferred_element_type=jnp.float32)
        return carry

    lax.fori_loop(0, rounds_of(tile), one_round, 0)
    turned = total[...].T
    out_ref[:, :size] = dot32(turned[:, :size], inverse_ref[:size, :size])
    out_ref[:, size:] = dot32(turned, inverse_ref[:, size:])


def far(counts, offsets, near_first, near_second, blocks, turned_near, inverse):
    tiles, slots = offsets.shape
    size = blocks.shape[1]
    whole = lambda *shape: pl.BlockSpec(shape, lambda t, *_: (0,) * len(shape))
    return pl.pallas_call(
        far_kernel,
        out_shape=jax.ShapeDtypeStruct((tiles * size, 2 * size), jnp.float32),
        grid_spec=pltpu.PrefetchScalarGridSpec(
            num_scalar_prefetch=4,
            grid=(tiles,),
            in_specs=[
                pl.BlockSpec(memory_space=pl.ANY),
                whole(*turned_near.shape),
                whole(*inverse.shape),
            ],
            out_specs=pl.BlockSpec((size, 2 * size), lambda t, *_: (t, 0)),
            scratch_shapes=[
                pltpu.VMEM((tiles, slots * size, size), jnp.bfloat16),
                pltpu.VMEM((2 * size, size), jnp.float32),
                pltpu.SemaphoreType.DMA((tiles, slots)),
            ],
        ),
        compiler_params=pltpu.CompilerParams(
            dimension_semantics=("arbitrary",), vmem_limit_bytes=40 << 20
        ),
        name="far",
    )(counts, offsets, near_first, near_second, blocks, turned_near, inverse)


def local_pairs(near_first, near_second, counts, near_total):
    slots = near_first.shape[1]
    usable = jnp.arange(slots, dtype=jnp.int32)[None, :] < counts[:, None]
    labels = jnp.arange(near_total, dtype=jnp.int32)
    first_hot = (near_first[:, :, None] == labels) & usable[:, :, None]
    second_hot = near_second[:, :, None] == labels
    both = first_hot[:, :, :, None] & second_hot[:, :, None, :]
    return jnp.sum(both.astype(jnp.float32), axis=(0, 1))


def total_pairs(value):
    for axis, bits in (("row", (1, 4, 2)), ("col", (8, 4, 2, 1))):
        size = lax.axis_size(axis)
        for bit in bits:
            value = value + lax.ppermute(value, axis, [(i, i ^ bit) for i in range(size)])
    return value


def shards(
    response_cache, near_cache, lead_diag, far_offsets, near_first, near_second, tile_counts
):
    near_total = near_cache.shape[0]
    share = response_cache.shape[0] // lax.axis_size("row")
    own = lax.dynamic_slice_in_dim(response_cache, lax.axis_index("row") * share, share, 0)
    blocks = lax.all_gather(own, ("col", "row"), axis=0, tiled=True)
    pairs = total_pairs(local_pairs(near_first, near_second, tile_counts, near_total))
    turned = jnp.transpose(near_cache, (0, 2, 1))
    padded = jnp.concatenate([turned, jnp.zeros_like(turned[:1])], axis=0)
    lead_factor, inverse = lead(pairs, near_cache, turned, lead_diag)
    far_factor = far(
        tile_counts, far_offsets, near_first, near_second, blocks, padded, inverse
    )
    return lead_factor, far_factor


def solution(mesh):
    return jax.shard_map(
        shards,
        mesh=mesh,
        in_specs=(
            P("col", None, None),
            P(),
            P(),
            P(("row", "col"), None),
            P(("row", "col"), None),
            P(("row", "col"), None),
            P(("row", "col")),
        ),
        out_specs=(P(), P(("row", "col"), None)),
        check_vma=False,
    )
```

profile of v0, /device:TPU:7, one launch (start us, length us, event | category | flops | bytes accessed | tf_op | source)
XLA Modules:
  0.0 145.1 jit_solution(7666231255697062958)
XLA Ops:
  7.2 0.0 copy-start
  7.2 0.0 all-gather.2.cloned.1.call-start
  7.2 1.5 %copy-done = bf16[16,256,256]{2,1,0:T(8,128)(2,1)S(1)} copy-done((bf16[16,256,256]{2,1,0:T(8,128)(2,1)S(1)}, bf16[16,256,256]{2,1,0:T(8,128)(2,1)}, u32[]{:S(2)}) %copy-start) | copy-done | bytes 2097176
  8.8 0.7 constant_dynamic-slice_fusion
  9.5 0.0 all-gather.2.cloned.1.call-update
  9.5 0.7 iota_compare_fusion.2
  10.2 0.7 iota_compare_fusion
  10.9 0.1 convert_reduce_fusion
  11.1 0.8 collective-permute-start
  11.8 0.8 collective-permute-done
  12.6 1.1 collective-permute-start.1
  13.8 2.8 %collective-permute-done.1 = f32[8,8]{1,0:T(8,128)S(1)} collective-permute-done((f32[8,8]{1,0:T(8,128)S(1)}, f32[8,8]{1,0:T(8,128)S(1)}, u32[]{:S(2)}, u32[]{:S(2)}) %collective-permute-start.1) | collective-permute-done | bytes 288 | tf_op jit(solution)/shard_map/ppermute | solution.py:221
  16.6 0.5 collective-permute-start.2
  17.1 1.9 %collective-permute-done.2 = f32[8,8]{1,0:T(8,128)S(1)} collective-permute-done((f32[8,8]{1,0:T(8,128)S(1)}, f32[8,8]{1,0:T(8,128)S(1)}, u32[]{:S(2)}, u32[]{:S(2)}) %collective-permute-start.2) | collective-permute-done | bytes 288 | tf_op jit(solution)/shard_map/ppermute | solution.py:221
  19.1 2.9 %collective-permute-start.3 = (f32[8,8]{1,0:T(8,128)S(1)}, f32[8,8]{1,0:T(8,128)S(1)}, u32[]{:S(2)}, u32[]{:S(2)}) collective-permute-start(f32[8,8]{1,0:T(8,128)S(1)} %add.28), channel_id=1, source_target_pairs={{0,8},{1,9},{2,10},{3,11},{4,12},{5,13},{6,14},{7,15},{8,0},{9,1},... | collective-permute-start | bytes 776 | tf_op jit(solution)/shard_map/ppermute | solution.py:221
  22.0 1.0 collective-permute-done.3
  23.0 1.3 collective-permute-start.4
  24.3 1.6 %collective-permute-done.4 = f32[8,8]{1,0:T(8,128)S(1)} collective-permute-done((f32[8,8]{1,0:T(8,128)S(1)}, f32[8,8]{1,0:T(8,128)S(1)}, u32[]{:S(2)}, u32[]{:S(2)}) %collective-permute-start.4) | collective-permute-done | bytes 288 | tf_op jit(solution)/shard_map/ppermute | solution.py:221
  25.9 3.6 %collective-permute-start.5 = (f32[8,8]{1,0:T(8,128)S(1)}, f32[8,8]{1,0:T(8,128)S(1)}, u32[]{:S(2)}, u32[]{:S(2)}) collective-permute-start(f32[8,8]{1,0:T(8,128)S(1)} %add.30), channel_id=1, source_target_pairs={{0,2},{1,3},{2,0},{3,1},{4,6},{5,7},{6,4},{7,5},{8,10},{9,11},{10,... | collective-permute-start | bytes 776 | tf_op jit(solution)/shard_map/ppermute | solution.py:221
  29.5 1.0 collective-permute-done.5
  30.5 0.0 copy-start.7
  30.5 1.0 collective-permute-start.6
  31.5 1.5 %copy.11 = bf16[8,256,256]{1,2,0:T(8,128)(2,1)S(1)} copy(bf16[8,256,256]{2,1,0:T(8,128)(2,1)} %near_ref.1) | data formatting | bytes 2097152 | tf_op args[1]
  33.0 0.0 copy-start.2
  33.0 0.0 copy-start.5
  33.0 0.0 copy-start.6
  33.0 0.0 copy-start.8
  33.0 0.0 copy-start.9
  33.0 1.1 concatenate.3.turned_ref
  34.1 0.0 collective-permute-done.6
  34.1 0.0 copy-done.7
  34.1 0.5 copy-done.2
  34.6 34.6 %lead.1 = (f32[512,512]{1,0:T(8,128)}, f32[512,512]{1,0:T(8,128)S(1)}) custom-call(f32[8,8]{1,0:T(8,128)S(1)} %add.32.pairs_ref, bf16[8,256,256]{2,1,0:T(8,128)(2,1)S(1)} %copy-done.2, bf16[8,256,256]{2,1,0:T(8,128)(2,1)S(1)} %bitcast.3, f32[1,512]{1,0:T(1,128)S(1)} %bitcast.4), custom_call_target="tpu_custom_call" | custom-call | tf_op jit(solution)/shard_map/lead/pallas_call | solution.py:106
  69.2 0.0 copy-start.3
  69.2 1.0 copy-done.3
  70.2 50.0 %all-gather.2.cloned.1.call-done.blocks_ref = bf16[256,256,256]{2,1,0:T(8,128)(2,1)} async-done(((bf16[2,256,256]{2,1,0:T(8,128)(2,1)}), bf16[256,256,256]{2,1,0:T(8,128)(2,1)}) %all-gather.2.cloned.1.call-update) | async-done | bytes 33554448 | tf_op jit(solution)/shard_map/all_gather | solution.py:231
  120.2 0.0 copy-done.5
  120.2 0.0 copy-done.6
  120.2 0.0 copy-done.8
  120.2 0.0 copy-done.9
  120.2 0.0 copy-start.1
  120.2 1.3 copy-done.1
  121.5 0.0 copy-start.4
  121.5 1.2 copy-done.4
  122.7 15.6 %far.1 = f32[1024,512]{1,0:T(8,128)} custom-call(s32[4]{0:T(128)S(1)} %copy-done.9, s32[4,24]{1,0:T(4,128)S(1)} %copy-done.8, s32[4,24]{1,0:T(4,128)S(1)} %copy-done.6, s32[4,24]{1,0:T(4,128)S(1)} %copy-done.5, bf16[256,256,256]{2,1,0:T(8,128)(2,1)} %all-gather.2.cloned.1.call-done.blocks_ref, bf16[9,256,256]{2,1,0:T(8,128)(2,1)S(1)} %copy-done.1, ...), custom_call_target="tpu_custom_call" | custom-call | tf_op jit(solution)/shard_map/far/pallas_call | solution.py:182
  (7 shorter events, 0.0 us)
Async XLA Ops:
  7.2 1.6 %copy-start = (bf16[16,256,256]{2,1,0:T(8,128)(2,1)S(1)}, bf16[16,256,256]{2,1,0:T(8,128)(2,1)}, u32[]{:S(2)}) copy-start(bf16[16,256,256]{2,1,0:T(8,128)(2,1)} %param.7) | copy-start | bytes 6291460
  7.2 113.0 %all-gather.2.cloned.1.call-start = ((), (), s32[]{:S(2)}) async-start(), calls=%async_computation | async-start | bytes 33816576 | tf_op jit(solution)/shard_map/all_gather | solution.py:231
  11.1 1.6 %collective-permute-start = (f32[8,8]{1,0:T(8,128)S(1)}, f32[8,8]{1,0:T(8,128)S(1)}, u32[]{:S(2)}, u32[]{:S(2)}) collective-permute-start(f32[8,8]{1,0:T(8,128)S(1)} %convert_reduce_fusion), channel_id=1, source_target_pairs={{0,16},{16,0},{32,48},{48,32},{64,80},{80,64},{96,112},{112,96},{1... | collective-permute-start | bytes 776 | tf_op jit(solution)/shard_map/ppermute | solution.py:221
  12.6 4.0 %collective-permute-start.1 = (f32[8,8]{1,0:T(8,128)S(1)}, f32[8,8]{1,0:T(8,128)S(1)}, u32[]{:S(2)}, u32[]{:S(2)}) collective-permute-start(f32[8,8]{1,0:T(8,128)S(1)} %add.26), channel_id=1, source_target_pairs={{0,64},{16,80},{32,96},{48,112},{64,0},{80,16},{96,32},{112,48},{1... | collective-permute-start | bytes 776 | tf_op jit(solution)/shard_map/ppermute | solution.py:221
  16.6 2.5 %collective-permute-start.2 = (f32[8,8]{1,0:T(8,128)S(1)}, f32[8,8]{1,0:T(8,128)S(1)}, u32[]{:S(2)}, u32[]{:S(2)}) collective-permute-start(f32[8,8]{1,0:T(8,128)S(1)} %add.27), channel_id=1, source_target_pairs={{0,32},{16,48},{32,0},{48,16},{64,96},{80,112},{96,64},{112,80},{1... | collective-permute-start | bytes 776 | tf_op jit(solution)/shard_map/ppermute | solution.py:221
  19.1 4.0 %collective-permute-start.3 = (f32[8,8]{1,0:T(8,128)S(1)}, f32[8,8]{1,0:T(8,128)S(1)}, u32[]{:S(2)}, u32[]{:S(2)}) collective-permute-start(f32[8,8]{1,0:T(8,128)S(1)} %add.28), channel_id=1, source_target_pairs={{0,8},{1,9},{2,10},{3,11},{4,12},{5,13},{6,14},{7,15},{8,0},{9,1},... | collective-permute-start | bytes 776 | tf_op jit(solution)/shard_map/ppermute | solution.py:221
  23.0 2.9 %collective-permute-start.4 = (f32[8,8]{1,0:T(8,128)S(1)}, f32[8,8]{1,0:T(8,128)S(1)}, u32[]{:S(2)}, u32[]{:S(2)}) collective-permute-start(f32[8,8]{1,0:T(8,128)S(1)} %add.29), channel_id=1, source_target_pairs={{0,4},{1,5},{2,6},{3,7},{4,0},{5,1},{6,2},{7,3},{8,12},{9,13},{10,... | collective-permute-start | bytes 776 | tf_op jit(solution)/shard_map/ppermute | solution.py:221
  25.9 4.6 %collective-permute-start.5 = (f32[8,8]{1,0:T(8,128)S(1)}, f32[8,8]{1,0:T(8,128)S(1)}, u32[]{:S(2)}, u32[]{:S(2)}) collective-permute-start(f32[8,8]{1,0:T(8,128)S(1)} %add.30), channel_id=1, source_target_pairs={{0,2},{1,3},{2,0},{3,1},{4,6},{5,7},{6,4},{7,5},{8,10},{9,11},{10,... | collective-permute-start | bytes 776 | tf_op jit(solution)/shard_map/ppermute | solution.py:221
  30.5 3.7 %copy-start.7 = (f32[512]{0:T(512)S(1)}, f32[512]{0:T(512)}, u32[]{:S(2)}) copy-start(f32[512]{0:T(512)} %param.9) | copy-start | bytes 6148
  30.5 3.6 %collective-permute-start.6 = (f32[8,8]{1,0:T(8,128)S(1)}, f32[8,8]{1,0:T(8,128)S(1)}, u32[]{:S(2)}, u32[]{:S(2)}) collective-permute-start(f32[8,8]{1,0:T(8,128)S(1)} %add.31), channel_id=1, source_target_pairs={{0,1},{1,0},{2,3},{3,2},{4,5},{5,4},{6,7},{7,6},{8,9},{9,8},{10,11... | collective-permute-start | bytes 776 | tf_op jit(solution)/shard_map/ppermute | solution.py:221
  33.0 1.7 %copy-start.2 = (bf16[8,256,256]{2,1,0:T(8,128)(2,1)S(1)}, bf16[8,256,256]{2,1,0:T(8,128)(2,1)}, u32[]{:S(2)}) copy-start(bf16[8,256,256]{2,1,0:T(8,128)(2,1)} %near_ref.1) | copy-start | bytes 3145732
  33.0 87.2 %copy-start.5 = (s32[4,24]{1,0:T(4,128)S(1)}, s32[4,24]{1,0:T(4,128)}, u32[]{:S(2)}) copy-start(s32[4,24]{1,0:T(4,128)} %second_ref.1) | copy-start | bytes 1156
  33.0 87.2 %copy-start.6 = (s32[4,24]{1,0:T(4,128)S(1)}, s32[4,24]{1,0:T(4,128)}, u32[]{:S(2)}) copy-start(s32[4,24]{1,0:T(4,128)} %first_ref.1) | copy-start | bytes 1156
  33.0 87.2 %copy-start.8 = (s32[4,24]{1,0:T(4,128)S(1)}, s32[4,24]{1,0:T(4,128)}, u32[]{:S(2)}) copy-start(s32[4,24]{1,0:T(4,128)} %offsets_ref.1) | copy-start | bytes 1156
  33.0 87.2 %copy-start.9 = (s32[4]{0:T(128)S(1)}, s32[4]{0:T(128)}, u32[]{:S(2)}) copy-start(s32[4]{0:T(128)} %counts_ref.1) | copy-start | bytes 52
  69.2 1.0 copy-start.3
  120.2 1.3 copy-start.1
  121.5 1.2 copy-start.4
Sparse Core Ops, SparseCore 0:
  11.0 109.1 all-gather.1
where the time goes:
time: 145 us
  waiting for transfers between devices  59.1 us (41%)
  Pallas kernels  50.1 us (35%)
  between operations  14.1 us (10%)
  starting transfers between devices  11.3 us (8%)
  local copies, waits for them, and re-layouts  8.85 us (6%)
  other arithmetic  1.57 us (1%)
    all_gather x1, waiting for transfers between devices, shards(): blocks = lax.all_gather(own, ('col', 'row'), axis=0, tiled=True)  50 us
    pallas_call x1, Pallas kernels, lead(): pl.pallas_call(lead_kernel, out_shape=(jax.ShapeDtypeStruct((whole, whole...  34.6 us
    pallas_call x1, Pallas kernels, far(): pl.pallas_call(far_kernel, out_shape=jax.ShapeDtypeStruct((tiles * size,...  15.6 us
    ppermute x7, starting transfers between devices, total_pairs(): lax.ppermute(value, axis, [(i, i ^ bit) for i in range(size)])  11.2 us
    ppermute x7, waiting for transfers between devices, total_pairs(): lax.ppermute(value, axis, [(i, i ^ bit) for i in range(size)])  9.17 us
    unnamed x21, local copies, waits for them, and re-layouts  7.04 us
  transfers between devices with their start and end apart: 8, of which 7 were waited for; matrix products, arithmetic and copies ran while one was open for 3% of the time, Pallas kernels for 24%

commit v1 on v0

v1 whole, which is shorter than its diff:
```python
import functools

import jax
import jax.numpy as jnp
from jax import lax
from jax.experimental import pallas as pl
from jax.experimental.pallas import tpu as pltpu
from jax.sharding import PartitionSpec as P

HIGHEST = lax.Precision.HIGHEST
BLOCK = 128
GROUP = 4
SIDE = 4
CACHED = 16
HALF = CACHED // 2
RING = 2


def dot32(left, right):
    return jnp.dot(left, right, precision=HIGHEST, preferred_element_type=jnp.float32)


def spread_rows(value, row):
    return jnp.broadcast_to(value[row : row + 1, :], (8, BLOCK))


def factor_block(block):
    groups = BLOCK // 8
    sub = lax.broadcasted_iota(jnp.int32, (8, BLOCK), 0)
    lane = lax.broadcasted_iota(jnp.int32, (8, BLOCK), 1)
    main = [block[8 * g : 8 * g + 8, :] for g in range(groups)]
    side = [(lane == sub + 8 * g).astype(jnp.float32) for g in range(groups)]
    for panel in range(groups):
        start = 8 * panel
        cols = {
            (g, m): jnp.broadcast_to(main[g][:, start + m : start + m + 1], (8, BLOCK))
            for g in range(panel, groups)
            for m in range(8)
        }
        scale = jnp.ones((8, BLOCK), jnp.float32)
        for j in range(8):
            pivots = {m: spread_rows(cols[panel, m], j) for m in range(j, 8)}
            root = lax.rsqrt(pivots[j])
            root = root * (1.5 - 0.5 * pivots[j] * root * root)
            inverse = root * root
            scale = jnp.where(sub == j, root, scale)
            main_row = spread_rows(main[panel], j)
            side_row = spread_rows(side[panel], j)
            for g in range(panel, groups):
                ratio = cols[g, j] * inverse
                if g == panel:
                    ratio = jnp.where(sub > j, ratio, 0.0)
                for m in range(j + 1, 8):
                    cols[g, m] = cols[g, m] - ratio * pivots[m]
                main[g] = main[g] - ratio * main_row
                side[g] = side[g] - ratio * side_row
        main[panel] = main[panel] * scale
        side[panel] = side[panel] * scale
    for g in range(groups):
        main[g] = jnp.where(lane >= sub + 8 * g, main[g], 0.0)
        side[g] = jnp.where(lane <= sub + 8 * g, side[g], 0.0)
    return jnp.concatenate(main, axis=0), jnp.concatenate(side, axis=0)


def factor_steps(work, upper, begin, end):
    whole = upper.shape[0]
    rows = lax.broadcasted_iota(jnp.int32, (BLOCK, whole), 0)
    columns = lax.broadcasted_iota(jnp.int32, (BLOCK, whole), 1)

    def step(b, carry):
        base = pl.multiple_of(b * BLOCK, BLOCK)
        own = pl.ds(base, BLOCK)
        _, turned = factor_block(work[own, own])
        solved = dot32(turned, work[own, :])
        solved_main = jnp.where(columns >= base + rows, solved[:, :whole], 0.0)
        upper[own, :] = solved_main
        work[own, whole:] = solved[:, whole:]
        below = jnp.where(columns >= base + BLOCK, solved_main, 0.0)
        change = dot32(below.T, jnp.concatenate([below, solved[:, whole:]], axis=1))
        work[...] = work[...] - change
        return carry

    lax.fori_loop(begin, end, step, 0)


def lead_start_kernel(pairs_ref, near_ref, turned_ref, diag_ref, work, upper):
    near_total, size, _ = near_ref.shape
    whole = 2 * size
    first_sums = [sum(pairs_ref[j, k] for k in range(near_total)) for j in range(near_total)]
    second_sums = [sum(pairs_ref[j, k] for j in range(near_total)) for k in range(near_total)]
    work[...] = jnp.zeros_like(work)
    for j in range(near_total):
        left = turned_ref[j]
        mixed = jnp.zeros((size, size), jnp.float32)
        for k in range(near_total):
            product = jnp.dot(left, near_ref[k], preferred_element_type=jnp.float32)
            mixed = mixed + pairs_ref[j, k] * product
            if k == j:
                own = product
        work[:size, :size] += first_sums[j] * own
        work[size:, size:whole] += second_sums[j] * own
        work[:size, size:whole] += mixed
    rows = lax.broadcasted_iota(jnp.int32, (whole, whole), 0)
    columns = lax.broadcasted_iota(jnp.int32, (whole, whole), 1)
    same = rows == columns
    work[:, :whole] += jnp.where(same, jnp.broadcast_to(diag_ref[...], (whole, whole)), 0.0)
    work[:, whole:] = same.astype(jnp.float32)
    factor_steps(work, upper, 0, size // BLOCK)


def lead_end_kernel(work_ref, upper_ref, factor_ref, inverse_ref, work, upper):
    whole = upper.shape[0]
    half = whole // 2
    work[...] = work_ref[...]
    upper[:half, :] = upper_ref[:half, :]
    factor_steps(work, upper, half // BLOCK, whole // BLOCK)
    factor_ref[...] = upper[...].T
    inverse_ref[...] = work[:, whole:].T


VMEM = pl.BlockSpec(memory_space=pltpu.VMEM)


def lead_start(pairs, near_cache, turned_near, lead_diag):
    whole = lead_diag.shape[0]
    return pl.pallas_call(
        lead_start_kernel,
        out_shape=(
            jax.ShapeDtypeStruct((whole, 2 * whole), jnp.float32),
            jax.ShapeDtypeStruct((whole, whole), jnp.float32),
        ),
        in_specs=[pl.BlockSpec(memory_space=pltpu.SMEM), VMEM, VMEM, VMEM],
        out_specs=(VMEM, VMEM),
        compiler_params=pltpu.CompilerParams(vmem_limit_bytes=24 << 20),
        cost_estimate=pl.CostEstimate(
            flops=9_000_000_000, bytes_accessed=6 << 20, transcendentals=0
        ),
        name="lead_start",
    )(pairs, near_cache, turned_near, lead_diag.reshape(1, whole))


def lead_end(work, upper):
    whole = upper.shape[0]
    square = jax.ShapeDtypeStruct((whole, whole), jnp.float32)
    return pl.pallas_call(
        lead_end_kernel,
        out_shape=(square, square),
        in_specs=[VMEM, VMEM],
        out_specs=(VMEM, VMEM),
        scratch_shapes=[
            pltpu.VMEM((whole, 2 * whole), jnp.float32),
            pltpu.VMEM((whole, whole), jnp.float32),
        ],
        compiler_params=pltpu.CompilerParams(vmem_limit_bytes=24 << 20),
        cost_estimate=pl.CostEstimate(
            flops=9_000_000_000, bytes_accessed=6 << 20, transcendentals=0
        ),
        name="lead_end",
    )(work, upper)


def position():
    row, col = lax.axis_index("row"), lax.axis_index("col")
    return row % 2, col // SIDE, col % SIDE


def ring_slot(offset, here):
    core, y, z = here
    col, local = offset // CACHED, offset % CACHED
    half, inner = local // HALF, local % HALF
    sign = 1 - 2 * core
    from_y = (sign * (y - col // SIDE)) & (SIDE - 1)
    from_z = (sign * (z - col % SIDE)) & (SIDE - 1)
    by_z = inner < RING
    major = jnp.where(by_z, from_z, from_y)
    minor = jnp.where(by_z, from_y, from_z)
    place = jnp.where(by_z, inner, inner - RING + SIDE * SIDE * RING)
    held = (half == core) & (inner < 2 * RING)
    return held, (major * SIDE + minor) * RING + place


def spread_slot(offset):
    col, local = offset // CACHED, offset % CACHED
    half, inner = local // HALF, local % HALF
    kept = HALF - 2 * RING
    return inner >= 2 * RING, col * (2 * kept) + half * kept + inner - 2 * RING


def list_slots(tile, slot_of, info_ref, items, slots):
    def visit(s, count):
        wanted, place = slot_of(info_ref[tile, s])
        items[0, tile, count] = place
        items[1, tile, count] = info_ref[tile, slots + s]
        items[2, tile, count] = info_ref[tile, 2 * slots + s]
        wanted = wanted & (s < info_ref[tile, 3 * slots])
        return count + wanted.astype(jnp.int32)

    return lax.fori_loop(0, slots, visit, 0)


def left_rows(tile, r, count, items, turned_ref):
    empty = turned_ref.shape[0] - 1
    firsts, seconds = [], []
    for i in range(GROUP):
        q = r * GROUP + i
        used = q < count
        firsts.append(turned_ref[jnp.where(used, items[1, tile, q], empty)])
        seconds.append(turned_ref[jnp.where(used, items[2, tile, q], empty)])
    return jnp.concatenate(
        [jnp.concatenate(firsts, axis=1), jnp.concatenate(seconds, axis=1)], axis=0
    )


def ring_kernel(slots, seeded, info_ref, *refs):
    if seeded:
        seed_ref, turned_ref = refs[:2]
        refs = refs[2:]
    else:
        turned_ref = refs[0]
        refs = refs[1:]
    *pieces, out_ref, held, items, arrived = refs
    size = turned_ref.shape[1]
    tile = pl.program_id(0)
    here = position()
    copies = []
    start = 0
    for n, piece in enumerate(pieces):
        copies.append(
            pltpu.make_async_copy(piece, held.at[pl.ds(start, piece.shape[0])], arrived.at[n])
        )
        start += piece.shape[0]

    @pl.when(tile == 0)
    def fetch():
        for copy in copies:
            copy.start()

    count = list_slots(tile, lambda offset: ring_slot(offset, here), info_ref, items, slots)

    @pl.when(tile == 0)
    def wait():
        for copy in copies:
            copy.wait()

    out_ref[...] = seed_ref[...] if seeded else jnp.zeros_like(out_ref)

    def one_round(r, carry):
        rights = []
        for i in range(GROUP):
            q = r * GROUP + i
            rights.append(held[jnp.where(q < count, items[0, tile, q], 0)])
        out_ref[0] += jnp.dot(
            left_rows(tile, r, count, items, turned_ref),
            jnp.concatenate(rights, axis=0),
            preferred_element_type=jnp.float32,
        )
        return carry

    lax.fori_loop(0, (count + GROUP - 1) // GROUP, one_round, 0)


def ring_sums(info, slots, turned_near, pieces, seed=None):
    tiles = info.shape[0]
    size = turned_near.shape[1]
    per_tile = pl.BlockSpec((1, 2 * size, size), lambda t, *_: (t, 0, 0))
    seeds = [] if seed is None else [seed]
    return pl.pallas_call(
        functools.partial(ring_kernel, slots, seed is not None),
        out_shape=jax.ShapeDtypeStruct((tiles, 2 * size, size), jnp.float32),
        grid_spec=pltpu.PrefetchScalarGridSpec(
            num_scalar_prefetch=1,
            grid=(tiles,),
            in_specs=[per_tile] * len(seeds)
            + [pl.BlockSpec(turned_near.shape, lambda t, *_: (0, 0, 0))]
            + [pl.BlockSpec(memory_space=pltpu.HBM)] * len(pieces),
            out_specs=per_tile,
            scratch_shapes=[
                pltpu.VMEM((sum(p.shape[0] for p in pieces), size, size), jnp.bfloat16),
                pltpu.SMEM((3, tiles, slots), jnp.int32),
                pltpu.SemaphoreType.DMA((len(pieces),)),
            ],
        ),
        compiler_params=pltpu.CompilerParams(
            dimension_semantics=("arbitrary",), vmem_limit_bytes=60 << 20
        ),
        cost_estimate=pl.CostEstimate(
            flops=3_000_000_000, bytes_accessed=12 << 20, transcendentals=0
        ),
        name="ring_sums",
    )(info, *seeds, turned_near, *pieces)


def far_kernel(
    slots, info_ref, sums_ref, blocks_ref, turned_hbm, inverse_hbm, out_hbm, held, total,
    turned_ref, inverse_ref, out_ref, items, arrived, loaded, stored,
):
    tiles = info_ref.shape[0]
    size = turned_ref.shape[1]
    span = GROUP * size

    def fetch(t, q, place):
        return pltpu.make_async_copy(
            blocks_ref.at[place],
            held.at[t, pl.ds(pl.multiple_of(q * size, size), size), :],
            arrived.at[t, q],
        )

    def store(t):
        return pltpu.make_async_copy(
            out_ref.at[t], out_hbm.at[pl.ds(t * size, size), :], stored.at[t]
        )

    load_turned = pltpu.make_async_copy(turned_hbm, turned_ref, loaded.at[0])
    load_sums = pltpu.make_async_copy(sums_ref, total, loaded.at[1])
    load_inverse = pltpu.make_async_copy(inverse_hbm, inverse_ref, loaded.at[2])
    load_turned.start()
    load_sums.start()
    counts = []
    for t in range(tiles):
        count = list_slots(t, spread_slot, info_ref, items, slots)
        counts.append(count)

        def begin(q, carry):
            fetch(t, q, jnp.where(q < count, items[0, t, q], 0)).start()
            return carry

        lax.fori_loop(0, (count + GROUP - 1) // GROUP * GROUP, begin, 0)
    load_inverse.start()
    load_turned.wait()
    load_sums.wait()
    for t in range(tiles):

        def one_round(r, carry):
            for i in range(GROUP):
                fetch(t, r * GROUP + i, 0).wait()
            right = held[t, pl.ds(pl.multiple_of(r * span, span), span), :]
            total[t] += jnp.dot(
                left_rows(t, r, counts[t], items, turned_ref),
                right,
                preferred_element_type=jnp.float32,
            )
            return carry

        lax.fori_loop(0, (counts[t] + GROUP - 1) // GROUP, one_round, 0)
        if t == 0:
            load_inverse.wait()
        turned = total[t].T
        out_ref[t, :, :size] = dot32(turned[:, :size], inverse_ref[:size, :size])
        out_ref[t, :, size:] = dot32(turned, inverse_ref[:, size:])
        store(t).start()
    for t in range(tiles):
        store(t).wait()


HBM = pl.BlockSpec(memory_space=pltpu.HBM)


def far(info, slots, sums, blocks, turned_near, inverse):
    tiles = info.shape[0]
    size = blocks.shape[1]
    return pl.pallas_call(
        functools.partial(far_kernel, slots),
        out_shape=jax.ShapeDtypeStruct((tiles * size, 2 * size), jnp.float32),
        in_specs=[pl.BlockSpec(memory_space=pltpu.SMEM), HBM, HBM, HBM, HBM],
        out_specs=HBM,
        scratch_shapes=[
            pltpu.VMEM((tiles, slots * size, size), jnp.bfloat16),
            pltpu.VMEM(sums.shape, jnp.float32),
            pltpu.VMEM(turned_near.shape, jnp.bfloat16),
            pltpu.VMEM(inverse.shape, jnp.float32),
            pltpu.VMEM((tiles, size, 2 * size), jnp.float32),
            pltpu.SMEM((3, tiles, slots), jnp.int32),
            pltpu.SemaphoreType.DMA((tiles, slots)),
            pltpu.SemaphoreType.DMA((3,)),
            pltpu.SemaphoreType.DMA((tiles,)),
        ],
        compiler_params=pltpu.CompilerParams(vmem_limit_bytes=63 << 20),
        name="far",
    )(info, sums, blocks, turned_near, inverse)


def local_pairs(near_first, near_second, counts, near_total):
    slots = near_first.shape[1]
    usable = jnp.arange(slots, dtype=jnp.int32)[None, :] < counts[:, None]
    labels = jnp.arange(near_total, dtype=jnp.int32)
    first_hot = (near_first[:, :, None] == labels) & usable[:, :, None]
    second_hot = near_second[:, :, None] == labels
    both = first_hot[:, :, :, None] & second_hot[:, :, None, :]
    return jnp.sum(both.astype(jnp.float32), axis=(0, 1))


def hop(value, along_y):
    rows, cols = lax.axis_size("row"), lax.axis_size("col")
    moves = []
    for row in range(rows):
        sign = 1 - 2 * (row % 2)
        for col in range(cols):
            y, z = col // SIDE, col % SIDE
            y, z = ((y + sign) % SIDE, z) if along_y else (y, (z + sign) % SIDE)
            moves.append((row * cols + col, row * cols + y * SIDE + z))
    return lax.ppermute(value, ("row", "col"), moves)


def swap(value, axis, bit):
    return lax.ppermute(value, axis, [(i, i ^ bit) for i in range(lax.axis_size(axis))])


def shards(
    response_cache, near_cache, lead_diag, far_offsets, near_first, near_second, tile_counts
):
    near_total = near_cache.shape[0]
    slots = far_offsets.shape[1]
    row = lax.axis_index("row")
    core = row % 2
    kept = HALF - 2 * RING
    share = 2 * kept // lax.axis_size("row")
    at = row * share
    own = lax.dynamic_slice_in_dim(
        response_cache, at // kept * HALF + 2 * RING + at % kept, share, 0
    )
    blocks = lax.all_gather(own, ("col", "row"), axis=0, tiled=True)
    line_y = [lax.dynamic_slice_in_dim(response_cache, core * HALF, RING, 0)]
    line_z = [lax.dynamic_slice_in_dim(response_cache, core * HALF + RING, RING, 0)]
    pairs = local_pairs(near_first, near_second, tile_counts, near_total)
    for stages in (
        (("row", 1), ("row", 4), ("row", 2)),
        (("col", 8), ("col", 4)),
        (("col", 2), ("col", 1)),
    ):
        line_y.append(hop(line_y[-1], True))
        line_z.append(hop(line_z[-1], False))
        for axis, bit in stages:
            pairs = pairs + swap(pairs, axis, bit)
        pairs, line_y[-1], line_z[-1] = lax.optimization_barrier((pairs, line_y[-1], line_z[-1]))
    info = jnp.concatenate([far_offsets, near_first, near_second, tile_counts[:, None]], axis=1)
    info_other = swap(info, "row", 1)
    turned = jnp.transpose(near_cache, (0, 2, 1))
    padded = jnp.concatenate([turned, jnp.zeros_like(turned[:1])], axis=0)
    by_z = [jnp.concatenate(line_y, axis=0)]
    by_y = [jnp.concatenate(line_z, axis=0)]
    pairs, by_z[0], by_y[0] = lax.optimization_barrier((pairs, by_z[0], by_y[0]))
    by_z.append(hop(by_z[0], False))
    by_y.append(hop(by_y[0], True))
    work, upper = lead_start(pairs, near_cache, turned, lead_diag)
    work, by_z[1], by_y[1] = lax.optimization_barrier((work, by_z[1], by_y[1]))
    by_z.append(hop(by_z[1], False))
    by_y.append(hop(by_y[1], True))
    lead_factor, inverse = lead_end(work, upper)
    inverse, by_z[2], by_y[2] = lax.optimization_barrier((inverse, by_z[2], by_y[2]))
    by_z.append(hop(by_z[2], False))
    by_y.append(hop(by_y[2], True))
    pieces = by_z + by_y
    sums_other = swap(ring_sums(info_other, slots, padded, pieces), "row", 1)
    sums = ring_sums(info, slots, padded, pieces, sums_other)
    far_factor = far(info, slots, sums, blocks, padded, inverse)
    return lead_factor, far_factor


def solution(mesh):
    return jax.shard_map(
        shards,
        mesh=mesh,
        in_specs=(
            P("col", None, None),
            P(),
            P(),
            P(("row", "col"), None),
            P(("row", "col"), None),
            P(("row", "col"), None),
            P(("row", "col")),
        ),
        out_specs=(P(), P(("row", "col"), None)),
        check_vma=False,
    )
```

time: 145 us -> 171 us (1.18)
  Pallas kernels: 50.1 us -> 72.5 us
  starting transfers between devices: 11.3 us -> 28.3 us
  waiting for transfers between devices: 59.1 us -> 46.8 us
  local copies, waits for them, and re-layouts: 8.85 us -> 6.74 us
    all_gather x1, waiting for transfers between devices: 50 us -> 0.02 us  [shards(): blocks = lax.all_gather(own, ('col', 'row'), axis=0, tiled=True)]
    ppermute x7 -> x21, waiting for transfers between devices: 9.17 us -> 46.8 us  [the longest x12 27.8 us: hop(): return lax.ppermute(value, ('row', 'col'), moves)]
    pallas_call x2 -> x5, Pallas kernels: 50.1 us -> 72.5 us  [the longest x2 23.2 us: ring_sums(): pl.pallas_call(functools.partial(ring_kernel, slots, seed is not None), o...]
    ppermute x7 -> x21, starting transfers between devices: 11.2 us -> 28.3 us  [the longest x12 18.5 us: hop(): return lax.ppermute(value, ('row', 'col'), moves)]
    unnamed x21 -> x27, local copies, waits for them, and re-layouts: 7.04 us -> 2.87 us
    dynamic_slice x1 -> x2, local copies, waits for them, and re-layouts: 0.72 us -> 2.65 us  [the longest x1 1.58 us: shards(): lax.dynamic_slice_in_dim(response_cache, at // kept * HALF + 2 * RING + a...]
  transfers between devices with their start and end apart: 8 -> 22, of which waited for: 7 -> 11; matrix products, arithmetic and copies ran while one was open for 3% -> 3% of each run, Pallas kernels for 24% -> 34%
where the time goes in v1:
time: 171 us; the launch traced here: 172 us
  Pallas kernels  72.5 us (42%)
  waiting for transfers between devices  46.8 us (27%)
  starting transfers between devices  28.3 us (17%)
  between operations  14.3 us (8%)
  local copies, waits for them, and re-layouts  6.74 us (4%)
  other arithmetic  2.88 us (2%)
    ppermute x12, waiting for transfers between devices, hop(): return lax.ppermute(value, ('row', 'col'), moves)  27.8 us
    pallas_call x2, Pallas kernels, ring_sums(): pl.pallas_call(functools.partial(ring_kernel, slots, seed is not None), o...  23.2 us
    ppermute x9, waiting for transfers between devices, swap(): lax.ppermute(value, axis, [(i, i ^ bit) for i in range(lax.axis_size(axis...  18.9 us
    ppermute x12, starting transfers between devices, hop(): return lax.ppermute(value, ('row', 'col'), moves)  18.5 us
    pallas_call x1, Pallas kernels, lead_start(): pl.pallas_call(lead_start_kernel, out_shape=(jax.ShapeDtypeStruct((whole,...  18.3 us
    pallas_call x1, Pallas kernels, lead_end(): pl.pallas_call(lead_end_kernel, out_shape=(square, square), in_specs=[VME...  16.6 us
    pallas_call x1, Pallas kernels, far(): pl.pallas_call(functools.partial(far_kernel, slots), out_shape=jax.ShapeD...  14.4 us
    ppermute x9, starting transfers between devices, swap(): lax.ppermute(value, axis, [(i, i ^ bit) for i in range(lax.axis_size(axis...  9.73 us
  transfers between devices with their start and end apart: 22, of which 11 were waited for; matrix products, arithmetic and copies ran while one was open for 3% of the time, Pallas kernels for 34%

profile of v1, /device:TPU:7, one launch (start us, length us, event | category | flops | bytes accessed | tf_op | source)
XLA Modules:
  0.0 171.6 jit_solution(18264602531929123017)
XLA Ops:
  7.2 0.0 all-gather.2.cloned.1.call-start
  7.2 1.6 constant_dynamic-slice_fusion
  8.8 0.0 all-gather.2.cloned.1.call-update
  8.9 1.1 constant_dynamic-slice_fusion.1
  9.9 2.8 %collective-permute-start.3 = (bf16[2,256,256]{2,1,0:T(8,128)(2,1)S(1)}, bf16[2,256,256]{2,1,0:T(8,128)(2,1)S(1)}, u32[]{:S(2)}, u32[]{:S(2)}) collective-permute-start(bf16[2,256,256]{2,1,0:T(8,128)(2,1)S(1)} %get-tuple-element.47), channel_id=1, source_target_pairs={{0,4},{1,5},{2,6},{3,7},{4,8},{5,9},{6,10},{7,11},{8,12},{9,13},{1... | collective-permute-start | bytes 786440 | tf_op jit(solution)/shard_map/ppermute | solution.py:401
  12.7 3.8 %collective-permute-start.4 = (bf16[2,256,256]{2,1,0:T(8,128)(2,1)S(1)}, bf16[2,256,256]{2,1,0:T(8,128)(2,1)S(1)}, u32[]{:S(2)}, u32[]{:S(2)}) collective-permute-start(bf16[2,256,256]{2,1,0:T(8,128)(2,1)S(1)} %get-tuple-element.46), channel_id=1, source_target_pairs={{0,1},{1,2},{2,3},{3,0},{4,5},{5,6},{6,7},{7,4},{8,9},{9,10},{10,1... | collective-permute-start | bytes 786440 | tf_op jit(solution)/shard_map/ppermute | solution.py:401
  16.5 0.7 iota_compare_fusion.2
  17.2 0.7 iota_compare_fusion
  17.9 0.1 convert_reduce_fusion
  18.0 0.1 collective-permute-start
  18.1 1.2 collective-permute-done
  19.3 1.1 collective-permute-start.1
  20.4 2.8 %collective-permute-done.1 = f32[8,8]{1,0:T(8,128)S(1)} collective-permute-done((f32[8,8]{1,0:T(8,128)S(1)}, f32[8,8]{1,0:T(8,128)S(1)}, u32[]{:S(2)}, u32[]{:S(2)}) %collective-permute-start.1) | collective-permute-done | bytes 288 | tf_op jit(solution)/shard_map/ppermute | solution.py:405
  23.3 0.5 collective-permute-start.2
  23.8 2.3 %collective-permute-done.2 = f32[8,8]{1,0:T(8,128)S(1)} collective-permute-done((f32[8,8]{1,0:T(8,128)S(1)}, f32[8,8]{1,0:T(8,128)S(1)}, u32[]{:S(2)}, u32[]{:S(2)}) %collective-permute-start.2) | collective-permute-done | bytes 288 | tf_op jit(solution)/shard_map/ppermute | solution.py:405
  26.1 0.0 collective-permute-done.3
  26.1 0.1 collective-permute-start.7
  26.3 0.1 collective-permute-start.8
  26.4 1.7 collective-permute-start.5
  28.1 2.3 %collective-permute-done.5 = f32[8,8]{1,0:T(8,128)S(1)} collective-permute-done((f32[8,8]{1,0:T(8,128)S(1)}, f32[8,8]{1,0:T(8,128)S(1)}, u32[]{:S(2)}, u32[]{:S(2)}) %collective-permute-start.5) | collective-permute-done | bytes 288 | tf_op jit(solution)/shard_map/ppermute | solution.py:405
  30.4 1.3 collective-permute-start.6
  31.6 1.6 collective-permute-done.6
  33.2 0.0 collective-permute-done.7
  33.2 0.0 collective-permute-done.8
  33.2 3.8 %collective-permute-start.11 = (bf16[2,256,256]{2,1,0:T(8,128)(2,1)S(1)}, bf16[2,256,256]{2,1,0:T(8,128)(2,1)S(1)}, u32[]{:S(2)}, u32[]{:S(2)}) collective-permute-start(bf16[2,256,256]{2,1,0:T(8,128)(2,1)S(1)} %collective-permute-done.7), channel_id=1, source_target_pairs={{0,4},{1,5},{2,6},{3,7},{4,8},{5,9},{6,10},{7,11},{8,12},{9,13},{1... | collective-permute-start | bytes 786440 | tf_op jit(solution)/shard_map/ppermute | solution.py:401
  37.0 0.0 collective-permute-start.12
  37.1 0.5 collective-permute-start.9
  37.5 3.5 %collective-permute-done.9 = f32[8,8]{1,0:T(8,128)S(1)} collective-permute-done((f32[8,8]{1,0:T(8,128)S(1)}, f32[8,8]{1,0:T(8,128)S(1)}, u32[]{:S(2)}, u32[]{:S(2)}) %collective-permute-start.9) | collective-permute-done | bytes 288 | tf_op jit(solution)/shard_map/ppermute | solution.py:405
  41.0 1.5 collective-permute-start.10
  42.5 1.3 collective-permute-done.10
  43.8 0.1 pad_maximum_fusion.refs_1_.refs_2_
  43.9 0.0 copy-start.2
  44.0 1.1 pad_maximum_fusion.1.refs_5_.refs_6_
  45.1 3.7 %collective-permute-start.13 = (bf16[8,256,256]{2,1,0:T(8,128)(2,1)S(1)}, bf16[8,256,256]{2,1,0:T(8,128)(2,1)}, u32[]{:S(2)}, u32[]{:S(2)}) collective-permute-start(bf16[8,256,256]{2,1,0:T(8,128)(2,1)S(1)} %pad_maximum_fusion.refs_1_.refs_2_), channel_id=1, source_target_pairs={{0,1},{1,2},{2,3},{3,0},{4,5},{5,6},{6,7},{7,4},{8,9},{9,10},{10,1... | collective-permute-start | bytes 3145736 | tf_op jit(solution)/shard_map/ppermute | solution.py:401
  48.8 0.1 collective-permute-start.14
  48.9 0.5 copy.13
  49.4 18.3 %lead_start.1 = (f32[512,1024]{1,0:T(8,128)S(1)}, f32[512,512]{1,0:T(8,128)S(1)}) custom-call(f32[8,8]{1,0:T(8,128)S(1)} %add.61.pairs_ref, bf16[8,256,256]{2,1,0:T(8,128)(2,1)S(1)} %copy-done.1, bf16[8,256,256]{2,1,0:T(8,128)(2,1)S(1)} %bitcast.3, f32[1,512]{1,0:T(1,128)S(1)} %bitcast.5), custom_call_target="tpu_custom_call" | custom-call | flops 8999999488 | bytes 6291456 | tf_op jit(solution)/shard_map/lead_start/pallas_call | solution.py:126
  67.7 0.0 collective-permute-done.13.refs_2_.refs_3_
  67.8 0.0 collective-permute-done.14.refs_6_.refs_7_
  67.8 0.2 collective-permute-start.16
  68.0 0.2 collective-permute-start.17
  68.2 0.0 copy-start.12
  68.2 0.0 copy-start.8
  68.2 0.0 copy-start.9
  68.2 0.0 copy-start.11
  68.2 16.6 %lead_end.1 = (f32[512,512]{1,0:T(8,128)}, f32[512,512]{1,0:T(8,128)S(1)}) custom-call(f32[512,1024]{1,0:T(8,128)S(1)} %get-tuple-element.37.work_ref, f32[512,512]{1,0:T(8,128)S(1)} %get-tuple-element.38.upper_ref), custom_call_target="tpu_custom_call" | custom-call | flops 8999999488 | bytes 6291456 | tf_op jit(solution)/shard_map/lead_end/pallas_call | solution.py:145
  84.8 1.0 copy-done
  85.8 16.6 %collective-permute-done.16.refs_3_.refs_4_ = bf16[8,256,256]{2,1,0:T(8,128)(2,1)S(1)} collective-permute-done((bf16[8,256,256]{2,1,0:T(8,128)(2,1)}, bf16[8,256,256]{2,1,0:T(8,128)(2,1)S(1)}, u32[]{:S(2)}, u32[]{:S(2)}) %collective-permute-start.16) | collective-permute-done | bytes 1048608 | tf_op jit(solution)/shard_map/ppermute | solution.py:401
  102.4 2.2 %collective-permute-start.18 = (bf16[8,256,256]{2,1,0:T(8,128)(2,1)S(1)}, bf16[8,256,256]{2,1,0:T(8,128)(2,1)}, u32[]{:S(2)}, u32[]{:S(2)}) collective-permute-start(bf16[8,256,256]{2,1,0:T(8,128)(2,1)S(1)} %collective-permute-done.16.refs_3_.refs_4_), channel_id=1, source_target_pairs={{0,1},{1,2},{2,3},{3,0},{4,5},{5,6},{6,7},{7,4},{8,9},{9,10},{10,1... | collective-permute-start | bytes 3145736 | tf_op jit(solution)/shard_map/ppermute | solution.py:401
  104.6 1.5 collective-permute-start.19
  106.1 0.1 copy.14
  106.2 0.1 pad_add_fusion.info_ref
  106.2 0.0 collective-permute-start.15
  106.3 1.1 concatenate.15.refs_0_.refs_1_.turned_hbm
  107.4 0.0 collective-permute-done.15.info_ref
  107.4 9.0 %collective-permute-done.18.refs_4_.refs_5_ = bf16[8,256,256]{2,1,0:T(8,128)(2,1)} collective-permute-done((bf16[8,256,256]{2,1,0:T(8,128)(2,1)S(1)}, bf16[8,256,256]{2,1,0:T(8,128)(2,1)}, u32[]{:S(2)}, u32[]{:S(2)}) %collective-permute-start.18) | collective-permute-done | bytes 1048608 | tf_op jit(solution)/shard_map/ppermute | solution.py:401
  116.5 2.2 %collective-permute-done.19.refs_8_.refs_9_ = bf16[8,256,256]{2,1,0:T(8,128)(2,1)} collective-permute-done((bf16[8,256,256]{2,1,0:T(8,128)(2,1)S(1)}, bf16[8,256,256]{2,1,0:T(8,128)(2,1)}, u32[]{:S(2)}, u32[]{:S(2)}) %collective-permute-start.19) | collective-permute-done | bytes 1048608 | tf_op jit(solution)/shard_map/ppermute | solution.py:401
  118.7 11.1 %ring_sums.2 = f32[4,512,256]{2,1,0:T(8,128)} custom-call(s32[4,73]{1,0:T(4,128)} %copy-done.10, bf16[9,256,256]{2,1,0:T(8,128)(2,1)} %concatenate.15.refs_0_.refs_1_.turned_hbm, bf16[8,256,256]{2,1,0:T(8,128)(2,1)} %copy-done.3, bf16[8,256,256]{2,1,0:T(8,128)(2,1)} %collective-permute-done.13.refs_2_.refs_3_, bf16[8,256,256]{2,1,0:T(8,128)(2,1)} %copy-done.4, ...), custom_call_target="tpu_custom_call" | custom-call | flops 3000000000 | bytes 12582912 | tf_op jit(solution)/shard_map/ring_sums/pallas_call | solution.py:267
  129.8 3.0 %collective-permute-start.20 = (f32[4,512,256]{2,1,0:T(8,128)}, f32[4,512,256]{2,1,0:T(8,128)S(1)}, u32[]{:S(2)}, u32[]{:S(2)}) collective-permute-start(f32[4,512,256]{2,1,0:T(8,128)} %ring_sums.2), channel_id=1, source_target_pairs={{0,16},{16,0},{32,48},{48,32},{64,80},{80,64},{96,112},{112,96},{1... | collective-permute-start | bytes 6291464 | tf_op jit(solution)/shard_map/ppermute | solution.py:405
  132.8 4.0 %collective-permute-done.20.refs_0_ = f32[4,512,256]{2,1,0:T(8,128)S(1)} collective-permute-done((f32[4,512,256]{2,1,0:T(8,128)}, f32[4,512,256]{2,1,0:T(8,128)S(1)}, u32[]{:S(2)}, u32[]{:S(2)}) %collective-permute-start.20) | collective-permute-done | bytes 2097184 | tf_op jit(solution)/shard_map/ppermute | solution.py:405
  136.8 1.3 copy-done.6
  138.1 12.2 %ring_sums.3.sums_ref = f32[4,512,256]{2,1,0:T(8,128)} custom-call(s32[4,73]{1,0:T(4,128)} %copy-done.7, f32[4,512,256]{2,1,0:T(8,128)} %copy-done.6, bf16[9,256,256]{2,1,0:T(8,128)(2,1)} %concatenate.15.refs_0_.refs_1_.turned_hbm, bf16[8,256,256]{2,1,0:T(8,128)(2,1)} %copy-done.3, bf16[8,256,256]{2,1,0:T(8,128)(2,1)} %collective-permute-done.13.refs_2_.refs_3_, ...), custom_call_target="tpu_custom_call" | custom-call | flops 3000000000 | bytes 12582912 | tf_op jit(solution)/shard_map/ring_sums/pallas_call | solution.py:267
  150.3 0.0 all-gather.2.cloned.1.call-done.blocks_ref
  150.3 14.4 %far.1 = f32[1024,512]{1,0:T(8,128)} custom-call(s32[4,73]{1,0:T(4,128)} %copy-done.7, f32[4,512,256]{2,1,0:T(8,128)} %ring_sums.3.sums_ref, bf16[128,256,256]{2,1,0:T(8,128)(2,1)} %all-gather.2.cloned.1.call-done.blocks_ref, bf16[9,256,256]{2,1,0:T(8,128)(2,1)} %concatenate.15.refs_0_.refs_1_.turned_hbm, f32[512,512]{1,0:T(8,128)} %copy-done), custom_call_target="tpu_custom_call" | custom-call | tf_op jit(solution)/shard_map/far/pallas_call | solution.py:361
  (30 shorter events, 0.1 us)
Async XLA Ops:
  7.2 143.1 %all-gather.2.cloned.1.call-start = ((), (), s32[]{:S(2)}) async-start(), calls=%async_computation | async-start | bytes 16908288 | tf_op jit(solution)/shard_map/all_gather | solution.py:421
  9.9 16.2 %collective-permute-start.3 = (bf16[2,256,256]{2,1,0:T(8,128)(2,1)S(1)}, bf16[2,256,256]{2,1,0:T(8,128)(2,1)S(1)}, u32[]{:S(2)}, u32[]{:S(2)}) collective-permute-start(bf16[2,256,256]{2,1,0:T(8,128)(2,1)S(1)} %get-tuple-element.47), channel_id=1, source_target_pairs={{0,4},{1,5},{2,6},{3,7},{4,8},{5,9},{6,10},{7,11},{8,12},{9,13},{1... | collective-permute-start | bytes 786440 | tf_op jit(solution)/shard_map/ppermute | solution.py:401
  12.7 13.4 %collective-permute-start.4 = (bf16[2,256,256]{2,1,0:T(8,128)(2,1)S(1)}, bf16[2,256,256]{2,1,0:T(8,128)(2,1)S(1)}, u32[]{:S(2)}, u32[]{:S(2)}) collective-permute-start(bf16[2,256,256]{2,1,0:T(8,128)(2,1)S(1)} %get-tuple-element.46), channel_id=1, source_target_pairs={{0,1},{1,2},{2,3},{3,0},{4,5},{5,6},{6,7},{7,4},{8,9},{9,10},{10,1... | collective-permute-start | bytes 786440 | tf_op jit(solution)/shard_map/ppermute | solution.py:401
  18.0 1.2 collective-permute-start
  19.3 4.0 %collective-permute-start.1 = (f32[8,8]{1,0:T(8,128)S(1)}, f32[8,8]{1,0:T(8,128)S(1)}, u32[]{:S(2)}, u32[]{:S(2)}) collective-permute-start(f32[8,8]{1,0:T(8,128)S(1)} %add.51), channel_id=1, source_target_pairs={{0,64},{16,80},{32,96},{48,112},{64,0},{80,16},{96,32},{112,48},{1... | collective-permute-start | bytes 776 | tf_op jit(solution)/shard_map/ppermute | solution.py:405
  23.3 2.9 %collective-permute-start.2 = (f32[8,8]{1,0:T(8,128)S(1)}, f32[8,8]{1,0:T(8,128)S(1)}, u32[]{:S(2)}, u32[]{:S(2)}) collective-permute-start(f32[8,8]{1,0:T(8,128)S(1)} %add.52), channel_id=1, source_target_pairs={{0,32},{16,48},{32,0},{48,16},{64,96},{80,112},{96,64},{112,80},{1... | collective-permute-start | bytes 776 | tf_op jit(solution)/shard_map/ppermute | solution.py:405
  26.1 7.1 %collective-permute-start.7 = (bf16[2,256,256]{2,1,0:T(8,128)(2,1)S(1)}, bf16[2,256,256]{2,1,0:T(8,128)(2,1)S(1)}, u32[]{:S(2)}, u32[]{:S(2)}) collective-permute-start(bf16[2,256,256]{2,1,0:T(8,128)(2,1)S(1)} %collective-permute-done.3), channel_id=1, source_target_pairs={{0,4},{1,5},{2,6},{3,7},{4,8},{5,9},{6,10},{7,11},{8,12},{9,13},{1... | collective-permute-start | bytes 786440 | tf_op jit(solution)/shard_map/ppermute | solution.py:401
  26.3 7.0 %collective-permute-start.8 = (bf16[2,256,256]{2,1,0:T(8,128)(2,1)S(1)}, bf16[2,256,256]{2,1,0:T(8,128)(2,1)S(1)}, u32[]{:S(2)}, u32[]{:S(2)}) collective-permute-start(bf16[2,256,256]{2,1,0:T(8,128)(2,1)S(1)} %collective-permute-done.4), channel_id=1, source_target_pairs={{0,1},{1,2},{2,3},{3,0},{4,5},{5,6},{6,7},{7,4},{8,9},{9,10},{10,1... | collective-permute-start | bytes 786440 | tf_op jit(solution)/shard_map/ppermute | solution.py:401
  26.4 4.0 %collective-permute-start.5 = (f32[8,8]{1,0:T(8,128)S(1)}, f32[8,8]{1,0:T(8,128)S(1)}, u32[]{:S(2)}, u32[]{:S(2)}) collective-permute-start(f32[8,8]{1,0:T(8,128)S(1)} %add.53), channel_id=1, source_target_pairs={{0,8},{1,9},{2,10},{3,11},{4,12},{5,13},{6,14},{7,15},{8,0},{9,1},... | collective-permute-start | bytes 776 | tf_op jit(solution)/shard_map/ppermute | solution.py:405
  30.4 2.9 %collective-permute-start.6 = (f32[8,8]{1,0:T(8,128)S(1)}, f32[8,8]{1,0:T(8,128)S(1)}, u32[]{:S(2)}, u32[]{:S(2)}) collective-permute-start(f32[8,8]{1,0:T(8,128)S(1)} %add.58), channel_id=1, source_target_pairs={{0,4},{1,5},{2,6},{3,7},{4,0},{5,1},{6,2},{7,3},{8,12},{9,13},{10,... | collective-permute-start | bytes 776 | tf_op jit(solution)/shard_map/ppermute | solution.py:405
  33.2 10.6 %collective-permute-start.11 = (bf16[2,256,256]{2,1,0:T(8,128)(2,1)S(1)}, bf16[2,256,256]{2,1,0:T(8,128)(2,1)S(1)}, u32[]{:S(2)}, u32[]{:S(2)}) collective-permute-start(bf16[2,256,256]{2,1,0:T(8,128)(2,1)S(1)} %collective-permute-done.7), channel_id=1, source_target_pairs={{0,4},{1,5},{2,6},{3,7},{4,8},{5,9},{6,10},{7,11},{8,12},{9,13},{1... | collective-permute-start | bytes 786440 | tf_op jit(solution)/shard_map/ppermute | solution.py:401
  37.0 6.7 %collective-permute-start.12 = (bf16[2,256,256]{2,1,0:T(8,128)(2,1)S(1)}, bf16[2,256,256]{2,1,0:T(8,128)(2,1)S(1)}, u32[]{:S(2)}, u32[]{:S(2)}) collective-permute-start(bf16[2,256,256]{2,1,0:T(8,128)(2,1)S(1)} %collective-permute-done.8), channel_id=1, source_target_pairs={{0,1},{1,2},{2,3},{3,0},{4,5},{5,6},{6,7},{7,4},{8,9},{9,10},{10,1... | collective-permute-start | bytes 786440 | tf_op jit(solution)/shard_map/ppermute | solution.py:401
  37.1 4.0 %collective-permute-start.9 = (f32[8,8]{1,0:T(8,128)S(1)}, f32[8,8]{1,0:T(8,128)S(1)}, u32[]{:S(2)}, u32[]{:S(2)}) collective-permute-start(f32[8,8]{1,0:T(8,128)S(1)} %add.59), channel_id=1, source_target_pairs={{0,2},{1,3},{2,0},{3,1},{4,6},{5,7},{6,4},{7,5},{8,10},{9,11},{10,... | collective-permute-start | bytes 776 | tf_op jit(solution)/shard_map/ppermute | solution.py:405
  41.0 2.8 %collective-permute-start.10 = (f32[8,8]{1,0:T(8,128)S(1)}, f32[8,8]{1,0:T(8,128)S(1)}, u32[]{:S(2)}, u32[]{:S(2)}) collective-permute-start(f32[8,8]{1,0:T(8,128)S(1)} %add.60), channel_id=1, source_target_pairs={{0,1},{1,0},{2,3},{3,2},{4,5},{5,4},{6,7},{7,6},{8,9},{9,8},{10,11... | collective-permute-start | bytes 776 | tf_op jit(solution)/shard_map/ppermute | solution.py:405
  43.8 5.1 %copy-start.1 = (bf16[8,256,256]{2,1,0:T(8,128)(2,1)S(1)}, bf16[8,256,256]{2,1,0:T(8,128)(2,1)}, u32[]{:S(2)}) copy-start(bf16[8,256,256]{2,1,0:T(8,128)(2,1)} %near_ref.1) | copy-start | bytes 3145732
  43.9 5.5 %copy-start.3 = (bf16[8,256,256]{2,1,0:T(8,128)(2,1)}, bf16[8,256,256]{2,1,0:T(8,128)(2,1)S(1)}, u32[]{:S(2)}) copy-start(bf16[8,256,256]{2,1,0:T(8,128)(2,1)S(1)} %pad_maximum_fusion.refs_1_.refs_2_) | copy-start | bytes 3145732
  43.9 5.5 %copy-start.2 = (f32[512]{0:T(512)S(1)}, f32[512]{0:T(512)}, u32[]{:S(2)}) copy-start(f32[512]{0:T(512)} %param.9) | copy-start | bytes 6148
  45.1 22.7 %collective-permute-start.13 = (bf16[8,256,256]{2,1,0:T(8,128)(2,1)S(1)}, bf16[8,256,256]{2,1,0:T(8,128)(2,1)}, u32[]{:S(2)}, u32[]{:S(2)}) collective-permute-start(bf16[8,256,256]{2,1,0:T(8,128)(2,1)S(1)} %pad_maximum_fusion.refs_1_.refs_2_), channel_id=1, source_target_pairs={{0,1},{1,2},{2,3},{3,0},{4,5},{5,6},{6,7},{7,4},{8,9},{9,10},{10,1... | collective-permute-start | bytes 3145736 | tf_op jit(solution)/shard_map/ppermute | solution.py:401
  48.8 19.0 %collective-permute-start.14 = (bf16[8,256,256]{2,1,0:T(8,128)(2,1)}, bf16[8,256,256]{2,1,0:T(8,128)(2,1)}, u32[]{:S(2)}, u32[]{:S(2)}) collective-permute-start(bf16[8,256,256]{2,1,0:T(8,128)(2,1)} %pad_maximum_fusion.1.refs_5_.refs_6_), channel_id=1, source_target_pairs={{0,4},{1,5},{2,6},{3,7},{4,8},{5,9},{6,10},{7,11},{8,12},{9,13},{1... | collective-permute-start | bytes 3145736 | tf_op jit(solution)/shard_map/ppermute | solution.py:401
  67.8 34.6 %collective-permute-start.16 = (bf16[8,256,256]{2,1,0:T(8,128)(2,1)}, bf16[8,256,256]{2,1,0:T(8,128)(2,1)S(1)}, u32[]{:S(2)}, u32[]{:S(2)}) collective-permute-start(bf16[8,256,256]{2,1,0:T(8,128)(2,1)} %collective-permute-done.13.refs_2_.refs_3_), channel_id=1, source_target_pairs={{0,1},{1,2},{2,3},{3,0},{4,5},{5,6},{6,7},{7,4},{8,9},{9,10},{10,1... | collective-permute-start | bytes 3145736 | tf_op jit(solution)/shard_map/ppermute | solution.py:401
  68.0 34.4 %collective-permute-start.17 = (bf16[8,256,256]{2,1,0:T(8,128)(2,1)}, bf16[8,256,256]{2,1,0:T(8,128)(2,1)S(1)}, u32[]{:S(2)}, u32[]{:S(2)}) collective-permute-start(bf16[8,256,256]{2,1,0:T(8,128)(2,1)} %collective-permute-done.14.refs_6_.refs_7_), channel_id=1, source_target_pairs={{0,4},{1,5},{2,6},{3,7},{4,8},{5,9},{6,10},{7,11},{8,12},{9,13},{1... | collective-permute-start | bytes 3145736 | tf_op jit(solution)/shard_map/ppermute | solution.py:401
  68.2 37.9 %copy-start.12 = (s32[4]{0:T(128)S(1)}, s32[4]{0:T(128)}, u32[]{:S(2)}) copy-start(s32[4]{0:T(128)} %param.13) | copy-start | bytes 52
  68.2 38.0 %copy-start.8 = (s32[4,24]{1,0:T(4,128)S(1)}, s32[4,24]{1,0:T(4,128)}, u32[]{:S(2)}) copy-start(s32[4,24]{1,0:T(4,128)} %param.12) | copy-start | bytes 1156
  68.2 38.0 %copy-start.9 = (s32[4,24]{1,0:T(4,128)S(1)}, s32[4,24]{1,0:T(4,128)}, u32[]{:S(2)}) copy-start(s32[4,24]{1,0:T(4,128)} %param.11) | copy-start | bytes 1156
  68.2 38.0 %copy-start.11 = (s32[4,24]{1,0:T(4,128)S(1)}, s32[4,24]{1,0:T(4,128)}, u32[]{:S(2)}) copy-start(s32[4,24]{1,0:T(4,128)} %param.10) | copy-start | bytes 1156
  84.8 1.0 copy-start
  102.4 16.3 %copy-start.4 = (bf16[8,256,256]{2,1,0:T(8,128)(2,1)}, bf16[8,256,256]{2,1,0:T(8,128)(2,1)S(1)}, u32[]{:S(2)}) copy-start(bf16[8,256,256]{2,1,0:T(8,128)(2,1)S(1)} %collective-permute-done.16.refs_3_.refs_4_) | copy-start | bytes 3145732
  102.4 16.3 %copy-start.5 = (bf16[8,256,256]{2,1,0:T(8,128)(2,1)}, bf16[8,256,256]{2,1,0:T(8,128)(2,1)S(1)}, u32[]{:S(2)}) copy-start(bf16[8,256,256]{2,1,0:T(8,128)(2,1)S(1)} %collective-permute-done.17.refs_7_.refs_8_) | copy-start | bytes 3145732
  102.4 14.1 %collective-permute-start.18 = (bf16[8,256,256]{2,1,0:T(8,128)(2,1)S(1)}, bf16[8,256,256]{2,1,0:T(8,128)(2,1)}, u32[]{:S(2)}, u32[]{:S(2)}) collective-permute-start(bf16[8,256,256]{2,1,0:T(8,128)(2,1)S(1)} %collective-permute-done.16.refs_3_.refs_4_), channel_id=1, source_target_pairs={{0,1},{1,2},{2,3},{3,0},{4,5},{5,6},{6,7},{7,4},{8,9},{9,10},{10,1... | collective-permute-start | bytes 3145736 | tf_op jit(solution)/shard_map/ppermute | solution.py:401
  104.6 14.0 %collective-permute-start.19 = (bf16[8,256,256]{2,1,0:T(8,128)(2,1)S(1)}, bf16[8,256,256]{2,1,0:T(8,128)(2,1)}, u32[]{:S(2)}, u32[]{:S(2)}) collective-permute-start(bf16[8,256,256]{2,1,0:T(8,128)(2,1)S(1)} %collective-permute-done.17.refs_7_.refs_8_), channel_id=1, source_target_pairs={{0,4},{1,5},{2,6},{3,7},{4,8},{5,9},{6,10},{7,11},{8,12},{9,13},{1... | collective-permute-start | bytes 3145736 | tf_op jit(solution)/shard_map/ppermute | solution.py:401
  106.2 23.5 %copy-start.7 = (s32[4,73]{1,0:T(4,128)}, s32[4,73]{1,0:T(4,128)S(1)}, u32[]{:S(2)}) copy-start(s32[4,73]{1,0:T(4,128)S(1)} %pad_add_fusion.info_ref) | copy-start | bytes 3508
  106.2 1.2 collective-permute-start.15
  107.4 11.2 %copy-start.10 = (s32[4,73]{1,0:T(4,128)}, s32[4,73]{1,0:T(4,128)S(1)}, u32[]{:S(2)}) copy-start(s32[4,73]{1,0:T(4,128)S(1)} %collective-permute-done.15.info_ref) | copy-start | bytes 3508
  129.8 7.0 %collective-permute-start.20 = (f32[4,512,256]{2,1,0:T(8,128)}, f32[4,512,256]{2,1,0:T(8,128)S(1)}, u32[]{:S(2)}, u32[]{:S(2)}) collective-permute-start(f32[4,512,256]{2,1,0:T(8,128)} %ring_sums.2), channel_id=1, source_target_pairs={{0,16},{16,0},{32,48},{48,32},{64,80},{80,64},{96,112},{112,96},{1... | collective-permute-start | bytes 6291464 | tf_op jit(solution)/shard_map/ppermute | solution.py:405
  136.8 1.3 copy-start.6
Sparse Core Ops, SparseCore 0:
  11.1 92.4 all-gather.1

commit v2 on v1

--- a/solution.py
+++ b/solution.py
@@ -159,14 +159,8 @@
     )(work, upper)
 
 
-def position():
-    row, col = lax.axis_index("row"), lax.axis_index("col")
-    return row % 2, col // SIDE, col % SIDE
-
-
-def ring_slot(offset, here):
-    core, y, z = here
-    col, local = offset // CACHED, offset % CACHED
+def ring_places(offsets, core, y, z):
+    col, local = offsets // CACHED, offsets % CACHED
     half, inner = local // HALF, local % HALF
     sign = 1 - 2 * core
     from_y = (sign * (y - col // SIDE)) & (SIDE - 1)
@@ -176,24 +170,24 @@
     minor = jnp.where(by_z, from_y, from_z)
     place = jnp.where(by_z, inner, inner - RING + SIDE * SIDE * RING)
     held = (half == core) & (inner < 2 * RING)
-    return held, (major * SIDE + minor) * RING + place
-
-
-def spread_slot(offset):
-    col, local = offset // CACHED, offset % CACHED
+    return jnp.where(held, (major * SIDE + minor) * RING + place, -1)
+
+
+def spread_places(offsets):
+    col, local = offsets // CACHED, offsets % CACHED
     half, inner = local // HALF, local % HALF
     kept = HALF - 2 * RING
-    return inner >= 2 * RING, col * (2 * kept) + half * kept + inner - 2 * RING
-
-
-def list_slots(tile, slot_of, info_ref, items, slots):
+    place = col * (2 * kept) + half * kept + inner - 2 * RING
+    return jnp.where(inner >= 2 * RING, place, -1)
+
+
+def list_slots(tile, info_ref, items, slots):
     def visit(s, count):
-        wanted, place = slot_of(info_ref[tile, s])
+        place = info_ref[tile, s]
         items[0, tile, count] = place
         items[1, tile, count] = info_ref[tile, slots + s]
         items[2, tile, count] = info_ref[tile, 2 * slots + s]
-        wanted = wanted & (s < info_ref[tile, 3 * slots])
-        return count + wanted.astype(jnp.int32)
+        return count + (place >= 0).astype(jnp.int32)
 
     return lax.fori_loop(0, slots, visit, 0)
 
@@ -211,17 +205,10 @@
     )
 
 
-def ring_kernel(slots, seeded, info_ref, *refs):
-    if seeded:
-        seed_ref, turned_ref = refs[:2]
-        refs = refs[2:]
-    else:
-        turned_ref = refs[0]
-        refs = refs[1:]
+def ring_kernel(slots, info_ref, turned_ref, *refs):
     *pieces, out_ref, held, items, arrived = refs
     size = turned_ref.shape[1]
     tile = pl.program_id(0)
-    here = position()
     copies = []
     start = 0
     for n, piece in enumerate(pieces):
@@ -235,14 +222,14 @@
         for copy in copies:
             copy.start()
 
-    count = list_slots(tile, lambda offset: ring_slot(offset, here), info_ref, items, slots)
+    count = list_slots(tile, info_ref, items, slots)
 
     @pl.when(tile == 0)
     def wait():
         for copy in copies:
             copy.wait()
 
-    out_ref[...] = seed_ref[...] if seeded else jnp.zeros_like(out_ref)
+    out_ref[...] = jnp.zeros_like(out_ref)
 
     def one_round(r, carry):
         rights = []
@@ -259,19 +246,17 @@
     lax.fori_loop(0, (count + GROUP - 1) // GROUP, one_round, 0)
 
 
-def ring_sums(info, slots, turned_near, pieces, seed=None):
+def ring_sums(info, slots, turned_near, pieces):
     tiles = info.shape[0]
     size = turned_near.shape[1]
     per_tile = pl.BlockSpec((1, 2 * size, size), lambda t, *_: (t, 0, 0))
-    seeds = [] if seed is None else [seed]
     return pl.pallas_call(
-        functools.partial(ring_kernel, slots, seed is not None),
+        functools.partial(ring_kernel, slots),
         out_shape=jax.ShapeDtypeStruct((tiles, 2 * size, size), jnp.float32),
         grid_spec=pltpu.PrefetchScalarGridSpec(
             num_scalar_prefetch=1,
             grid=(tiles,),
-            in_specs=[per_tile] * len(seeds)
-            + [pl.BlockSpec(turned_near.shape, lambda t, *_: (0, 0, 0))]
+            in_specs=[pl.BlockSpec(turned_near.shape, lambda t, *_: (0, 0, 0))]
             + [pl.BlockSpec(memory_space=pltpu.HBM)] * len(pieces),
             out_specs=per_tile,
             scratch_shapes=[
@@ -287,12 +272,12 @@
             flops=3_000_000_000, bytes_accessed=12 << 20, transcendentals=0
         ),
         name="ring_sums",
-    )(info, *seeds, turned_near, *pieces)
+    )(info, turned_near, *pieces)
 
 
 def far_kernel(
-    slots, info_ref, sums_ref, blocks_ref, turned_hbm, inverse_hbm, out_hbm, held, total,
-    turned_ref, inverse_ref, out_ref, items, arrived, loaded, stored,
+    slots, info_ref, own_hbm, other_hbm, blocks_ref, turned_hbm, inverse_hbm, out_hbm, held, total,
+    other_ref, turned_ref, inverse_ref, out_ref, items, arrived, loaded, stored,
 ):
     tiles = info_ref.shape[0]
     size = turned_ref.shape[1]
@@ -311,13 +296,14 @@
         )
 
     load_turned = pltpu.make_async_copy(turned_hbm, turned_ref, loaded.at[0])
-    load_sums = pltpu.make_async_copy(sums_ref, total, loaded.at[1])
+    load_own = pltpu.make_async_copy(own_hbm, total, loaded.at[1])
     load_inverse = pltpu.make_async_copy(inverse_hbm, inverse_ref, loaded.at[2])
+    load_other = pltpu.make_async_copy(other_hbm, other_ref, loaded.at[3])
     load_turned.start()
-    load_sums.start()
+    load_own.start()
     counts = []
     for t in range(tiles):
-        count = list_slots(t, spread_slot, info_ref, items, slots)
+        count = list_slots(t, info_ref, items, slots)
         counts.append(count)
 
         def begin(q, carry):
@@ -325,9 +311,10 @@
             return carry
 
         lax.fori_loop(0, (count + GROUP - 1) // GROUP * GROUP, begin, 0)
+    load_other.start()
     load_inverse.start()
     load_turned.wait()
-    load_sums.wait()
+    load_own.wait()
     for t in range(tiles):
 
         def one_round(r, carry):
@@ -343,8 +330,9 @@
 
         lax.fori_loop(0, (counts[t] + GROUP - 1) // GROUP, one_round, 0)
         if t == 0:
+            load_other.wait()
             load_inverse.wait()
-        turned = total[t].T
+        turned = (total[t] + other_ref[t]).T
         out_ref[t, :, :size] = dot32(turned[:, :size], inverse_ref[:size, :size])
         out_ref[t, :, size:] = dot32(turned, inverse_ref[:, size:])
         store(t).start()
@@ -355,28 +343,29 @@
 HBM = pl.BlockSpec(memory_space=pltpu.HBM)
 
 
-def far(info, slots, sums, blocks, turned_near, inverse):
+def far(info, slots, sums, other_sums, blocks, turned_near, inverse):
     tiles = info.shape[0]
     size = blocks.shape[1]
     return pl.pallas_call(
         functools.partial(far_kernel, slots),
         out_shape=jax.ShapeDtypeStruct((tiles * size, 2 * size), jnp.float32),
-        in_specs=[pl.BlockSpec(memory_space=pltpu.SMEM), HBM, HBM, HBM, HBM],
+        in_specs=[pl.BlockSpec(memory_space=pltpu.SMEM)] + [HBM] * 5,
         out_specs=HBM,
         scratch_shapes=[
             pltpu.VMEM((tiles, slots * size, size), jnp.bfloat16),
+            pltpu.VMEM(sums.shape, jnp.float32),
             pltpu.VMEM(sums.shape, jnp.float32),
             pltpu.VMEM(turned_near.shape, jnp.bfloat16),
             pltpu.VMEM(inverse.shape, jnp.float32),
             pltpu.VMEM((tiles, size, 2 * size), jnp.float32),
             pltpu.SMEM((3, tiles, slots), jnp.int32),
             pltpu.SemaphoreType.DMA((tiles, slots)),
-            pltpu.SemaphoreType.DMA((3,)),
+            pltpu.SemaphoreType.DMA((4,)),
             pltpu.SemaphoreType.DMA((tiles,)),
         ],
         compiler_params=pltpu.CompilerParams(vmem_limit_bytes=63 << 20),
         name="far",
-    )(info, sums, blocks, turned_near, inverse)
+    )(info, sums, other_sums, blocks, turned_near, inverse)
 
 
 def local_pairs(near_first, near_second, counts, near_total):
@@ -421,38 +410,55 @@
     blocks = lax.all_gather(own, ("col", "row"), axis=0, tiled=True)
     line_y = [lax.dynamic_slice_in_dim(response_cache, core * HALF, RING, 0)]
     line_z = [lax.dynamic_slice_in_dim(response_cache, core * HALF + RING, RING, 0)]
+    usable = jnp.arange(slots, dtype=jnp.int32)[None, :] < tile_counts[:, None]
+    y, z = lax.axis_index("col") // SIDE, lax.axis_index("col") % SIDE
+    info, info_own, info_other = (
+        jnp.concatenate([jnp.where(usable, places, -1), near_first, near_second], axis=1)
+        for places in (
+            spread_places(far_offsets),
+            ring_places(far_offsets, core, y, z),
+            ring_places(far_offsets, 1 - core, y, z),
+        )
+    )
+    turned = jnp.transpose(near_cache, (0, 2, 1))
+    padded = jnp.concatenate([turned, jnp.zeros_like(turned[:1])], axis=0)
     pairs = local_pairs(near_first, near_second, tile_counts, near_total)
-    for stages in (
-        (("row", 1), ("row", 4), ("row", 2)),
-        (("col", 8), ("col", 4)),
-        (("col", 2), ("col", 1)),
-    ):
-        line_y.append(hop(line_y[-1], True))
-        line_z.append(hop(line_z[-1], False))
+
+    def advance(pairs, rings, stages):
+        (to_z, along_y), (to_y, along_z) = rings
+        to_z, to_y = hop(to_z, along_y), hop(to_y, along_z)
         for axis, bit in stages:
             pairs = pairs + swap(pairs, axis, bit)
-        pairs, line_y[-1], line_z[-1] = lax.optimization_barrier((pairs, line_y[-1], line_z[-1]))
-    info = jnp.concatenate([far_offsets, near_first, near_second, tile_counts[:, None]], axis=1)
-    info_other = swap(info, "row", 1)
-    turned = jnp.transpose(near_cache, (0, 2, 1))
-    padded = jnp.concatenate([turned, jnp.zeros_like(turned[:1])], axis=0)
+        return lax.optimization_barrier((pairs, to_z, to_y))
+
+    for stages in ((("row", 1),), (("row", 4),), (("row", 2),)):
+        pairs, step_y, step_z = advance(
+            pairs, ((line_y[-1], True), (line_z[-1], False)), stages
+        )
+        line_y.append(step_y)
+        line_z.append(step_z)
     by_z = [jnp.concatenate(line_y, axis=0)]
     by_y = [jnp.concatenate(line_z, axis=0)]
-    pairs, by_z[0], by_y[0] = lax.optimization_barrier((pairs, by_z[0], by_y[0]))
-    by_z.append(hop(by_z[0], False))
-    by_y.append(hop(by_y[0], True))
+    pairs, step_z, step_y = advance(
+        pairs, ((by_z[-1], False), (by_y[-1], True)), (("col", 8), ("col", 4), ("col", 2))
+    )
+    by_z.append(step_z)
+    by_y.append(step_y)
+    info_other = swap(info_other, "row", 1)
+    pairs = pairs + swap(pairs, "col", 1)
+    step_z, step_y = hop(by_z[-1], False), hop(by_y[-1], True)
     work, upper = lead_start(pairs, near_cache, turned, lead_diag)
-    work, by_z[1], by_y[1] = lax.optimization_barrier((work, by_z[1], by_y[1]))
-    by_z.append(hop(by_z[1], False))
-    by_y.append(hop(by_y[1], True))
+    work, step_z, step_y = lax.optimization_barrier((work, step_z, step_y))
+    by_z.append(step_z)
+    by_y.append(step_y)
+    step_z, step_y = hop(by_z[-1], False), hop(by_y[-1], True)
     lead_factor, inverse = lead_end(work, upper)
-    inverse, by_z[2], by_y[2] = lax.optimization_barrier((inverse, by_z[2], by_y[2]))
-    by_z.append(hop(by_z[2], False))
-    by_y.append(hop(by_y[2], True))
-    pieces = by_z + by_y
-    sums_other = swap(ring_sums(info_other, slots, padded, pieces), "row", 1)
-    sums = ring_sums(info, slots, padded, pieces, sums_other)
-    far_factor = far(info, slots, sums, blocks, padded, inverse)
+    inverse, step_z, step_y = lax.optimization_barrier((inverse, step_z, step_y))
+    pieces = by_z + [step_z] + by_y + [step_y]
+    sums_other = ring_sums(info_other, slots, padded, pieces)
+    moved = swap(sums_other, "row", 1)
+    sums = ring_sums(info_own, slots, padded, pieces)
+    far_factor = far(info, slots, sums, moved, blocks, padded, inverse)
     return lead_factor, far_factor
 
 

time: 171 us -> 187 us (1.094); the launches traced: 172 us -> 185 us
  starting transfers between devices: 28.3 us -> 47.9 us
  Pallas kernels: 72.5 us -> 67 us
    ppermute x12, waiting for transfers between devices: 27.8 us -> 1.24 us  [hop(): return lax.ppermute(value, ('row', 'col'), moves)]
    ppermute x9, waiting for transfers between devices: 18.9 us -> 44.9 us  [swap(): lax.ppermute(value, axis, [(i, i ^ bit) for i in range(lax.axis_size(axis...]
    ppermute x9, starting transfers between devices: 9.73 us -> 29.5 us  [swap(): lax.ppermute(value, axis, [(i, i ^ bit) for i in range(lax.axis_size(axis...]
    pallas_call x2, Pallas kernels: 23.2 us -> 19.3 us  [ring_sums(): pl.pallas_call(functools.partial(ring_kernel, slots), out_shape=jax.Shape...]
  transfers between devices with their start and end apart: 22 -> 22, of which waited for: 11 -> 10; matrix products, arithmetic and copies ran while one was open for 3% -> 3% of each run, Pallas kernels for 34% -> 29%
where the time goes in v2:
time: 187 us; the launch traced here: 185 us
  Pallas kernels  67 us (36%)
  starting transfers between devices  47.9 us (26%)
  waiting for transfers between devices  46.2 us (25%)
  between operations  14.4 us (8%)
  local copies, waits for them, and re-layouts  7.16 us (4%)
  other arithmetic  2.52 us (1%)
    ppermute x9, waiting for transfers between devices, swap(): lax.ppermute(value, axis, [(i, i ^ bit) for i in range(lax.axis_size(axis...  44.9 us
    ppermute x9, starting transfers between devices, swap(): lax.ppermute(value, axis, [(i, i ^ bit) for i in range(lax.axis_size(axis...  29.5 us
    pallas_call x2, Pallas kernels, ring_sums(): pl.pallas_call(functools.partial(ring_kernel, slots), out_shape=jax.Shape...  19.3 us
    pallas_call x1, Pallas kernels, lead_start(): pl.pallas_call(lead_start_kernel, out_shape=(jax.ShapeDtypeStruct((whole,...  18.4 us
    ppermute x12, starting transfers between devices, hop(): return lax.ppermute(value, ('row', 'col'), moves)  18.4 us
    pallas_call x1, Pallas kernels, lead_end(): pl.pallas_call(lead_end_kernel, out_shape=(square, square), in_specs=[VME...  16.6 us
    pallas_call x1, Pallas kernels, far(): pl.pallas_call(functools.partial(far_kernel, slots), out_shape=jax.ShapeD...  12.7 us
  transfers between devices with their start and end apart: 22, of which 10 were waited for; matrix products, arithmetic and copies ran while one was open for 3% of the time, Pallas kernels for 29%

profile of v2, /device:TPU:7, one launch (start us, length us, event | category | flops | bytes accessed | tf_op | source)
XLA Modules:
  0.0 185.2 jit_solution(10053117435789011308)
XLA Ops:
  7.2 0.0 all-gather.2.cloned.1.call-start
  7.2 1.6 constant_dynamic-slice_fusion
  8.8 0.0 all-gather.2.cloned.1.call-update
  8.8 1.1 constant_dynamic-slice_fusion.1
  9.9 2.8 %collective-permute-start.1 = (bf16[2,256,256]{2,1,0:T(8,128)(2,1)S(1)}, bf16[2,256,256]{2,1,0:T(8,128)(2,1)S(1)}, u32[]{:S(2)}, u32[]{:S(2)}) collective-permute-start(bf16[2,256,256]{2,1,0:T(8,128)(2,1)S(1)} %get-tuple-element.47), channel_id=1, source_target_pairs={{0,4},{1,5},{2,6},{3,7},{4,8},{5,9},{6,10},{7,11},{8,12},{9,13},{1... | collective-permute-start | bytes 786440 | tf_op jit(solution)/shard_map/ppermute | solution.py:390
  12.7 3.8 %collective-permute-start.2 = (bf16[2,256,256]{2,1,0:T(8,128)(2,1)S(1)}, bf16[2,256,256]{2,1,0:T(8,128)(2,1)S(1)}, u32[]{:S(2)}, u32[]{:S(2)}) collective-permute-start(bf16[2,256,256]{2,1,0:T(8,128)(2,1)S(1)} %get-tuple-element.46), channel_id=1, source_target_pairs={{0,1},{1,2},{2,3},{3,0},{4,5},{5,6},{6,7},{7,4},{8,9},{9,10},{10,1... | collective-permute-start | bytes 786440 | tf_op jit(solution)/shard_map/ppermute | solution.py:390
  16.5 0.7 iota_compare_fusion.2
  17.2 0.7 iota_compare_fusion
  17.9 0.1 convert_reduce_fusion
  18.0 0.1 collective-permute-start
  18.1 1.2 collective-permute-done
  19.3 0.0 collective-permute-done.1
  19.3 0.5 collective-permute-done.2
  19.8 0.5 collective-permute-start.4
  20.3 3.1 %collective-permute-start.5 = (bf16[2,256,256]{2,1,0:T(8,128)(2,1)S(1)}, bf16[2,256,256]{2,1,0:T(8,128)(2,1)S(1)}, u32[]{:S(2)}, u32[]{:S(2)}) collective-permute-start(bf16[2,256,256]{2,1,0:T(8,128)(2,1)S(1)} %collective-permute-done.2), channel_id=1, source_target_pairs={{0,1},{1,2},{2,3},{3,0},{4,5},{5,6},{6,7},{7,4},{8,9},{9,10},{10,1... | collective-permute-start | bytes 786440 | tf_op jit(solution)/shard_map/ppermute | solution.py:390
  23.4 1.1 collective-permute-start.3
  24.5 2.8 %collective-permute-done.3 = f32[8,8]{1,0:T(8,128)S(1)} collective-permute-done((f32[8,8]{1,0:T(8,128)S(1)}, f32[8,8]{1,0:T(8,128)S(1)}, u32[]{:S(2)}, u32[]{:S(2)}) %collective-permute-start.3) | collective-permute-done | bytes 288 | tf_op jit(solution)/shard_map/ppermute | solution.py:394
  27.4 0.0 collective-permute-done.4
  27.4 0.0 collective-permute-done.5
  27.4 0.2 collective-permute-start.7
  27.6 2.7 %collective-permute-start.8 = (bf16[2,256,256]{2,1,0:T(8,128)(2,1)S(1)}, bf16[2,256,256]{2,1,0:T(8,128)(2,1)S(1)}, u32[]{:S(2)}, u32[]{:S(2)}) collective-permute-start(bf16[2,256,256]{2,1,0:T(8,128)(2,1)S(1)} %collective-permute-done.5), channel_id=1, source_target_pairs={{0,1},{1,2},{2,3},{3,0},{4,5},{5,6},{6,7},{7,4},{8,9},{9,10},{10,1... | collective-permute-start | bytes 786440 | tf_op jit(solution)/shard_map/ppermute | solution.py:390
  30.3 0.5 collective-permute-start.6
  30.8 2.3 %collective-permute-done.6 = f32[8,8]{1,0:T(8,128)S(1)} collective-permute-done((f32[8,8]{1,0:T(8,128)S(1)}, f32[8,8]{1,0:T(8,128)S(1)}, u32[]{:S(2)}, u32[]{:S(2)}) %collective-permute-start.6) | collective-permute-done | bytes 288 | tf_op jit(solution)/shard_map/ppermute | solution.py:394
  33.1 0.4 collective-permute-done.7
  33.5 0.3 collective-permute-done.8
  33.8 0.1 pad_maximum_fusion.refs_0_
  34.0 0.0 copy-start.2
  34.0 3.5 %collective-permute-start.12 = (bf16[8,256,256]{2,1,0:T(8,128)(2,1)S(1)}, bf16[8,256,256]{2,1,0:T(8,128)(2,1)}, u32[]{:S(2)}, u32[]{:S(2)}) collective-permute-start(bf16[8,256,256]{2,1,0:T(8,128)(2,1)S(1)} %pad_maximum_fusion.refs_0_), channel_id=1, source_target_pairs={{0,1},{1,2},{2,3},{3,0},{4,5},{5,6},{6,7},{7,4},{8,9},{9,10},{10,1... | collective-permute-start | bytes 3145736 | tf_op jit(solution)/shard_map/ppermute | solution.py:390
  37.5 0.1 pad_maximum_fusion.1.refs_4_
  37.6 0.2 collective-permute-start.13
  37.9 3.4 %collective-permute-start.9 = (f32[8,8]{1,0:T(8,128)S(1)}, f32[8,8]{1,0:T(8,128)S(1)}, u32[]{:S(2)}, u32[]{:S(2)}) collective-permute-start(f32[8,8]{1,0:T(8,128)S(1)} %add.116), channel_id=1, source_target_pairs={{0,8},{1,9},{2,10},{3,11},{4,12},{5,13},{6,14},{7,15},{8,0},{9,1},... | collective-permute-start | bytes 776 | tf_op jit(solution)/shard_map/ppermute | solution.py:394
  41.3 1.0 collective-permute-done.9
  42.3 17.7 %collective-permute-start.10 = (f32[8,8]{1,0:T(8,128)S(1)}, f32[8,8]{1,0:T(8,128)S(1)}, u32[]{:S(2)}, u32[]{:S(2)}) collective-permute-start(f32[8,8]{1,0:T(8,128)S(1)} %add.117), channel_id=1, source_target_pairs={{0,4},{1,5},{2,6},{3,7},{4,0},{5,1},{6,2},{7,3},{8,12},{9,13},{10,... | collective-permute-start | bytes 776 | tf_op jit(solution)/shard_map/ppermute | solution.py:394
  59.9 1.3 collective-permute-done.10
  61.2 4.0 %collective-permute-done.11 = f32[8,8]{1,0:T(8,128)S(1)} collective-permute-done((f32[8,8]{1,0:T(8,128)S(1)}, f32[8,8]{1,0:T(8,128)S(1)}, u32[]{:S(2)}, u32[]{:S(2)}) %collective-permute-start.11) | collective-permute-done | bytes 288 | tf_op jit(solution)/shard_map/ppermute | solution.py:394
  65.2 0.1 collective-permute-start.15
  65.3 1.4 collective-permute-start.16
  66.7 0.5 copy.11
  67.2 1.6 collective-permute-start.14
  68.9 32.4 %collective-permute-done.14 = f32[8,8]{1,0:T(8,128)S(1)} collective-permute-done((f32[8,8]{1,0:T(8,128)S(1)}, f32[8,8]{1,0:T(8,128)S(1)}, u32[]{:S(2)}, u32[]{:S(2)}) %collective-permute-start.14) | collective-permute-done | bytes 288 | tf_op jit(solution)/shard_map/ppermute | solution.py:394
  101.2 0.0 copy-start.11
  101.2 0.0 copy-start.7
  101.3 0.0 copy-start.8
  101.3 18.4 %lead_start.1 = (f32[512,1024]{1,0:T(8,128)S(1)}, f32[512,512]{1,0:T(8,128)S(1)}) custom-call(f32[8,8]{1,0:T(8,128)S(1)} %add.120.pairs_ref, bf16[8,256,256]{2,1,0:T(8,128)(2,1)S(1)} %copy-done.1, bf16[8,256,256]{2,1,0:T(8,128)(2,1)S(1)} %bitcast.2, f32[1,512]{1,0:T(1,128)S(1)} %bitcast.4), custom_call_target="tpu_custom_call" | custom-call | flops 8999999488 | bytes 6291456 | tf_op jit(solution)/shard_map/lead_start/pallas_call | solution.py:126
  119.7 0.0 collective-permute-done.15.refs_2_
  119.7 0.1 collective-permute-start.17
  119.8 0.1 collective-permute-start.18
  119.9 0.1 select_select_fusion
  120.0 0.6 add_add_fusion.2
  120.6 3.6 %collective-permute-start.19 = (s32[4,72]{1,0:T(4,128)S(1)}, s32[4,72]{1,0:T(4,128)S(1)}, u32[]{:S(2)}, u32[]{:S(2)}) collective-permute-start(s32[4,72]{1,0:T(4,128)S(1)} %get-tuple-element.48), channel_id=1, source_target_pairs={{0,16},{16,0},{32,48},{48,32},{64,80},{80,64},{96,112},{112,96},{1... | collective-permute-start | bytes 3464 | tf_op jit(solution)/shard_map/ppermute | solution.py:394
  124.2 1.1 concatenate.22.turned_ref.turned_hbm
  125.4 16.6 %lead_end.1 = (f32[512,512]{1,0:T(8,128)}, f32[512,512]{1,0:T(8,128)S(1)}) custom-call(f32[512,1024]{1,0:T(8,128)S(1)} %get-tuple-element.37.work_ref, f32[512,512]{1,0:T(8,128)S(1)} %get-tuple-element.38.upper_ref), custom_call_target="tpu_custom_call" | custom-call | flops 8999999488 | bytes 6291456 | tf_op jit(solution)/shard_map/lead_end/pallas_call | solution.py:145
  142.0 1.0 copy-done
  142.9 0.0 collective-permute-done.17.refs_3_
  142.9 0.0 collective-permute-done.18.refs_7_
  143.0 0.9 copy-done.5
  143.9 0.3 copy-done.6
  144.2 0.6 copy-done.9
  144.8 10.1 %ring_sums.3 = f32[4,512,256]{2,1,0:T(8,128)} custom-call(s32[4,72]{1,0:T(4,128)} %copy-done.9, bf16[9,256,256]{2,1,0:T(8,128)(2,1)} %concatenate.22.turned_ref.turned_hbm, bf16[8,256,256]{2,1,0:T(8,128)(2,1)} %copy-done.3, bf16[8,256,256]{2,1,0:T(8,128)(2,1)} %collective-permute-done.12.refs_1_, bf16[8,256,256]{2,1,0:T(8,128)(2,1)} %collective-permute-done.15.refs_2_, ...), custom_call_target="tpu_custom_call" | custom-call | flops 3000000000 | bytes 12582912 | tf_op jit(solution)/shard_map/ring_sums/pallas_call | solution.py:253
  154.9 1.4 collective-permute-start.20
  156.3 9.2 %ring_sums.2.own_hbm = f32[4,512,256]{2,1,0:T(8,128)} custom-call(s32[4,72]{1,0:T(4,128)} %get-tuple-element.49.info_ref, bf16[9,256,256]{2,1,0:T(8,128)(2,1)} %concatenate.22.turned_ref.turned_hbm, bf16[8,256,256]{2,1,0:T(8,128)(2,1)} %copy-done.3, bf16[8,256,256]{2,1,0:T(8,128)(2,1)} %collective-permute-done.12.refs_1_, ...), custom_call_target="tpu_custom_call" | custom-call | flops 3000000000 | bytes 12582912 | tf_op jit(solution)/shard_map/ring_sums/pallas_call | solution.py:253
  165.5 0.0 collective-permute-done.20.other_hbm
  165.6 0.0 all-gather.2.cloned.1.call-done.blocks_ref
  165.6 12.7 %far.1 = f32[1024,512]{1,0:T(8,128)} custom-call(s32[4,72]{1,0:T(4,128)} %get-tuple-element.50.info_ref, f32[4,512,256]{2,1,0:T(8,128)} %ring_sums.2.own_hbm, f32[4,512,256]{2,1,0:T(8,128)} %collective-permute-done.20.other_hbm, bf16[128,256,256]{2,1,0:T(8,128)(2,1)} %all-gather.2.cloned.1.call-done.blocks_ref, ...), custom_call_target="tpu_custom_call" | custom-call | tf_op jit(solution)/shard_map/far/pallas_call | solution.py:349
  (28 shorter events, 0.1 us)
Async XLA Ops:
  7.2 158.4 %all-gather.2.cloned.1.call-start = ((), (), s32[]{:S(2)}) async-start(), calls=%async_computation | async-start | bytes 16908288 | tf_op jit(solution)/shard_map/all_gather | solution.py:410
  9.9 9.4 %collective-permute-start.1 = (bf16[2,256,256]{2,1,0:T(8,128)(2,1)S(1)}, bf16[2,256,256]{2,1,0:T(8,128)(2,1)S(1)}, u32[]{:S(2)}, u32[]{:S(2)}) collective-permute-start(bf16[2,256,256]{2,1,0:T(8,128)(2,1)S(1)} %get-tuple-element.47), channel_id=1, source_target_pairs={{0,4},{1,5},{2,6},{3,7},{4,8},{5,9},{6,10},{7,11},{8,12},{9,13},{1... | collective-permute-start | bytes 786440 | tf_op jit(solution)/shard_map/ppermute | solution.py:390
  12.7 7.1 %collective-permute-start.2 = (bf16[2,256,256]{2,1,0:T(8,128)(2,1)S(1)}, bf16[2,256,256]{2,1,0:T(8,128)(2,1)S(1)}, u32[]{:S(2)}, u32[]{:S(2)}) collective-permute-start(bf16[2,256,256]{2,1,0:T(8,128)(2,1)S(1)} %get-tuple-element.46), channel_id=1, source_target_pairs={{0,1},{1,2},{2,3},{3,0},{4,5},{5,6},{6,7},{7,4},{8,9},{9,10},{10,1... | collective-permute-start | bytes 786440 | tf_op jit(solution)/shard_map/ppermute | solution.py:390
  18.0 1.2 collective-permute-start
  19.8 7.6 %collective-permute-start.4 = (bf16[2,256,256]{2,1,0:T(8,128)(2,1)S(1)}, bf16[2,256,256]{2,1,0:T(8,128)(2,1)S(1)}, u32[]{:S(2)}, u32[]{:S(2)}) collective-permute-start(bf16[2,256,256]{2,1,0:T(8,128)(2,1)S(1)} %collective-permute-done.1), channel_id=1, source_target_pairs={{0,4},{1,5},{2,6},{3,7},{4,8},{5,9},{6,10},{7,11},{8,12},{9,13},{1... | collective-permute-start | bytes 786440 | tf_op jit(solution)/shard_map/ppermute | solution.py:390
  20.3 7.1 %collective-permute-start.5 = (bf16[2,256,256]{2,1,0:T(8,128)(2,1)S(1)}, bf16[2,256,256]{2,1,0:T(8,128)(2,1)S(1)}, u32[]{:S(2)}, u32[]{:S(2)}) collective-permute-start(bf16[2,256,256]{2,1,0:T(8,128)(2,1)S(1)} %collective-permute-done.2), channel_id=1, source_target_pairs={{0,1},{1,2},{2,3},{3,0},{4,5},{5,6},{6,7},{7,4},{8,9},{9,10},{10,1... | collective-permute-start | bytes 786440 | tf_op jit(solution)/shard_map/ppermute | solution.py:390
  23.4 4.0 %collective-permute-start.3 = (f32[8,8]{1,0:T(8,128)S(1)}, f32[8,8]{1,0:T(8,128)S(1)}, u32[]{:S(2)}, u32[]{:S(2)}) collective-permute-start(f32[8,8]{1,0:T(8,128)S(1)} %add.110), channel_id=1, source_target_pairs={{0,64},{16,80},{32,96},{48,112},{64,0},{80,16},{96,32},{112,48},{1... | collective-permute-start | bytes 776 | tf_op jit(solution)/shard_map/ppermute | solution.py:394
  27.4 6.2 %collective-permute-start.7 = (bf16[2,256,256]{2,1,0:T(8,128)(2,1)S(1)}, bf16[2,256,256]{2,1,0:T(8,128)(2,1)S(1)}, u32[]{:S(2)}, u32[]{:S(2)}) collective-permute-start(bf16[2,256,256]{2,1,0:T(8,128)(2,1)S(1)} %collective-permute-done.4), channel_id=1, source_target_pairs={{0,4},{1,5},{2,6},{3,7},{4,8},{5,9},{6,10},{7,11},{8,12},{9,13},{1... | collective-permute-start | bytes 786440 | tf_op jit(solution)/shard_map/ppermute | solution.py:390
  27.6 6.2 %collective-permute-start.8 = (bf16[2,256,256]{2,1,0:T(8,128)(2,1)S(1)}, bf16[2,256,256]{2,1,0:T(8,128)(2,1)S(1)}, u32[]{:S(2)}, u32[]{:S(2)}) collective-permute-start(bf16[2,256,256]{2,1,0:T(8,128)(2,1)S(1)} %collective-permute-done.5), channel_id=1, source_target_pairs={{0,1},{1,2},{2,3},{3,0},{4,5},{5,6},{6,7},{7,4},{8,9},{9,10},{10,1... | collective-permute-start | bytes 786440 | tf_op jit(solution)/shard_map/ppermute | solution.py:390
  30.3 2.9 %collective-permute-start.6 = (f32[8,8]{1,0:T(8,128)S(1)}, f32[8,8]{1,0:T(8,128)S(1)}, u32[]{:S(2)}, u32[]{:S(2)}) collective-permute-start(f32[8,8]{1,0:T(8,128)S(1)} %add.115), channel_id=1, source_target_pairs={{0,32},{16,48},{32,0},{48,16},{64,96},{80,112},{96,64},{112,80},{1... | collective-permute-start | bytes 776 | tf_op jit(solution)/shard_map/ppermute | solution.py:394
  33.1 33.5 %copy-start.1 = (bf16[8,256,256]{2,1,0:T(8,128)(2,1)S(1)}, bf16[8,256,256]{2,1,0:T(8,128)(2,1)}, u32[]{:S(2)}) copy-start(bf16[8,256,256]{2,1,0:T(8,128)(2,1)} %near_ref.1) | copy-start | bytes 3145732
  34.0 33.2 %copy-start.3 = (bf16[8,256,256]{2,1,0:T(8,128)(2,1)}, bf16[8,256,256]{2,1,0:T(8,128)(2,1)S(1)}, u32[]{:S(2)}) copy-start(bf16[8,256,256]{2,1,0:T(8,128)(2,1)S(1)} %pad_maximum_fusion.refs_0_) | copy-start | bytes 3145732
  34.0 67.2 %copy-start.2 = (f32[512]{0:T(512)S(1)}, f32[512]{0:T(512)}, u32[]{:S(2)}) copy-start(f32[512]{0:T(512)} %param.9) | copy-start | bytes 6148
  34.0 31.2 %collective-permute-start.12 = (bf16[8,256,256]{2,1,0:T(8,128)(2,1)S(1)}, bf16[8,256,256]{2,1,0:T(8,128)(2,1)}, u32[]{:S(2)}, u32[]{:S(2)}) collective-permute-start(bf16[8,256,256]{2,1,0:T(8,128)(2,1)S(1)} %pad_maximum_fusion.refs_0_), channel_id=1, source_target_pairs={{0,1},{1,2},{2,3},{3,0},{4,5},{5,6},{6,7},{7,4},{8,9},{9,10},{10,1... | collective-permute-start | bytes 3145736 | tf_op jit(solution)/shard_map/ppermute | solution.py:390
  37.6 27.6 %copy-start.4 = (bf16[8,256,256]{2,1,0:T(8,128)(2,1)}, bf16[8,256,256]{2,1,0:T(8,128)(2,1)S(1)}, u32[]{:S(2)}) copy-start(bf16[8,256,256]{2,1,0:T(8,128)(2,1)S(1)} %pad_maximum_fusion.1.refs_4_) | copy-start | bytes 3145732
  37.6 27.6 %collective-permute-start.13 = (bf16[8,256,256]{2,1,0:T(8,128)(2,1)S(1)}, bf16[8,256,256]{2,1,0:T(8,128)(2,1)}, u32[]{:S(2)}, u32[]{:S(2)}) collective-permute-start(bf16[8,256,256]{2,1,0:T(8,128)(2,1)S(1)} %pad_maximum_fusion.1.refs_4_), channel_id=1, source_target_pairs={{0,4},{1,5},{2,6},{3,7},{4,8},{5,9},{6,10},{7,11},{8,12},{9,13},{1... | collective-permute-start | bytes 3145736 | tf_op jit(solution)/shard_map/ppermute | solution.py:390
  37.9 4.4 %collective-permute-start.9 = (f32[8,8]{1,0:T(8,128)S(1)}, f32[8,8]{1,0:T(8,128)S(1)}, u32[]{:S(2)}, u32[]{:S(2)}) collective-permute-start(f32[8,8]{1,0:T(8,128)S(1)} %add.116), channel_id=1, source_target_pairs={{0,8},{1,9},{2,10},{3,11},{4,12},{5,13},{6,14},{7,15},{8,0},{9,1},... | collective-permute-start | bytes 776 | tf_op jit(solution)/shard_map/ppermute | solution.py:394
  42.3 18.9 %collective-permute-start.10 = (f32[8,8]{1,0:T(8,128)S(1)}, f32[8,8]{1,0:T(8,128)S(1)}, u32[]{:S(2)}, u32[]{:S(2)}) collective-permute-start(f32[8,8]{1,0:T(8,128)S(1)} %add.117), channel_id=1, source_target_pairs={{0,4},{1,5},{2,6},{3,7},{4,0},{5,1},{6,2},{7,3},{8,12},{9,13},{10,... | collective-permute-start | bytes 776 | tf_op jit(solution)/shard_map/ppermute | solution.py:394
  61.2 4.0 %collective-permute-start.11 = (f32[8,8]{1,0:T(8,128)S(1)}, f32[8,8]{1,0:T(8,128)S(1)}, u32[]{:S(2)}, u32[]{:S(2)}) collective-permute-start(f32[8,8]{1,0:T(8,128)S(1)} %add.118), channel_id=1, source_target_pairs={{0,2},{1,3},{2,0},{3,1},{4,6},{5,7},{6,4},{7,5},{8,10},{9,11},{10,... | collective-permute-start | bytes 776 | tf_op jit(solution)/shard_map/ppermute | solution.py:394
  65.2 54.5 %collective-permute-start.15 = (bf16[8,256,256]{2,1,0:T(8,128)(2,1)}, bf16[8,256,256]{2,1,0:T(8,128)(2,1)}, u32[]{:S(2)}, u32[]{:S(2)}) collective-permute-start(bf16[8,256,256]{2,1,0:T(8,128)(2,1)} %collective-permute-done.12.refs_1_), channel_id=1, source_target_pairs={{0,1},{1,2},{2,3},{3,0},{4,5},{5,6},{6,7},{7,4},{8,9},{9,10},{10,1... | collective-permute-start | bytes 3145736 | tf_op jit(solution)/shard_map/ppermute | solution.py:390
  65.3 54.4 %collective-permute-start.16 = (bf16[8,256,256]{2,1,0:T(8,128)(2,1)}, bf16[8,256,256]{2,1,0:T(8,128)(2,1)}, u32[]{:S(2)}, u32[]{:S(2)}) collective-permute-start(bf16[8,256,256]{2,1,0:T(8,128)(2,1)} %collective-permute-done.13.refs_5_), channel_id=1, source_target_pairs={{0,4},{1,5},{2,6},{3,7},{4,8},{5,9},{6,10},{7,11},{8,12},{9,13},{1... | collective-permute-start | bytes 3145736 | tf_op jit(solution)/shard_map/ppermute | solution.py:390
  67.2 34.0 %collective-permute-start.14 = (f32[8,8]{1,0:T(8,128)S(1)}, f32[8,8]{1,0:T(8,128)S(1)}, u32[]{:S(2)}, u32[]{:S(2)}) collective-permute-start(f32[8,8]{1,0:T(8,128)S(1)} %add.119), channel_id=1, source_target_pairs={{0,1},{1,0},{2,3},{3,2},{4,5},{5,4},{6,7},{7,6},{8,9},{9,8},{10,11... | collective-permute-start | bytes 776 | tf_op jit(solution)/shard_map/ppermute | solution.py:394
  101.2 18.6 %copy-start.10 = (s32[4,24]{1,0:T(4,128)S(1)}, s32[4,24]{1,0:T(4,128)}, u32[]{:S(2)}) copy-start(s32[4,24]{1,0:T(4,128)} %param.10) | copy-start | bytes 1156
  101.2 18.7 %copy-start.11 = (s32[4]{0:T(128)S(1)}, s32[4]{0:T(128)}, u32[]{:S(2)}) copy-start(s32[4]{0:T(128)} %param.13) | copy-start | bytes 52
  101.2 18.7 %copy-start.7 = (s32[4,24]{1,0:T(4,128)S(1)}, s32[4,24]{1,0:T(4,128)}, u32[]{:S(2)}) copy-start(s32[4,24]{1,0:T(4,128)} %param.12) | copy-start | bytes 1156
  101.3 18.7 %copy-start.8 = (s32[4,24]{1,0:T(4,128)S(1)}, s32[4,24]{1,0:T(4,128)}, u32[]{:S(2)}) copy-start(s32[4,24]{1,0:T(4,128)} %param.11) | copy-start | bytes 1156
  119.7 23.2 %collective-permute-start.17 = (bf16[8,256,256]{2,1,0:T(8,128)(2,1)}, bf16[8,256,256]{2,1,0:T(8,128)(2,1)S(1)}, u32[]{:S(2)}, u32[]{:S(2)}) collective-permute-start(bf16[8,256,256]{2,1,0:T(8,128)(2,1)} %collective-permute-done.15.refs_2_), channel_id=1, source_target_pairs={{0,1},{1,2},{2,3},{3,0},{4,5},{5,6},{6,7},{7,4},{8,9},{9,10},{10,1... | collective-permute-start | bytes 3145736 | tf_op jit(solution)/shard_map/ppermute | solution.py:390
  119.8 23.1 %collective-permute-start.18 = (bf16[8,256,256]{2,1,0:T(8,128)(2,1)}, bf16[8,256,256]{2,1,0:T(8,128)(2,1)S(1)}, u32[]{:S(2)}, u32[]{:S(2)}) collective-permute-start(bf16[8,256,256]{2,1,0:T(8,128)(2,1)} %collective-permute-done.16.refs_6_), channel_id=1, source_target_pairs={{0,4},{1,5},{2,6},{3,7},{4,8},{5,9},{6,10},{7,11},{8,12},{9,13},{1... | collective-permute-start | bytes 3145736 | tf_op jit(solution)/shard_map/ppermute | solution.py:390
  120.6 22.4 %collective-permute-start.19 = (s32[4,72]{1,0:T(4,128)S(1)}, s32[4,72]{1,0:T(4,128)S(1)}, u32[]{:S(2)}, u32[]{:S(2)}) collective-permute-start(s32[4,72]{1,0:T(4,128)S(1)} %get-tuple-element.48), channel_id=1, source_target_pairs={{0,16},{16,0},{32,48},{48,32},{64,80},{80,64},{96,112},{112,96},{1... | collective-permute-start | bytes 3464 | tf_op jit(solution)/shard_map/ppermute | solution.py:394
  142.0 1.0 copy-start
  142.9 1.0 copy-start.5
  142.9 1.3 copy-start.6
  144.2 0.6 copy-start.9
  154.9 10.6 %collective-permute-start.20 = (f32[4,512,256]{2,1,0:T(8,128)}, f32[4,512,256]{2,1,0:T(8,128)}, u32[]{:S(2)}, u32[]{:S(2)}) collective-permute-start(f32[4,512,256]{2,1,0:T(8,128)} %ring_sums.3), channel_id=1, source_target_pairs={{0,16},{16,0},{32,48},{48,32},{64,80},{80,64},{96,112},{112,96},{1... | collective-permute-start | bytes 6291464 | tf_op jit(solution)/shard_map/ppermute | solution.py:394
Sparse Core Ops, SparseCore 0:
  11.1 93.2 all-gather.1

commit v3 on v2

--- a/solution.py
+++ b/solution.py
@@ -13,7 +13,7 @@
 SIDE = 4
 CACHED = 16
 HALF = CACHED // 2
-RING = 2
+RING = 1
 
 
 def dot32(left, right):
@@ -402,12 +402,16 @@
     row = lax.axis_index("row")
     core = row % 2
     kept = HALF - 2 * RING
-    share = 2 * kept // lax.axis_size("row")
+    size = near_cache.shape[1]
+    share = 2 * kept * size // lax.axis_size("row")
     at = row * share
     own = lax.dynamic_slice_in_dim(
-        response_cache, at // kept * HALF + 2 * RING + at % kept, share, 0
+        response_cache.reshape(CACHED * size, size),
+        at // (kept * size) * HALF * size + 2 * RING * size + at % (kept * size),
+        share,
+        0,
     )
-    blocks = lax.all_gather(own, ("col", "row"), axis=0, tiled=True)
+    blocks = lax.all_gather(own, ("col", "row"), axis=0, tiled=True).reshape(-1, size, size)
     line_y = [lax.dynamic_slice_in_dim(response_cache, core * HALF, RING, 0)]
     line_z = [lax.dynamic_slice_in_dim(response_cache, core * HALF + RING, RING, 0)]
     usable = jnp.arange(slots, dtype=jnp.int32)[None, :] < tile_counts[:, None]
@@ -431,7 +435,11 @@
             pairs = pairs + swap(pairs, axis, bit)
         return lax.optimization_barrier((pairs, to_z, to_y))
 
-    for stages in ((("row", 1),), (("row", 4),), (("row", 2),)):
+    for stages in (
+        (("row", 1), ("row", 4), ("row", 2)),
+        (("col", 8), ("col", 4)),
+        (("col", 2), ("col", 1)),
+    ):
         pairs, step_y, step_z = advance(
             pairs, ((line_y[-1], True), (line_z[-1], False)), stages
         )
@@ -439,19 +447,13 @@
         line_z.append(step_z)
     by_z = [jnp.concatenate(line_y, axis=0)]
     by_y = [jnp.concatenate(line_z, axis=0)]
-    pairs, step_z, step_y = advance(
-        pairs, ((by_z[-1], False), (by_y[-1], True)), (("col", 8), ("col", 4), ("col", 2))
-    )
-    by_z.append(step_z)
-    by_y.append(step_y)
+    for _ in range(2):
+        pairs, step_z, step_y = advance(pairs, ((by_z[-1], False), (by_y[-1], True)), ())
+        by_z.append(step_z)
+        by_y.append(step_y)
+    step_z, step_y = hop(by_z[-1], False), hop(by_y[-1], True)
     info_other = swap(info_other, "row", 1)
-    pairs = pairs + swap(pairs, "col", 1)
-    step_z, step_y = hop(by_z[-1], False), hop(by_y[-1], True)
     work, upper = lead_start(pairs, near_cache, turned, lead_diag)
-    work, step_z, step_y = lax.optimization_barrier((work, step_z, step_y))
-    by_z.append(step_z)
-    by_y.append(step_y)
-    step_z, step_y = hop(by_z[-1], False), hop(by_y[-1], True)
     lead_factor, inverse = lead_end(work, upper)
     inverse, step_z, step_y = lax.optimization_barrier((inverse, step_z, step_y))
     pieces = by_z + [step_z] + by_y + [step_y]

time: 187 us -> 161 us (0.86)
  waiting for transfers between devices: 46.2 us -> 34 us
  starting transfers between devices: 47.9 us -> 35.9 us
    ppermute x9, waiting for transfers between devices: 44.9 us -> 15.8 us  [swap(): lax.ppermute(value, axis, [(i, i ^ bit) for i in range(lax.axis_size(axis...]
    ppermute x12, waiting for transfers between devices: 1.24 us -> 18.1 us  [hop(): return lax.ppermute(value, ('row', 'col'), moves)]
    ppermute x9, starting transfers between devices: 29.5 us -> 20.4 us  [swap(): lax.ppermute(value, axis, [(i, i ^ bit) for i in range(lax.axis_size(axis...]
    pallas_call x2, Pallas kernels: 19.3 us -> 15.6 us  [ring_sums(): pl.pallas_call(functools.partial(ring_kernel, slots), out_shape=jax.Shape...]
    ppermute x12, starting transfers between devices: 18.4 us -> 15.5 us  [hop(): return lax.ppermute(value, ('row', 'col'), moves)]
    pallas_call x1, Pallas kernels: 12.7 us -> 15.6 us  [far(): pl.pallas_call(functools.partial(far_kernel, slots), out_shape=jax.ShapeD...]
  transfers between devices with their start and end apart: 22 -> 22, of which waited for: 10 -> 11; matrix products, arithmetic and copies ran while one was open for 3% -> 3% of each run, Pallas kernels for 29% -> 32%
where the time goes in v3:
time: 161 us; the launch traced here: 160 us
  Pallas kernels  66.1 us (41%)
  starting transfers between devices  35.9 us (22%)
  waiting for transfers between devices  34 us (21%)
  between operations  14.3 us (9%)
  local copies, waits for them, and re-layouts  6.88 us (4%)
  other arithmetic  2.44 us (2%)
    ppermute x9, starting transfers between devices, swap(): lax.ppermute(value, axis, [(i, i ^ bit) for i in range(lax.axis_size(axis...  20.4 us
    pallas_call x1, Pallas kernels, lead_start(): pl.pallas_call(lead_start_kernel, out_shape=(jax.ShapeDtypeStruct((whole,...  18.4 us
    ppermute x12, waiting for transfers between devices, hop(): return lax.ppermute(value, ('row', 'col'), moves)  18.1 us
    pallas_call x1, Pallas kernels, lead_end(): pl.pallas_call(lead_end_kernel, out_shape=(square, square), in_specs=[VME...  16.6 us
    ppermute x9, waiting for transfers between devices, swap(): lax.ppermute(value, axis, [(i, i ^ bit) for i in range(lax.axis_size(axis...  15.8 us
    pallas_call x2, Pallas kernels, ring_sums(): pl.pallas_call(functools.partial(ring_kernel, slots), out_shape=jax.Shape...  15.6 us
    pallas_call x1, Pallas kernels, far(): pl.pallas_call(functools.partial(far_kernel, slots), out_shape=jax.ShapeD...  15.6 us
    ppermute x12, starting transfers between devices, hop(): return lax.ppermute(value, ('row', 'col'), moves)  15.5 us
  transfers between devices with their start and end apart: 22, of which 11 were waited for; matrix products, arithmetic and copies ran while one was open for 3% of the time, Pallas kernels for 32%

profile of v3, /device:TPU:7, one launch (start us, length us, event | category | flops | bytes accessed | tf_op | source)
XLA Modules:
  0.0 159.7 jit_solution(10899746164619876940)
XLA Ops:
  7.2 0.0 copy-start.8
  7.2 0.0 copy-start.5
  7.2 0.0 copy-start.6
  7.2 0.0 all-gather.2.cloned.1.call-start
  7.3 1.7 %constant_dynamic-slice_fusion = bf16[384,256]{1,0:T(8,128)(2,1)} fusion(bf16[4096,256]{1,0:T(8,128)(2,1)} %bitcast.8, s32[]{:T(128)S(6)} %select_n.130), kind=kLoop, calls=%fused_computation.41 | loop fusion | bytes 393220 | tf_op jit(solution)/shard_map/dynamic_slice | solution.py:408
  9.0 0.0 all-gather.2.cloned.1.call-update
  9.1 1.0 constant_dynamic-slice_fusion.1
  10.1 2.8 %collective-permute-start.3 = (bf16[1,256,256]{2,1,0:T(8,128)(2,1)S(1)}, bf16[1,256,256]{2,1,0:T(8,128)(2,1)S(1)}, u32[]{:S(2)}, u32[]{:S(2)}) collective-permute-start(bf16[1,256,256]{2,1,0:T(8,128)(2,1)S(1)} %get-tuple-element.47), channel_id=1, source_target_pairs={{0,4},{1,5},{2,6},{3,7},{4,8},{5,9},{6,10},{7,11},{8,12},{9,13},{1... | collective-permute-start | bytes 393224 | tf_op jit(solution)/shard_map/ppermute | solution.py:390
  12.9 3.8 %collective-permute-start.4 = (bf16[1,256,256]{2,1,0:T(8,128)(2,1)S(1)}, bf16[1,256,256]{2,1,0:T(8,128)(2,1)S(1)}, u32[]{:S(2)}, u32[]{:S(2)}) collective-permute-start(bf16[1,256,256]{2,1,0:T(8,128)(2,1)S(1)} %get-tuple-element.46), channel_id=1, source_target_pairs={{0,1},{1,2},{2,3},{3,0},{4,5},{5,6},{6,7},{7,4},{8,9},{9,10},{10,1... | collective-permute-start | bytes 393224 | tf_op jit(solution)/shard_map/ppermute | solution.py:390
  16.6 0.7 iota_compare_fusion.2
  17.4 0.7 iota_compare_fusion
  18.1 0.1 convert_reduce_fusion
  18.2 0.1 collective-permute-start
  18.3 1.2 collective-permute-done
  19.4 1.1 collective-permute-start.1
  20.6 2.8 %collective-permute-done.1 = f32[8,8]{1,0:T(8,128)S(1)} collective-permute-done((f32[8,8]{1,0:T(8,128)S(1)}, f32[8,8]{1,0:T(8,128)S(1)}, u32[]{:S(2)}, u32[]{:S(2)}) %collective-permute-start.1) | collective-permute-done | bytes 288 | tf_op jit(solution)/shard_map/ppermute | solution.py:394
  23.4 0.6 collective-permute-start.2
  23.9 2.3 %collective-permute-done.2 = f32[8,8]{1,0:T(8,128)S(1)} collective-permute-done((f32[8,8]{1,0:T(8,128)S(1)}, f32[8,8]{1,0:T(8,128)S(1)}, u32[]{:S(2)}, u32[]{:S(2)}) %collective-permute-start.2) | collective-permute-done | bytes 288 | tf_op jit(solution)/shard_map/ppermute | solution.py:394
  26.3 0.1 collective-permute-start.7
  26.4 0.1 collective-permute-start.8
  26.5 1.7 %collective-permute-start.5 = (f32[8,8]{1,0:T(8,128)S(1)}, f32[8,8]{1,0:T(8,128)S(1)}, u32[]{:S(2)}, u32[]{:S(2)}) collective-permute-start(f32[8,8]{1,0:T(8,128)S(1)} %add.110), channel_id=1, source_target_pairs={{0,8},{1,9},{2,10},{3,11},{4,12},{5,13},{6,14},{7,15},{8,0},{9,1},... | collective-permute-start | bytes 776 | tf_op jit(solution)/shard_map/ppermute | solution.py:394
  28.2 2.3 %collective-permute-done.5 = f32[8,8]{1,0:T(8,128)S(1)} collective-permute-done((f32[8,8]{1,0:T(8,128)S(1)}, f32[8,8]{1,0:T(8,128)S(1)}, u32[]{:S(2)}, u32[]{:S(2)}) %collective-permute-start.5) | collective-permute-done | bytes 288 | tf_op jit(solution)/shard_map/ppermute | solution.py:394
  30.5 1.3 collective-permute-start.6
  31.8 1.6 collective-permute-done.6
  33.3 0.0 collective-permute-done.7
  33.3 0.0 collective-permute-done.8
  33.4 2.2 %collective-permute-start.11 = (bf16[1,256,256]{2,1,0:T(8,128)(2,1)S(1)}, bf16[1,256,256]{2,1,0:T(8,128)(2,1)S(1)}, u32[]{:S(2)}, u32[]{:S(2)}) collective-permute-start(bf16[1,256,256]{2,1,0:T(8,128)(2,1)S(1)} %collective-permute-done.7), channel_id=1, source_target_pairs={{0,4},{1,5},{2,6},{3,7},{4,8},{5,9},{6,10},{7,11},{8,12},{9,13},{1... | collective-permute-start | bytes 393224 | tf_op jit(solution)/shard_map/ppermute | solution.py:390
  35.5 1.2 collective-permute-start.12
  36.7 0.7 collective-permute-start.9
  37.4 3.2 %collective-permute-done.9 = f32[8,8]{1,0:T(8,128)S(1)} collective-permute-done((f32[8,8]{1,0:T(8,128)S(1)}, f32[8,8]{1,0:T(8,128)S(1)}, u32[]{:S(2)}, u32[]{:S(2)}) %collective-permute-start.9) | collective-permute-done | bytes 288 | tf_op jit(solution)/shard_map/ppermute | solution.py:394
  40.6 0.3 collective-permute-start.10
  40.9 2.4 %collective-permute-done.10 = f32[8,8]{1,0:T(8,128)S(1)} collective-permute-done((f32[8,8]{1,0:T(8,128)S(1)}, f32[8,8]{1,0:T(8,128)S(1)}, u32[]{:S(2)}, u32[]{:S(2)}) %collective-permute-start.10) | collective-permute-done | bytes 288 | tf_op jit(solution)/shard_map/ppermute | solution.py:394
  43.4 0.0 collective-permute-done.11
  43.4 0.0 collective-permute-done.12
  43.4 0.1 pad_maximum_fusion.refs_0_
  43.5 1.2 collective-permute-start.13
  44.7 0.1 pad_maximum_fusion.1.refs_4_
  44.8 0.1 collective-permute-start.14
  44.9 15.4 %collective-permute-done.13.refs_1_ = bf16[4,256,256]{2,1,0:T(8,128)(2,1)} collective-permute-done((bf16[4,256,256]{2,1,0:T(8,128)(2,1)S(1)}, bf16[4,256,256]{2,1,0:T(8,128)(2,1)}, u32[]{:S(2)}, u32[]{:S(2)}) %collective-permute-start.13) | collective-permute-done | bytes 524320 | tf_op jit(solution)/shard_map/ppermute | solution.py:390
  60.3 0.4 collective-permute-done.14.refs_5_
  60.8 1.1 collective-permute-start.15
  61.9 0.3 collective-permute-start.16
  62.2 0.1 select_select_fusion
  62.3 0.7 add_add_fusion.2
  63.0 3.7 %collective-permute-start.19 = (s32[4,72]{1,0:T(4,128)S(1)}, s32[4,72]{1,0:T(4,128)S(1)}, u32[]{:S(2)}, u32[]{:S(2)}) collective-permute-start(s32[4,72]{1,0:T(4,128)S(1)} %get-tuple-element.48), channel_id=1, source_target_pairs={{0,16},{16,0},{32,48},{48,32},{64,80},{80,64},{96,112},{112,96},{1... | collective-permute-start | bytes 3464 | tf_op jit(solution)/shard_map/ppermute | solution.py:394
  66.7 0.5 copy.10
  67.2 1.1 concatenate.22.turned_ref.turned_hbm
  68.3 0.8 collective-permute-done.15.refs_2_
  69.1 1.4 collective-permute-done.16.refs_6_
  70.5 0.9 collective-permute-start.17
  71.5 1.7 %collective-permute-start.18 = (bf16[4,256,256]{2,1,0:T(8,128)(2,1)}, bf16[4,256,256]{2,1,0:T(8,128)(2,1)S(1)}, u32[]{:S(2)}, u32[]{:S(2)}) collective-permute-start(bf16[4,256,256]{2,1,0:T(8,128)(2,1)} %collective-permute-done.16.refs_6_), channel_id=1, source_target_pairs={{0,4},{1,5},{2,6},{3,7},{4,8},{5,9},{6,10},{7,11},{8,12},{9,13},{1... | collective-permute-start | bytes 1572872 | tf_op jit(solution)/shard_map/ppermute | solution.py:390
  73.1 18.4 %lead_start.1 = (f32[512,1024]{1,0:T(8,128)S(1)}, f32[512,512]{1,0:T(8,128)S(1)}) custom-call(f32[8,8]{1,0:T(8,128)S(1)} %add.118.pairs_ref, bf16[8,256,256]{2,1,0:T(8,128)(2,1)S(1)} %copy-done.1, bf16[8,256,256]{2,1,0:T(8,128)(2,1)S(1)} %bitcast.5, f32[1,512]{1,0:T(1,128)S(1)} %bitcast.6), custom_call_target="tpu_custom_call" | custom-call | flops 8999999488 | bytes 6291456 | tf_op jit(solution)/shard_map/lead_start/pallas_call | solution.py:126
  91.5 16.6 %lead_end.1 = (f32[512,512]{1,0:T(8,128)}, f32[512,512]{1,0:T(8,128)S(1)}) custom-call(f32[512,1024]{1,0:T(8,128)S(1)} %get-tuple-element.37.work_ref, f32[512,512]{1,0:T(8,128)S(1)} %get-tuple-element.38.upper_ref), custom_call_target="tpu_custom_call" | custom-call | flops 8999999488 | bytes 6291456 | tf_op jit(solution)/shard_map/lead_end/pallas_call | solution.py:145
  108.1 1.0 copy-done
  109.0 0.0 collective-permute-done.17.refs_3_
  109.1 0.0 collective-permute-done.19.info_ref
  109.1 0.7 copy-done.9
  109.8 0.2 copy-done.10
  110.0 0.6 copy-done.11
  110.6 8.0 %ring_sums.3 = f32[4,512,256]{2,1,0:T(8,128)} custom-call(s32[4,72]{1,0:T(4,128)} %copy-done.11, bf16[9,256,256]{2,1,0:T(8,128)(2,1)} %concatenate.22.turned_ref.turned_hbm, bf16[4,256,256]{2,1,0:T(8,128)(2,1)} %copy-done.3, bf16[4,256,256]{2,1,0:T(8,128)(2,1)} %collective-permute-done.13.refs_1_, bf16[4,256,256]{2,1,0:T(8,128)(2,1)} %collective-permute-done.15.refs_2_, ...), custom_call_target="tpu_custom_call" | custom-call | flops 3000000000 | bytes 12582912 | tf_op jit(solution)/shard_map/ring_sums/pallas_call | solution.py:253
  118.6 10.9 %collective-permute-start.20 = (f32[4,512,256]{2,1,0:T(8,128)}, f32[4,512,256]{2,1,0:T(8,128)}, u32[]{:S(2)}, u32[]{:S(2)}) collective-permute-start(f32[4,512,256]{2,1,0:T(8,128)} %ring_sums.3), channel_id=1, source_target_pairs={{0,16},{16,0},{32,48},{48,32},{64,80},{80,64},{96,112},{112,96},{1... | collective-permute-start | bytes 6291464 | tf_op jit(solution)/shard_map/ppermute | solution.py:394
  129.6 7.6 %ring_sums.2.own_hbm = f32[4,512,256]{2,1,0:T(8,128)} custom-call(s32[4,72]{1,0:T(4,128)} %get-tuple-element.49.info_ref, bf16[9,256,256]{2,1,0:T(8,128)(2,1)} %concatenate.22.turned_ref.turned_hbm, bf16[4,256,256]{2,1,0:T(8,128)(2,1)} %copy-done.3, bf16[4,256,256]{2,1,0:T(8,128)(2,1)} %collective-permute-done.13.refs_1_, ...), custom_call_target="tpu_custom_call" | custom-call | flops 3000000000 | bytes 12582912 | tf_op jit(solution)/shard_map/ring_sums/pallas_call | solution.py:253
  137.2 0.0 all-gather.2.cloned.1.call-done
  137.2 15.6 %far.1 = f32[1024,512]{1,0:T(8,128)} custom-call(s32[4,72]{1,0:T(4,128)} %get-tuple-element.50.info_ref, f32[4,512,256]{2,1,0:T(8,128)} %ring_sums.2.own_hbm, f32[4,512,256]{2,1,0:T(8,128)} %collective-permute-done.20.other_hbm, bf16[192,256,256]{2,1,0:T(8,128)(2,1)} %bitcast.7, bf16[9,256,256]{2,1,0:T(8,128)(2,1)} %concatenate.22.turned_ref.turned_hbm, ...), custom_call_target="tpu_custom_call" | custom-call | tf_op jit(solution)/shard_map/far/pallas_call | solution.py:349
  (28 shorter events, 0.1 us)
Async XLA Ops:
  7.2 55.1 %copy-start.8 = (s32[4]{0:T(128)S(1)}, s32[4]{0:T(128)}, u32[]{:S(2)}) copy-start(s32[4]{0:T(128)} %param.13) | copy-start | bytes 52
  7.2 55.1 %copy-start.5 = (s32[4,24]{1,0:T(4,128)S(1)}, s32[4,24]{1,0:T(4,128)}, u32[]{:S(2)}) copy-start(s32[4,24]{1,0:T(4,128)} %param.12) | copy-start | bytes 1156
  7.2 55.1 %copy-start.6 = (s32[4,24]{1,0:T(4,128)S(1)}, s32[4,24]{1,0:T(4,128)}, u32[]{:S(2)}) copy-start(s32[4,24]{1,0:T(4,128)} %param.11) | copy-start | bytes 1156
  7.2 55.0 %copy-start.7 = (s32[4,24]{1,0:T(4,128)S(1)}, s32[4,24]{1,0:T(4,128)}, u32[]{:S(2)}) copy-start(s32[4,24]{1,0:T(4,128)} %param.10) | copy-start | bytes 1156
  7.2 59.5 %copy-start.1 = (bf16[8,256,256]{2,1,0:T(8,128)(2,1)S(1)}, bf16[8,256,256]{2,1,0:T(8,128)(2,1)}, u32[]{:S(2)}) copy-start(bf16[8,256,256]{2,1,0:T(8,128)(2,1)} %near_ref.1) | copy-start | bytes 3145732
  7.2 130.0 %all-gather.2.cloned.1.call-start = ((), (), s32[]{:S(2)}) async-start(), calls=%async_computation | async-start | bytes 25362432 | tf_op jit(solution)/shard_map/all_gather | solution.py:414
  10.1 16.2 %collective-permute-start.3 = (bf16[1,256,256]{2,1,0:T(8,128)(2,1)S(1)}, bf16[1,256,256]{2,1,0:T(8,128)(2,1)S(1)}, u32[]{:S(2)}, u32[]{:S(2)}) collective-permute-start(bf16[1,256,256]{2,1,0:T(8,128)(2,1)S(1)} %get-tuple-element.47), channel_id=1, source_target_pairs={{0,4},{1,5},{2,6},{3,7},{4,8},{5,9},{6,10},{7,11},{8,12},{9,13},{1... | collective-permute-start | bytes 393224 | tf_op jit(solution)/shard_map/ppermute | solution.py:390
  12.9 13.4 %collective-permute-start.4 = (bf16[1,256,256]{2,1,0:T(8,128)(2,1)S(1)}, bf16[1,256,256]{2,1,0:T(8,128)(2,1)S(1)}, u32[]{:S(2)}, u32[]{:S(2)}) collective-permute-start(bf16[1,256,256]{2,1,0:T(8,128)(2,1)S(1)} %get-tuple-element.46), channel_id=1, source_target_pairs={{0,1},{1,2},{2,3},{3,0},{4,5},{5,6},{6,7},{7,4},{8,9},{9,10},{10,1... | collective-permute-start | bytes 393224 | tf_op jit(solution)/shard_map/ppermute | solution.py:390
  18.2 1.2 collective-permute-start
  19.4 4.0 %collective-permute-start.1 = (f32[8,8]{1,0:T(8,128)S(1)}, f32[8,8]{1,0:T(8,128)S(1)}, u32[]{:S(2)}, u32[]{:S(2)}) collective-permute-start(f32[8,8]{1,0:T(8,128)S(1)} %add.108), channel_id=1, source_target_pairs={{0,64},{16,80},{32,96},{48,112},{64,0},{80,16},{96,32},{112,48},{1... | collective-permute-start | bytes 776 | tf_op jit(solution)/shard_map/ppermute | solution.py:394
  23.4 2.9 %collective-permute-start.2 = (f32[8,8]{1,0:T(8,128)S(1)}, f32[8,8]{1,0:T(8,128)S(1)}, u32[]{:S(2)}, u32[]{:S(2)}) collective-permute-start(f32[8,8]{1,0:T(8,128)S(1)} %add.109), channel_id=1, source_target_pairs={{0,32},{16,48},{32,0},{48,16},{64,96},{80,112},{96,64},{112,80},{1... | collective-permute-start | bytes 776 | tf_op jit(solution)/shard_map/ppermute | solution.py:394
  26.3 7.1 %collective-permute-start.7 = (bf16[1,256,256]{2,1,0:T(8,128)(2,1)S(1)}, bf16[1,256,256]{2,1,0:T(8,128)(2,1)S(1)}, u32[]{:S(2)}, u32[]{:S(2)}) collective-permute-start(bf16[1,256,256]{2,1,0:T(8,128)(2,1)S(1)} %collective-permute-done.3), channel_id=1, source_target_pairs={{0,4},{1,5},{2,6},{3,7},{4,8},{5,9},{6,10},{7,11},{8,12},{9,13},{1... | collective-permute-start | bytes 393224 | tf_op jit(solution)/shard_map/ppermute | solution.py:390
  26.4 7.0 %collective-permute-start.8 = (bf16[1,256,256]{2,1,0:T(8,128)(2,1)S(1)}, bf16[1,256,256]{2,1,0:T(8,128)(2,1)S(1)}, u32[]{:S(2)}, u32[]{:S(2)}) collective-permute-start(bf16[1,256,256]{2,1,0:T(8,128)(2,1)S(1)} %collective-permute-done.4), channel_id=1, source_target_pairs={{0,1},{1,2},{2,3},{3,0},{4,5},{5,6},{6,7},{7,4},{8,9},{9,10},{10,1... | collective-permute-start | bytes 393224 | tf_op jit(solution)/shard_map/ppermute | solution.py:390
  26.5 4.0 %collective-permute-start.5 = (f32[8,8]{1,0:T(8,128)S(1)}, f32[8,8]{1,0:T(8,128)S(1)}, u32[]{:S(2)}, u32[]{:S(2)}) collective-permute-start(f32[8,8]{1,0:T(8,128)S(1)} %add.110), channel_id=1, source_target_pairs={{0,8},{1,9},{2,10},{3,11},{4,12},{5,13},{6,14},{7,15},{8,0},{9,1},... | collective-permute-start | bytes 776 | tf_op jit(solution)/shard_map/ppermute | solution.py:394
  30.5 2.9 %collective-permute-start.6 = (f32[8,8]{1,0:T(8,128)S(1)}, f32[8,8]{1,0:T(8,128)S(1)}, u32[]{:S(2)}, u32[]{:S(2)}) collective-permute-start(f32[8,8]{1,0:T(8,128)S(1)} %add.115), channel_id=1, source_target_pairs={{0,4},{1,5},{2,6},{3,7},{4,0},{5,1},{6,2},{7,3},{8,12},{9,13},{10,... | collective-permute-start | bytes 776 | tf_op jit(solution)/shard_map/ppermute | solution.py:394
  33.4 10.0 %collective-permute-start.11 = (bf16[1,256,256]{2,1,0:T(8,128)(2,1)S(1)}, bf16[1,256,256]{2,1,0:T(8,128)(2,1)S(1)}, u32[]{:S(2)}, u32[]{:S(2)}) collective-permute-start(bf16[1,256,256]{2,1,0:T(8,128)(2,1)S(1)} %collective-permute-done.7), channel_id=1, source_target_pairs={{0,4},{1,5},{2,6},{3,7},{4,8},{5,9},{6,10},{7,11},{8,12},{9,13},{1... | collective-permute-start | bytes 393224 | tf_op jit(solution)/shard_map/ppermute | solution.py:390
  35.5 7.9 %collective-permute-start.12 = (bf16[1,256,256]{2,1,0:T(8,128)(2,1)S(1)}, bf16[1,256,256]{2,1,0:T(8,128)(2,1)S(1)}, u32[]{:S(2)}, u32[]{:S(2)}) collective-permute-start(bf16[1,256,256]{2,1,0:T(8,128)(2,1)S(1)} %collective-permute-done.8), channel_id=1, source_target_pairs={{0,1},{1,2},{2,3},{3,0},{4,5},{5,6},{6,7},{7,4},{8,9},{9,10},{10,1... | collective-permute-start | bytes 393224 | tf_op jit(solution)/shard_map/ppermute | solution.py:390
  36.7 4.0 %collective-permute-start.9 = (f32[8,8]{1,0:T(8,128)S(1)}, f32[8,8]{1,0:T(8,128)S(1)}, u32[]{:S(2)}, u32[]{:S(2)}) collective-permute-start(f32[8,8]{1,0:T(8,128)S(1)} %add.116), channel_id=1, source_target_pairs={{0,2},{1,3},{2,0},{3,1},{4,6},{5,7},{6,4},{7,5},{8,10},{9,11},{10,... | collective-permute-start | bytes 776 | tf_op jit(solution)/shard_map/ppermute | solution.py:394
  40.6 2.8 %collective-permute-start.10 = (f32[8,8]{1,0:T(8,128)S(1)}, f32[8,8]{1,0:T(8,128)S(1)}, u32[]{:S(2)}, u32[]{:S(2)}) collective-permute-start(f32[8,8]{1,0:T(8,128)S(1)} %add.117), channel_id=1, source_target_pairs={{0,1},{1,0},{2,3},{3,2},{4,5},{5,4},{6,7},{7,6},{8,9},{9,8},{10,11... | collective-permute-start | bytes 776 | tf_op jit(solution)/shard_map/ppermute | solution.py:394
  43.5 24.8 %copy-start.3 = (bf16[4,256,256]{2,1,0:T(8,128)(2,1)}, bf16[4,256,256]{2,1,0:T(8,128)(2,1)S(1)}, u32[]{:S(2)}) copy-start(bf16[4,256,256]{2,1,0:T(8,128)(2,1)S(1)} %pad_maximum_fusion.refs_0_) | copy-start | bytes 1572868
  43.5 16.9 %collective-permute-start.13 = (bf16[4,256,256]{2,1,0:T(8,128)(2,1)S(1)}, bf16[4,256,256]{2,1,0:T(8,128)(2,1)}, u32[]{:S(2)}, u32[]{:S(2)}) collective-permute-start(bf16[4,256,256]{2,1,0:T(8,128)(2,1)S(1)} %pad_maximum_fusion.refs_0_), channel_id=1, source_target_pairs={{0,1},{1,2},{2,3},{3,0},{4,5},{5,6},{6,7},{7,4},{8,9},{9,10},{10,1... | collective-permute-start | bytes 1572872 | tf_op jit(solution)/shard_map/ppermute | solution.py:390
  44.8 23.5 %copy-start.4 = (bf16[4,256,256]{2,1,0:T(8,128)(2,1)}, bf16[4,256,256]{2,1,0:T(8,128)(2,1)S(1)}, u32[]{:S(2)}) copy-start(bf16[4,256,256]{2,1,0:T(8,128)(2,1)S(1)} %pad_maximum_fusion.1.refs_4_) | copy-start | bytes 1572868
  44.8 15.9 %collective-permute-start.14 = (bf16[4,256,256]{2,1,0:T(8,128)(2,1)S(1)}, bf16[4,256,256]{2,1,0:T(8,128)(2,1)}, u32[]{:S(2)}, u32[]{:S(2)}) collective-permute-start(bf16[4,256,256]{2,1,0:T(8,128)(2,1)S(1)} %pad_maximum_fusion.1.refs_4_), channel_id=1, source_target_pairs={{0,4},{1,5},{2,6},{3,7},{4,8},{5,9},{6,10},{7,11},{8,12},{9,13},{1... | collective-permute-start | bytes 1572872 | tf_op jit(solution)/shard_map/ppermute | solution.py:390
  60.8 8.3 %collective-permute-start.15 = (bf16[4,256,256]{2,1,0:T(8,128)(2,1)}, bf16[4,256,256]{2,1,0:T(8,128)(2,1)}, u32[]{:S(2)}, u32[]{:S(2)}) collective-permute-start(bf16[4,256,256]{2,1,0:T(8,128)(2,1)} %collective-permute-done.13.refs_1_), channel_id=1, source_target_pairs={{0,1},{1,2},{2,3},{3,0},{4,5},{5,6},{6,7},{7,4},{8,9},{9,10},{10,1... | collective-permute-start | bytes 1572872 | tf_op jit(solution)/shard_map/ppermute | solution.py:390
  61.9 8.6 %collective-permute-start.16 = (bf16[4,256,256]{2,1,0:T(8,128)(2,1)}, bf16[4,256,256]{2,1,0:T(8,128)(2,1)}, u32[]{:S(2)}, u32[]{:S(2)}) collective-permute-start(bf16[4,256,256]{2,1,0:T(8,128)(2,1)} %collective-permute-done.14.refs_5_), channel_id=1, source_target_pairs={{0,4},{1,5},{2,6},{3,7},{4,8},{5,9},{6,10},{7,11},{8,12},{9,13},{1... | collective-permute-start | bytes 1572872 | tf_op jit(solution)/shard_map/ppermute | solution.py:390
  63.0 10.1 %copy-start.2 = (f32[512]{0:T(512)S(1)}, f32[512]{0:T(512)}, u32[]{:S(2)}) copy-start(f32[512]{0:T(512)} %param.9) | copy-start | bytes 6148
  63.0 46.1 %collective-permute-start.19 = (s32[4,72]{1,0:T(4,128)S(1)}, s32[4,72]{1,0:T(4,128)S(1)}, u32[]{:S(2)}, u32[]{:S(2)}) collective-permute-start(s32[4,72]{1,0:T(4,128)S(1)} %get-tuple-element.48), channel_id=1, source_target_pairs={{0,16},{16,0},{32,48},{48,32},{64,80},{80,64},{96,112},{112,96},{1... | collective-permute-start | bytes 3464 | tf_op jit(solution)/shard_map/ppermute | solution.py:394
  70.5 38.5 %collective-permute-start.17 = (bf16[4,256,256]{2,1,0:T(8,128)(2,1)}, bf16[4,256,256]{2,1,0:T(8,128)(2,1)S(1)}, u32[]{:S(2)}, u32[]{:S(2)}) collective-permute-start(bf16[4,256,256]{2,1,0:T(8,128)(2,1)} %collective-permute-done.15.refs_2_), channel_id=1, source_target_pairs={{0,1},{1,2},{2,3},{3,0},{4,5},{5,6},{6,7},{7,4},{8,9},{9,10},{10,1... | collective-permute-start | bytes 1572872 | tf_op jit(solution)/shard_map/ppermute | solution.py:390
  71.5 37.6 %collective-permute-start.18 = (bf16[4,256,256]{2,1,0:T(8,128)(2,1)}, bf16[4,256,256]{2,1,0:T(8,128)(2,1)S(1)}, u32[]{:S(2)}, u32[]{:S(2)}) collective-permute-start(bf16[4,256,256]{2,1,0:T(8,128)(2,1)} %collective-permute-done.16.refs_6_), channel_id=1, source_target_pairs={{0,4},{1,5},{2,6},{3,7},{4,8},{5,9},{6,10},{7,11},{8,12},{9,13},{1... | collective-permute-start | bytes 1572872 | tf_op jit(solution)/shard_map/ppermute | solution.py:390
  108.1 1.0 copy-start
  109.0 0.8 copy-start.9
  109.1 1.0 copy-start.10
  110.0 0.6 copy-start.11
  118.6 18.5 %collective-permute-start.20 = (f32[4,512,256]{2,1,0:T(8,128)}, f32[4,512,256]{2,1,0:T(8,128)}, u32[]{:S(2)}, u32[]{:S(2)}) collective-permute-start(f32[4,512,256]{2,1,0:T(8,128)} %ring_sums.3), channel_id=1, source_target_pairs={{0,16},{16,0},{32,48},{48,32},{64,80},{80,64},{96,112},{112,96},{1... | collective-permute-start | bytes 6291464 | tf_op jit(solution)/shard_map/ppermute | solution.py:394
Sparse Core Ops, SparseCore 0:
  11.1 105.8 all-gather.1

commit v4 on v0

--- a/solution.py
+++ b/solution.py
@@ -9,11 +9,20 @@
 
 HIGHEST = lax.Precision.HIGHEST
 BLOCK = 128
-GROUP = 4
+GROUP = 12
+AHEAD = 2
 
 
 def dot32(left, right):
     return jnp.dot(left, right, precision=HIGHEST, preferred_element_type=jnp.float32)
+
+
+def split3(value):
+    high = value.astype(jnp.bfloat16)
+    rest = value - high.astype(jnp.float32)
+    middle = rest.astype(jnp.bfloat16)
+    low = (rest - middle.astype(jnp.float32)).astype(jnp.bfloat16)
+    return high, middle, low
 
 
 def spread_rows(value, row):
@@ -58,7 +67,7 @@
     return jnp.concatenate(main, axis=0), jnp.concatenate(side, axis=0)
 
 
-def lead_kernel(pairs_ref, near_ref, turned_ref, diag_ref, factor_ref, inverse_ref, work, upper):
+def lead_kernel(pairs_ref, near_ref, turned_ref, diag_ref, factor_ref, parts_ref, work, upper):
     near_total, size, _ = near_ref.shape
     whole = 2 * size
     first_sums = [sum(pairs_ref[j, k] for k in range(near_total)) for j in range(near_total)]
@@ -97,7 +106,10 @@
 
     lax.fori_loop(0, whole // BLOCK, step, 0)
     factor_ref[...] = upper[...].T
-    inverse_ref[...] = work[:, whole:].T
+    high, middle, low = split3(work[:, whole:].T)
+    for n, part in enumerate((high, middle, high, low, middle, high)):
+        parts_ref[n * size : (n + 1) * size, :] = part[:size, :size]
+        parts_ref[(6 + 2 * n) * size : (8 + 2 * n) * size, :] = part[:, size:]
 
 
 def lead(pairs, near_cache, turned_near, lead_diag):
@@ -107,7 +119,7 @@
         lead_kernel,
         out_shape=(
             jax.ShapeDtypeStruct((whole, whole), jnp.float32),
-            jax.ShapeDtypeStruct((whole, whole), jnp.float32),
+            jax.ShapeDtypeStruct((9 * whole, whole // 2), jnp.bfloat16),
         ),
         in_specs=[pl.BlockSpec(memory_space=pltpu.SMEM), vmem, vmem, vmem],
         out_specs=(vmem, vmem),
@@ -121,87 +133,116 @@
 
 
 def far_kernel(
-    counts_ref, offsets_ref, first_ref, second_ref, blocks_ref, turned_ref, inverse_ref, out_ref,
-    held, total, arrived,
+    slots, info_ref, blocks_ref, near_hbm, parts_hbm, out_hbm, held, near_ref, parts_ref, out_ref,
+    arrived, loaded, stored,
 ):
-    tiles, slots = offsets_ref.shape
-    size = turned_ref.shape[1]
-    tile = pl.program_id(0)
+    tiles = info_ref.shape[0]
+    size = near_ref.shape[1]
     rounds = slots // GROUP
-    empty = turned_ref.shape[0] - 1
-
-    def fetch(t, s):
-        return pltpu.make_async_copy(
-            blocks_ref.at[offsets_ref[t, s]],
-            held.at[t, pl.ds(pl.multiple_of(s * size, size), size), :],
-            arrived.at[t, s],
-        )
-
-    def rounds_of(t):
-        return (counts_ref[t] + GROUP - 1) // GROUP
-
-    @pl.when(tile == 0)
-    def start():
-        for t in range(tiles):
-            def begin(s, carry):
-                fetch(t, s).start()
-                return carry
-
-            lax.fori_loop(0, rounds_of(t) * GROUP, begin, 0)
-
-    total[...] = jnp.zeros_like(total)
-
-    def one_round(r, carry):
+    last = tiles * rounds
+
+    def begin(k):
+        t, r = k // rounds, k % rounds
         for i in range(GROUP):
-            fetch(tile, r * GROUP + i).wait()
-        firsts = []
-        seconds = []
+            pltpu.make_async_copy(
+                blocks_ref.at[info_ref[t, r * GROUP + i]], held.at[k, i], arrived.at[k]
+            ).start()
+
+    def finish(k):
+        pltpu.make_async_copy(blocks_ref.at[pl.ds(0, GROUP)], held.at[k], arrived.at[k]).wait()
+
+    def store(t):
+        rows = pl.ds(pl.multiple_of(t * size, size), size)
+        return pltpu.make_async_copy(out_ref.at[t], out_hbm.at[rows, :], stored.at[t])
+
+    load_near = pltpu.make_async_copy(near_hbm, near_ref, loaded.at[0])
+    load_parts = pltpu.make_async_copy(parts_hbm, parts_ref, loaded.at[1])
+    load_near.start()
+    for k in range(AHEAD):
+        begin(k)
+    load_parts.start()
+    load_near.wait()
+
+    def step(k, carry):
+        @pl.when(k + AHEAD < last)
+        def following():
+            begin(k + AHEAD)
+
+        t, r = k // rounds, k % rounds
+        finish(k)
+        rows = []
         for i in range(GROUP):
             s = r * GROUP + i
-            used = s < counts_ref[tile]
-            firsts.append(turned_ref[jnp.where(used, first_ref[tile, s], empty)])
-            seconds.append(turned_ref[jnp.where(used, second_ref[tile, s], empty)])
-        left = jnp.concatenate(
-            [jnp.concatenate(firsts, axis=1), jnp.concatenate(seconds, axis=1)], axis=0
+            rows.append(
+                jnp.concatenate(
+                    [near_ref[info_ref[t, slots + s]], near_ref[info_ref[t, 2 * slots + s]]],
+                    axis=1,
+                )
+            )
+        change = lax.dot_general(
+            held[k].reshape(GROUP * size, size),
+            jnp.concatenate(rows, axis=0),
+            (((0,), (0,)), ((), ())),
+            preferred_element_type=jnp.float32,
         )
-        span = GROUP * size
-        right = held[tile, pl.ds(pl.multiple_of(r * span, span), span), :]
-        total[...] += jnp.dot(left, right, preferred_element_type=jnp.float32)
+
+        @pl.when(r == 0)
+        def first():
+            out_ref[t] = change
+
+        @pl.when(r > 0)
+        def later():
+            out_ref[t] += change
+
+        @pl.when(k == 0)
+        def factors():
+            load_parts.wait()
+
+        @pl.when(r == rounds - 1)
+        def solve():
+            high, middle, low = split3(out_ref[t])
+            wide = jnp.concatenate([high, high, middle, high, middle, low], axis=1)
+            narrow = jnp.concatenate(
+                [p[:, :size] for p in (high, high, middle, high, middle, low)], axis=1
+            )
+            out_ref[t, :, :size] = jnp.dot(
+                narrow, parts_ref[: 6 * size, :], preferred_element_type=jnp.float32
+            )
+            out_ref[t, :, size:] = jnp.dot(
+                wide, parts_ref[6 * size :, :], preferred_element_type=jnp.float32
+            )
+            store(t).start()
+
         return carry
 
-    lax.fori_loop(0, rounds_of(tile), one_round, 0)
-    turned = total[...].T
-    out_ref[:, :size] = dot32(turned[:, :size], inverse_ref[:size, :size])
-    out_ref[:, size:] = dot32(turned, inverse_ref[:, size:])
-
-
-def far(counts, offsets, near_first, near_second, blocks, turned_near, inverse):
-    tiles, slots = offsets.shape
+    lax.fori_loop(0, last, step, 0)
+    for t in range(tiles):
+        store(t).wait()
+
+
+def far(info, blocks, near, parts):
+    tiles = info.shape[0]
+    slots = info.shape[1] // 3
     size = blocks.shape[1]
-    whole = lambda *shape: pl.BlockSpec(shape, lambda t, *_: (0,) * len(shape))
+    rounds = tiles * slots // GROUP
+    hbm = pl.BlockSpec(memory_space=pltpu.HBM)
     return pl.pallas_call(
-        far_kernel,
+        functools.partial(far_kernel, slots),
         out_shape=jax.ShapeDtypeStruct((tiles * size, 2 * size), jnp.float32),
-        grid_spec=pltpu.PrefetchScalarGridSpec(
-            num_scalar_prefetch=4,
-            grid=(tiles,),
-            in_specs=[
-                pl.BlockSpec(memory_space=pl.ANY),
-                whole(*turned_near.shape),
-                whole(*inverse.shape),
-            ],
-            out_specs=pl.BlockSpec((size, 2 * size), lambda t, *_: (t, 0)),
-            scratch_shapes=[
-                pltpu.VMEM((tiles, slots * size, size), jnp.bfloat16),
-                pltpu.VMEM((2 * size, size), jnp.float32),
-                pltpu.SemaphoreType.DMA((tiles, slots)),
-            ],
-        ),
-        compiler_params=pltpu.CompilerParams(
-            dimension_semantics=("arbitrary",), vmem_limit_bytes=40 << 20
-        ),
+        in_specs=[pl.BlockSpec(memory_space=pltpu.SMEM), hbm, hbm, hbm],
+        out_specs=hbm,
+        scratch_shapes=[
+            pltpu.VMEM((rounds, GROUP, size, size), jnp.bfloat16),
+            pltpu.VMEM(near.shape, jnp.bfloat16),
+            pltpu.VMEM(parts.shape, jnp.bfloat16),
+            pltpu.VMEM((tiles, size, 2 * size), jnp.float32),
+            pltpu.SemaphoreType.DMA((rounds,)),
+            pltpu.SemaphoreType.DMA((2,)),
+            pltpu.SemaphoreType.DMA((tiles,)),
+        ],
+        compiler_params=pltpu.CompilerParams(vmem_limit_bytes=63 << 20),
         name="far",
-    )(counts, offsets, near_first, near_second, blocks, turned_near, inverse)
+    )(info, blocks, near, parts)
 
 
 def local_pairs(near_first, near_second, counts, near_total):
@@ -226,16 +267,23 @@
     response_cache, near_cache, lead_diag, far_offsets, near_first, near_second, tile_counts
 ):
     near_total = near_cache.shape[0]
-    share = response_cache.shape[0] // lax.axis_size("row")
-    own = lax.dynamic_slice_in_dim(response_cache, lax.axis_index("row") * share, share, 0)
-    blocks = lax.all_gather(own, ("col", "row"), axis=0, tiled=True)
+    cached, size = response_cache.shape[:2]
+    share = cached * size // lax.axis_size("row")
+    own = lax.dynamic_slice_in_dim(
+        response_cache.reshape(cached * size, size), lax.axis_index("row") * share, share, 0
+    )
+    blocks = lax.all_gather(own, ("col", "row"), axis=0, tiled=True).reshape(-1, size, size)
     pairs = total_pairs(local_pairs(near_first, near_second, tile_counts, near_total))
     turned = jnp.transpose(near_cache, (0, 2, 1))
-    padded = jnp.concatenate([turned, jnp.zeros_like(turned[:1])], axis=0)
-    lead_factor, inverse = lead(pairs, near_cache, turned, lead_diag)
-    far_factor = far(
-        tile_counts, far_offsets, near_first, near_second, blocks, padded, inverse
+    padded = jnp.concatenate([near_cache, jnp.zeros_like(near_cache[:1])], axis=0)
+    lead_factor, parts = lead(pairs, near_cache, turned, lead_diag)
+    usable = jnp.arange(far_offsets.shape[1], dtype=jnp.int32)[None, :] < tile_counts[:, None]
+    info = jnp.concatenate(
+        [far_offsets]
+        + [jnp.where(usable, labels, near_total) for labels in (near_first, near_second)],
+        axis=1,
     )
+    far_factor = far(info, blocks, padded, parts)
     return lead_factor, far_factor
 
 

time: 145 us -> 144 us (level)
  local copies, waits for them, and re-layouts: 8.85 us -> 5.91 us
  other arithmetic: 1.57 us -> 3.69 us
    unnamed x21 -> x7, local copies, waits for them, and re-layouts: 7.04 us -> 3.07 us
  transfers between devices with their start and end apart: 8 -> 8, of which waited for: 7 -> 7; matrix products, arithmetic and copies ran while one was open for 3% -> 4% of each run, Pallas kernels for 24% -> 24%
where the time goes in v4:
time: 144 us; the launch traced here: 143 us
  waiting for transfers between devices  57.8 us (40%)
  Pallas kernels  50.3 us (35%)
  between operations  14.1 us (10%)
  starting transfers between devices  11.5 us (8%)
  local copies, waits for them, and re-layouts  5.91 us (4%)
  other arithmetic  3.69 us (3%)
    all_gather x1, waiting for transfers between devices, shards(): lax.all_gather(own, ('col', 'row'), axis=0, tiled=True)  49.4 us
    pallas_call x1, Pallas kernels, lead(): pl.pallas_call(lead_kernel, out_shape=(jax.ShapeDtypeStruct((whole, whole...  34.6 us
    pallas_call x1, Pallas kernels, far(): pl.pallas_call(functools.partial(far_kernel, slots), out_shape=jax.ShapeD...  15.7 us
    ppermute x7, starting transfers between devices, total_pairs(): lax.ppermute(value, axis, [(i, i ^ bit) for i in range(size)])  11.5 us
    ppermute x7, waiting for transfers between devices, total_pairs(): lax.ppermute(value, axis, [(i, i ^ bit) for i in range(size)])  8.34 us
    unnamed x7, local copies, waits for them, and re-layouts  3.07 us
  transfers between devices with their start and end apart: 8, of which 7 were waited for; matrix products, arithmetic and copies ran while one was open for 4% of the time, Pallas kernels for 24%

profile of v4, /device:TPU:7, one launch (start us, length us, event | category | flops | bytes accessed | tf_op | source)
XLA Modules:
  0.0 143.2 jit_solution(7129364571166550845)
XLA Ops:
  7.2 0.0 copy-start
  7.2 0.0 all-gather.2.cloned.1.call-start
  7.2 1.8 %constant_dynamic-slice_fusion = bf16[512,256]{1,0:T(8,128)(2,1)} fusion(bf16[4096,256]{1,0:T(8,128)(2,1)} %bitcast.7, s32[]{:T(128)S(6)} %select_n.12), kind=kLoop, calls=%fused_computation.8 | loop fusion | bytes 524292 | tf_op jit(solution)/shard_map/dynamic_slice | solution.py:272
  9.0 0.0 all-gather.2.cloned.1.call-update
  9.0 0.7 iota_compare_fusion.2
  9.7 0.7 iota_compare_fusion
  10.4 0.1 convert_reduce_fusion
  10.5 0.8 collective-permute-start
  11.3 0.8 collective-permute-done
  12.1 1.1 collective-permute-start.1
  13.3 2.8 %collective-permute-done.1 = f32[8,8]{1,0:T(8,128)S(1)} collective-permute-done((f32[8,8]{1,0:T(8,128)S(1)}, f32[8,8]{1,0:T(8,128)S(1)}, u32[]{:S(2)}, u32[]{:S(2)}) %collective-permute-start.1) | collective-permute-done | bytes 288 | tf_op jit(solution)/shard_map/ppermute | solution.py:262
  16.1 0.5 collective-permute-start.2
  16.6 1.9 %collective-permute-done.2 = f32[8,8]{1,0:T(8,128)S(1)} collective-permute-done((f32[8,8]{1,0:T(8,128)S(1)}, f32[8,8]{1,0:T(8,128)S(1)}, u32[]{:S(2)}, u32[]{:S(2)}) %collective-permute-start.2) | collective-permute-done | bytes 288 | tf_op jit(solution)/shard_map/ppermute | solution.py:262
  18.6 2.9 %collective-permute-start.3 = (f32[8,8]{1,0:T(8,128)S(1)}, f32[8,8]{1,0:T(8,128)S(1)}, u32[]{:S(2)}, u32[]{:S(2)}) collective-permute-start(f32[8,8]{1,0:T(8,128)S(1)} %add.28), channel_id=1, source_target_pairs={{0,8},{1,9},{2,10},{3,11},{4,12},{5,13},{6,14},{7,15},{8,0},{9,1},... | collective-permute-start | bytes 776 | tf_op jit(solution)/shard_map/ppermute | solution.py:262
  21.5 1.0 collective-permute-done.3
  22.5 1.3 collective-permute-start.4
  23.8 1.5 %collective-permute-done.4 = f32[8,8]{1,0:T(8,128)S(1)} collective-permute-done((f32[8,8]{1,0:T(8,128)S(1)}, f32[8,8]{1,0:T(8,128)S(1)}, u32[]{:S(2)}, u32[]{:S(2)}) %collective-permute-start.4) | collective-permute-done | bytes 288 | tf_op jit(solution)/shard_map/ppermute | solution.py:262
  25.3 3.6 %collective-permute-start.5 = (f32[8,8]{1,0:T(8,128)S(1)}, f32[8,8]{1,0:T(8,128)S(1)}, u32[]{:S(2)}, u32[]{:S(2)}) collective-permute-start(f32[8,8]{1,0:T(8,128)S(1)} %add.30), channel_id=1, source_target_pairs={{0,2},{1,3},{2,0},{3,1},{4,6},{5,7},{6,4},{7,5},{8,10},{9,11},{10,... | collective-permute-start | bytes 776 | tf_op jit(solution)/shard_map/ppermute | solution.py:262
  28.9 0.8 broadcast_select_fusion.1
  29.7 0.3 collective-permute-done.5
  29.9 1.2 collective-permute-start.6
  31.2 1.3 pad_add_fusion.info_ref
  32.5 0.0 copy-start.2
  32.5 1.5 %copy.10 = bf16[8,256,256]{1,2,0:T(8,128)(2,1)S(1)} copy(bf16[8,256,256]{2,1,0:T(8,128)(2,1)} %near_ref.1) | data formatting | bytes 2097152 | tf_op args[1]
  34.0 0.0 copy-done
  34.0 1.1 concatenate.7.near_hbm
  35.1 0.0 collective-permute-done.6
  35.1 0.0 copy-done.2
  35.1 34.6 %lead.1 = (f32[512,512]{1,0:T(8,128)}, bf16[4608,256]{1,0:T(8,128)(2,1)S(1)}) custom-call(f32[8,8]{1,0:T(8,128)S(1)} %add.32.pairs_ref, bf16[8,256,256]{2,1,0:T(8,128)(2,1)S(1)} %copy-done, bf16[8,256,256]{2,1,0:T(8,128)(2,1)S(1)} %bitcast.4, f32[1,512]{1,0:T(1,128)S(1)} %bitcast.5), custom_call_target="tpu_custom_call" | custom-call | tf_op jit(solution)/shard_map/lead/pallas_call | solution.py:118
  69.7 0.0 copy-start.1
  69.7 1.6 %copy-done.1 = bf16[4608,256]{1,0:T(8,128)(2,1)} copy-done((bf16[4608,256]{1,0:T(8,128)(2,1)}, bf16[4608,256]{1,0:T(8,128)(2,1)S(1)}, u32[]{:S(2)}) %copy-start.1) | copy-done | bytes 2359320
  71.3 49.4 %all-gather.2.cloned.1.call-done = bf16[65536,256]{1,0:T(8,128)(2,1)} async-done(((bf16[512,256]{1,0:T(8,128)(2,1)}), bf16[65536,256]{1,0:T(8,128)(2,1)}) %all-gather.2.cloned.1.call-update) | async-done | bytes 33554448 | tf_op jit(solution)/shard_map/all_gather | solution.py:275
  120.7 15.7 %far.1 = f32[1024,512]{1,0:T(8,128)} custom-call(s32[4,72]{1,0:T(4,128)} %pad_add_fusion.info_ref, bf16[256,256,256]{2,1,0:T(8,128)(2,1)} %bitcast.6, bf16[9,256,256]{2,1,0:T(8,128)(2,1)} %concatenate.7.near_hbm, bf16[4608,256]{1,0:T(8,128)(2,1)} %copy-done.1), custom_call_target="tpu_custom_call" | custom-call | tf_op jit(solution)/shard_map/far/pallas_call | solution.py:229
  (7 shorter events, 0.0 us)
Async XLA Ops:
  7.2 26.8 %copy-start = (bf16[8,256,256]{2,1,0:T(8,128)(2,1)S(1)}, bf16[8,256,256]{2,1,0:T(8,128)(2,1)}, u32[]{:S(2)}) copy-start(bf16[8,256,256]{2,1,0:T(8,128)(2,1)} %near_ref.1) | copy-start | bytes 3145732
  7.2 113.5 %all-gather.2.cloned.1.call-start = ((), (), s32[]{:S(2)}) async-start(), calls=%async_computation | async-start | bytes 33816576 | tf_op jit(solution)/shard_map/all_gather | solution.py:275
  10.5 1.6 %collective-permute-start = (f32[8,8]{1,0:T(8,128)S(1)}, f32[8,8]{1,0:T(8,128)S(1)}, u32[]{:S(2)}, u32[]{:S(2)}) collective-permute-start(f32[8,8]{1,0:T(8,128)S(1)} %convert_reduce_fusion), channel_id=1, source_target_pairs={{0,16},{16,0},{32,48},{48,32},{64,80},{80,64},{96,112},{112,96},{1... | collective-permute-start | bytes 776 | tf_op jit(solution)/shard_map/ppermute | solution.py:262
  12.1 4.0 %collective-permute-start.1 = (f32[8,8]{1,0:T(8,128)S(1)}, f32[8,8]{1,0:T(8,128)S(1)}, u32[]{:S(2)}, u32[]{:S(2)}) collective-permute-start(f32[8,8]{1,0:T(8,128)S(1)} %add.26), channel_id=1, source_target_pairs={{0,64},{16,80},{32,96},{48,112},{64,0},{80,16},{96,32},{112,48},{1... | collective-permute-start | bytes 776 | tf_op jit(solution)/shard_map/ppermute | solution.py:262
  16.1 2.5 %collective-permute-start.2 = (f32[8,8]{1,0:T(8,128)S(1)}, f32[8,8]{1,0:T(8,128)S(1)}, u32[]{:S(2)}, u32[]{:S(2)}) collective-permute-start(f32[8,8]{1,0:T(8,128)S(1)} %add.27), channel_id=1, source_target_pairs={{0,32},{16,48},{32,0},{48,16},{64,96},{80,112},{96,64},{112,80},{1... | collective-permute-start | bytes 776 | tf_op jit(solution)/shard_map/ppermute | solution.py:262
  18.6 4.0 %collective-permute-start.3 = (f32[8,8]{1,0:T(8,128)S(1)}, f32[8,8]{1,0:T(8,128)S(1)}, u32[]{:S(2)}, u32[]{:S(2)}) collective-permute-start(f32[8,8]{1,0:T(8,128)S(1)} %add.28), channel_id=1, source_target_pairs={{0,8},{1,9},{2,10},{3,11},{4,12},{5,13},{6,14},{7,15},{8,0},{9,1},... | collective-permute-start | bytes 776 | tf_op jit(solution)/shard_map/ppermute | solution.py:262
  22.5 2.8 %collective-permute-start.4 = (f32[8,8]{1,0:T(8,128)S(1)}, f32[8,8]{1,0:T(8,128)S(1)}, u32[]{:S(2)}, u32[]{:S(2)}) collective-permute-start(f32[8,8]{1,0:T(8,128)S(1)} %add.29), channel_id=1, source_target_pairs={{0,4},{1,5},{2,6},{3,7},{4,0},{5,1},{6,2},{7,3},{8,12},{9,13},{10,... | collective-permute-start | bytes 776 | tf_op jit(solution)/shard_map/ppermute | solution.py:262
  25.3 4.7 %collective-permute-start.5 = (f32[8,8]{1,0:T(8,128)S(1)}, f32[8,8]{1,0:T(8,128)S(1)}, u32[]{:S(2)}, u32[]{:S(2)}) collective-permute-start(f32[8,8]{1,0:T(8,128)S(1)} %add.30), channel_id=1, source_target_pairs={{0,2},{1,3},{2,0},{3,1},{4,6},{5,7},{6,4},{7,5},{8,10},{9,11},{10,... | collective-permute-start | bytes 776 | tf_op jit(solution)/shard_map/ppermute | solution.py:262
  29.9 5.2 %collective-permute-start.6 = (f32[8,8]{1,0:T(8,128)S(1)}, f32[8,8]{1,0:T(8,128)S(1)}, u32[]{:S(2)}, u32[]{:S(2)}) collective-permute-start(f32[8,8]{1,0:T(8,128)S(1)} %add.31), channel_id=1, source_target_pairs={{0,1},{1,0},{2,3},{3,2},{4,5},{5,4},{6,7},{7,6},{8,9},{9,8},{10,11... | collective-permute-start | bytes 776 | tf_op jit(solution)/shard_map/ppermute | solution.py:262
  32.5 2.6 %copy-start.2 = (f32[512]{0:T(512)S(1)}, f32[512]{0:T(512)}, u32[]{:S(2)}) copy-start(f32[512]{0:T(512)} %param.9) | copy-start | bytes 6148
  69.7 1.6 %copy-start.1 = (bf16[4608,256]{1,0:T(8,128)(2,1)}, bf16[4608,256]{1,0:T(8,128)(2,1)S(1)}, u32[]{:S(2)}) copy-start(bf16[4608,256]{1,0:T(8,128)(2,1)S(1)} %get-tuple-element.5.parts_hbm) | copy-start | bytes 7077892
Sparse Core Ops, SparseCore 0:
  11.6 109.0 all-gather.1

commit v5 on v4

--- a/solution.py
+++ b/solution.py
@@ -9,8 +9,7 @@
 
 HIGHEST = lax.Precision.HIGHEST
 BLOCK = 128
-GROUP = 12
-AHEAD = 2
+GROUP = 4
 
 
 def dot32(left, right):
@@ -107,9 +106,12 @@
     lax.fori_loop(0, whole // BLOCK, step, 0)
     factor_ref[...] = upper[...].T
     high, middle, low = split3(work[:, whole:].T)
-    for n, part in enumerate((high, middle, high, low, middle, high)):
-        parts_ref[n * size : (n + 1) * size, :] = part[:size, :size]
-        parts_ref[(6 + 2 * n) * size : (8 + 2 * n) * size, :] = part[:, size:]
+    for n, part in enumerate((high, middle, low)):
+        for half in range(2):
+            for columns in range(2):
+                parts_ref[n, half, columns] = part[
+                    half * size : (half + 1) * size, columns * size : (columns + 1) * size
+                ]
 
 
 def lead(pairs, near_cache, turned_near, lead_diag):
@@ -119,7 +121,7 @@
         lead_kernel,
         out_shape=(
             jax.ShapeDtypeStruct((whole, whole), jnp.float32),
-            jax.ShapeDtypeStruct((9 * whole, whole // 2), jnp.bfloat16),
+            jax.ShapeDtypeStruct((3, 2, 2, whole // 2, whole // 2), jnp.bfloat16),
         ),
         in_specs=[pl.BlockSpec(memory_space=pltpu.SMEM), vmem, vmem, vmem],
         out_specs=(vmem, vmem),
@@ -133,116 +135,129 @@
 
 
 def far_kernel(
-    slots, info_ref, blocks_ref, near_hbm, parts_hbm, out_hbm, held, near_ref, parts_ref, out_ref,
-    arrived, loaded, stored,
+    slots, sums, info_ref, blocks_ref, turned_hbm, parts_hbm, out_hbm, held, turned_ref, parts_ref,
+    out_ref, arrived, loaded, stored,
 ):
     tiles = info_ref.shape[0]
-    size = near_ref.shape[1]
-    rounds = slots // GROUP
-    last = tiles * rounds
-
-    def begin(k):
-        t, r = k // rounds, k % rounds
+    size = turned_ref.shape[1]
+
+    def rounds_of(t):
+        return (info_ref[t, 3 * slots] + GROUP - 1) // GROUP
+
+    def begin(t, r):
         for i in range(GROUP):
+            s = r * GROUP + i
             pltpu.make_async_copy(
-                blocks_ref.at[info_ref[t, r * GROUP + i]], held.at[k, i], arrived.at[k]
+                blocks_ref.at[info_ref[t, s]], held.at[t, s], arrived.at[t, r]
             ).start()
 
-    def finish(k):
-        pltpu.make_async_copy(blocks_ref.at[pl.ds(0, GROUP)], held.at[k], arrived.at[k]).wait()
+    def begin_rounds(t, first, past):
+        def begin_round(r, carry):
+            begin(t, r)
+            return carry
+
+        lax.fori_loop(first, past, begin_round, 0)
+
+    def finish(t, r):
+        pltpu.make_async_copy(
+            blocks_ref.at[pl.ds(0, GROUP)],
+            held.at[t, pl.ds(r * GROUP, GROUP)],
+            arrived.at[t, r],
+        ).wait()
 
     def store(t):
         rows = pl.ds(pl.multiple_of(t * size, size), size)
         return pltpu.make_async_copy(out_ref.at[t], out_hbm.at[rows, :], stored.at[t])
 
-    load_near = pltpu.make_async_copy(near_hbm, near_ref, loaded.at[0])
-    load_parts = pltpu.make_async_copy(parts_hbm, parts_ref, loaded.at[1])
-    load_near.start()
-    for k in range(AHEAD):
-        begin(k)
-    load_parts.start()
-    load_near.wait()
-
-    def step(k, carry):
-        @pl.when(k + AHEAD < last)
-        def following():
-            begin(k + AHEAD)
-
-        t, r = k // rounds, k % rounds
-        finish(k)
-        rows = []
-        for i in range(GROUP):
-            s = r * GROUP + i
-            rows.append(
-                jnp.concatenate(
-                    [near_ref[info_ref[t, slots + s]], near_ref[info_ref[t, 2 * slots + s]]],
-                    axis=1,
-                )
+    def multiply(total, unit, terms):
+        for n, (left, right) in enumerate(terms):
+            pltpu.matmul_push_rhs(right, n % 2, unit)
+            pltpu.matmul_acc_lhs(total, left, n % 2)
+
+    def main(first_sum, second_sum):
+        load_turned = pltpu.make_async_copy(turned_hbm, turned_ref, loaded.at[0])
+        load_parts = pltpu.make_async_copy(parts_hbm, parts_ref, loaded.at[1])
+        load_turned.start()
+        begin_rounds(0, 0, rounds_of(0))
+        load_parts.start()
+        pltpu.matmul_pop(first_sum)
+        pltpu.matmul_pop(second_sum)
+        load_turned.wait()
+
+        def tile_step(t, carry):
+            rounds = rounds_of(t)
+            following = jnp.minimum(t + 1, tiles - 1)
+            next_rounds = jnp.where(t + 1 < tiles, rounds_of(following), 0)
+
+            def one_round(r, carry):
+                @pl.when(r < next_rounds)
+                def fetch():
+                    begin(following, r)
+
+                finish(t, r)
+                for i in range(GROUP):
+                    s = r * GROUP + i
+                    block = held[t, s]
+                    pltpu.matmul_push_rhs(block, i % 2, 0)
+                    pltpu.matmul_push_rhs(block, i % 2, 1)
+                    pltpu.matmul_acc_lhs(first_sum, turned_ref[info_ref[t, slots + s]], i % 2)
+                    pltpu.matmul_acc_lhs(second_sum, turned_ref[info_ref[t, 2 * slots + s]], i % 2)
+                return carry
+
+            lax.fori_loop(0, rounds, one_round, 0)
+            begin_rounds(following, rounds, jnp.maximum(rounds, next_rounds))
+
+            @pl.when(t == 0)
+            def factors():
+                load_parts.wait()
+
+            rows = (
+                split3(pltpu.matmul_pop(first_sum).T),
+                split3(pltpu.matmul_pop(second_sum).T),
             )
-        change = lax.dot_general(
-            held[k].reshape(GROUP * size, size),
-            jnp.concatenate(rows, axis=0),
-            (((0,), (0,)), ((), ())),
-            preferred_element_type=jnp.float32,
-        )
-
-        @pl.when(r == 0)
-        def first():
-            out_ref[t] = change
-
-        @pl.when(r > 0)
-        def later():
-            out_ref[t] += change
-
-        @pl.when(k == 0)
-        def factors():
-            load_parts.wait()
-
-        @pl.when(r == rounds - 1)
-        def solve():
-            high, middle, low = split3(out_ref[t])
-            wide = jnp.concatenate([high, high, middle, high, middle, low], axis=1)
-            narrow = jnp.concatenate(
-                [p[:, :size] for p in (high, high, middle, high, middle, low)], axis=1
-            )
-            out_ref[t, :, :size] = jnp.dot(
-                narrow, parts_ref[: 6 * size, :], preferred_element_type=jnp.float32
-            )
-            out_ref[t, :, size:] = jnp.dot(
-                wide, parts_ref[6 * size :, :], preferred_element_type=jnp.float32
-            )
+            products = ((0, 0), (0, 1), (1, 0), (0, 2), (1, 1), (2, 0))
+
+            def terms(half, columns, chosen):
+                return [(rows[half][i], parts_ref[j, half, columns]) for i, j in chosen]
+
+            multiply(first_sum, 0, terms(0, 0, products))
+            multiply(second_sum, 1, terms(0, 1, products) + terms(1, 1, products[3:]))
+            out_ref[t, :, :size] = pltpu.matmul_pop(first_sum)
+            multiply(first_sum, 0, terms(1, 1, products[:3]))
+            out_ref[t, :, size:] = pltpu.matmul_pop(second_sum) + pltpu.matmul_pop(first_sum)
             store(t).start()
-
-        return carry
-
-    lax.fori_loop(0, last, step, 0)
-    for t in range(tiles):
-        store(t).wait()
-
-
-def far(info, blocks, near, parts):
+            return carry
+
+        lax.fori_loop(0, tiles, tile_step, 0)
+        for t in range(tiles):
+            store(t).wait()
+
+    pl.run_scoped(main, *sums)
+
+
+def far(info, blocks, turned_near, parts):
     tiles = info.shape[0]
     slots = info.shape[1] // 3
     size = blocks.shape[1]
-    rounds = tiles * slots // GROUP
     hbm = pl.BlockSpec(memory_space=pltpu.HBM)
+    sums = [pltpu.ACC(mxu_id=n)((size, size), jnp.float32) for n in range(2)]
     return pl.pallas_call(
-        functools.partial(far_kernel, slots),
+        functools.partial(far_kernel, slots, sums),
         out_shape=jax.ShapeDtypeStruct((tiles * size, 2 * size), jnp.float32),
         in_specs=[pl.BlockSpec(memory_space=pltpu.SMEM), hbm, hbm, hbm],
         out_specs=hbm,
         scratch_shapes=[
-            pltpu.VMEM((rounds, GROUP, size, size), jnp.bfloat16),
-            pltpu.VMEM(near.shape, jnp.bfloat16),
+            pltpu.VMEM((tiles, slots, size, size), jnp.bfloat16),
+            pltpu.VMEM(turned_near.shape, jnp.bfloat16),
             pltpu.VMEM(parts.shape, jnp.bfloat16),
             pltpu.VMEM((tiles, size, 2 * size), jnp.float32),
-            pltpu.SemaphoreType.DMA((rounds,)),
+            pltpu.SemaphoreType.DMA((tiles, slots // GROUP)),
             pltpu.SemaphoreType.DMA((2,)),
             pltpu.SemaphoreType.DMA((tiles,)),
         ],
         compiler_params=pltpu.CompilerParams(vmem_limit_bytes=63 << 20),
         name="far",
-    )(info, blocks, near, parts)
+    )(info, blocks, turned_near, parts)
 
 
 def local_pairs(near_first, near_second, counts, near_total):
@@ -275,12 +290,13 @@
     blocks = lax.all_gather(own, ("col", "row"), axis=0, tiled=True).reshape(-1, size, size)
     pairs = total_pairs(local_pairs(near_first, near_second, tile_counts, near_total))
     turned = jnp.transpose(near_cache, (0, 2, 1))
-    padded = jnp.concatenate([near_cache, jnp.zeros_like(near_cache[:1])], axis=0)
+    padded = jnp.concatenate([turned, jnp.zeros_like(turned[:1])], axis=0)
     lead_factor, parts = lead(pairs, near_cache, turned, lead_diag)
     usable = jnp.arange(far_offsets.shape[1], dtype=jnp.int32)[None, :] < tile_counts[:, None]
     info = jnp.concatenate(
         [far_offsets]
-        + [jnp.where(usable, labels, near_total) for labels in (near_first, near_second)],
+        + [jnp.where(usable, labels, near_total) for labels in (near_first, near_second)]
+        + [tile_counts[:, None]],
         axis=1,
     )
     far_factor = far(info, blocks, padded, parts)

time: 144 us -> 142 us (0.986)
  Pallas kernels: 50.3 us -> 48.3 us
    pallas_call x1, Pallas kernels: 15.7 us -> 13.7 us  [far(): pl.pallas_call(functools.partial(far_kernel, slots, sums), out_shape=jax....]
    all_gather x1, waiting for transfers between devices: 49.4 us -> 51.1 us  [shards(): lax.all_gather(own, ('col', 'row'), axis=0, tiled=True)]
    ppermute x7, waiting for transfers between devices: 8.34 us -> 6.62 us  [total_pairs(): lax.ppermute(value, axis, [(i, i ^ bit) for i in range(size)])]
  transfers between devices with their start and end apart: 8 -> 8, of which waited for: 7 -> 5; matrix products, arithmetic and copies ran while one was open for 4% -> 5% of each run, Pallas kernels for 24% -> 25%
where the time goes in v5:
time: 142 us; the launch traced here: 141 us
  waiting for transfers between devices  57.8 us (41%)
  Pallas kernels  48.3 us (34%)
  between operations  14.1 us (10%)
  starting transfers between devices  11.3 us (8%)
  local copies, waits for them, and re-layouts  6.11 us (4%)
  other arithmetic  3.68 us (3%)
    all_gather x1, waiting for transfers between devices, shards(): lax.all_gather(own, ('col', 'row'), axis=0, tiled=True)  51.1 us
    pallas_call x1, Pallas kernels, lead(): pl.pallas_call(lead_kernel, out_shape=(jax.ShapeDtypeStruct((whole, whole...  34.6 us
    pallas_call x1, Pallas kernels, far(): pl.pallas_call(functools.partial(far_kernel, slots, sums), out_shape=jax....  13.7 us
    ppermute x7, starting transfers between devices, total_pairs(): lax.ppermute(value, axis, [(i, i ^ bit) for i in range(size)])  11.3 us
    ppermute x7, waiting for transfers between devices, total_pairs(): lax.ppermute(value, axis, [(i, i ^ bit) for i in range(size)])  6.62 us
  transfers between devices with their start and end apart: 8, of which 5 were waited for; matrix products, arithmetic and copies ran while one was open for 5% of the time, Pallas kernels for 25%

profile of v5, /device:TPU:7, one launch (start us, length us, event | category | flops | bytes accessed | tf_op | source)
XLA Modules:
  0.0 141.2 jit_solution(7889519959680979310)
XLA Ops:
  7.2 0.0 all-gather.2.cloned.1.call-start
  7.2 1.7 %constant_dynamic-slice_fusion = bf16[512,256]{1,0:T(8,128)(2,1)} fusion(bf16[4096,256]{1,0:T(8,128)(2,1)} %bitcast.9, s32[]{:T(128)S(6)} %select_n.12), kind=kLoop, calls=%fused_computation.8 | loop fusion | bytes 524292 | tf_op jit(solution)/shard_map/dynamic_slice | solution.py:287
  8.9 0.0 all-gather.2.cloned.1.call-update
  8.9 0.7 iota_compare_fusion.2
  9.6 0.7 iota_compare_fusion
  10.4 0.1 convert_reduce_fusion
  10.5 0.8 collective-permute-start
  11.2 0.8 collective-permute-done
  12.0 1.1 collective-permute-start.1
  13.2 2.8 %collective-permute-done.1 = f32[8,8]{1,0:T(8,128)S(1)} collective-permute-done((f32[8,8]{1,0:T(8,128)S(1)}, f32[8,8]{1,0:T(8,128)S(1)}, u32[]{:S(2)}, u32[]{:S(2)}) %collective-permute-start.1) | collective-permute-done | bytes 288 | tf_op jit(solution)/shard_map/ppermute | solution.py:277
  16.0 0.5 collective-permute-start.2
  16.6 1.9 %collective-permute-done.2 = f32[8,8]{1,0:T(8,128)S(1)} collective-permute-done((f32[8,8]{1,0:T(8,128)S(1)}, f32[8,8]{1,0:T(8,128)S(1)}, u32[]{:S(2)}, u32[]{:S(2)}) %collective-permute-start.2) | collective-permute-done | bytes 288 | tf_op jit(solution)/shard_map/ppermute | solution.py:277
  18.5 2.9 %collective-permute-start.3 = (f32[8,8]{1,0:T(8,128)S(1)}, f32[8,8]{1,0:T(8,128)S(1)}, u32[]{:S(2)}, u32[]{:S(2)}) collective-permute-start(f32[8,8]{1,0:T(8,128)S(1)} %add.28), channel_id=1, source_target_pairs={{0,8},{1,9},{2,10},{3,11},{4,12},{5,13},{6,14},{7,15},{8,0},{9,1},... | collective-permute-start | bytes 776 | tf_op jit(solution)/shard_map/ppermute | solution.py:277
  21.4 1.0 collective-permute-done.3
  22.4 1.3 collective-permute-start.4
  23.7 0.8 broadcast_select_fusion.1
  24.5 0.7 copy.12
  25.3 0.0 collective-permute-done.4
  25.3 3.7 %collective-permute-start.5 = (f32[8,8]{1,0:T(8,128)S(1)}, f32[8,8]{1,0:T(8,128)S(1)}, u32[]{:S(2)}, u32[]{:S(2)}) collective-permute-start(f32[8,8]{1,0:T(8,128)S(1)} %add.30), channel_id=1, source_target_pairs={{0,2},{1,3},{2,0},{3,1},{4,6},{5,7},{6,4},{7,5},{8,10},{9,11},{10,... | collective-permute-start | bytes 776 | tf_op jit(solution)/shard_map/ppermute | solution.py:277
  28.9 1.3 pad_add_fusion.info_ref
  30.3 0.0 collective-permute-done.5
  30.3 0.0 copy-start
  30.3 0.0 copy-start.2
  30.3 0.9 collective-permute-start.6
  31.2 1.5 %copy.11 = bf16[8,256,256]{1,2,0:T(8,128)(2,1)S(1)} copy(bf16[8,256,256]{2,1,0:T(8,128)(2,1)} %near_ref.1) | data formatting | bytes 2097152 | tf_op args[1]
  32.7 1.1 concatenate.7.turned_hbm
  33.8 0.0 collective-permute-done.6
  33.8 0.0 copy-done
  33.8 0.0 copy-done.2
  33.8 34.6 %lead.1 = (f32[512,512]{1,0:T(8,128)}, bf16[3,2,2,256,256]{4,3,2,1,0:T(8,128)(2,1)S(1)}) custom-call(f32[8,8]{1,0:T(8,128)S(1)} %add.32.pairs_ref, bf16[8,256,256]{2,1,0:T(8,128)(2,1)S(1)} %copy-done, bf16[8,256,256]{2,1,0:T(8,128)(2,1)S(1)} %bitcast.6, f32[1,512]{1,0:T(1,128)S(1)} %bitcast.7), custom_call_target="tpu_custom_call" | custom-call | tf_op jit(solution)/shard_map/lead/pallas_call | solution.py:120
  68.4 0.0 copy-start.1
  68.4 1.1 copy-done.1
  69.6 51.1 %all-gather.2.cloned.1.call-done = bf16[65536,256]{1,0:T(8,128)(2,1)} async-done(((bf16[512,256]{1,0:T(8,128)(2,1)}), bf16[65536,256]{1,0:T(8,128)(2,1)}) %all-gather.2.cloned.1.call-update) | async-done | bytes 33554448 | tf_op jit(solution)/shard_map/all_gather | solution.py:290
  120.7 13.7 %far.1 = f32[1024,512]{1,0:T(8,128)} custom-call(s32[4,73]{1,0:T(4,128)} %pad_add_fusion.info_ref, bf16[256,256,256]{2,1,0:T(8,128)(2,1)} %bitcast.8, bf16[9,256,256]{2,1,0:T(8,128)(2,1)} %concatenate.7.turned_hbm, bf16[3,2,2,256,256]{4,3,2,1,0:T(8,128)(2,1)} %copy-done.1), custom_call_target="tpu_custom_call" | custom-call | tf_op jit(solution)/shard_map/far/pallas_call | solution.py:244
  (7 shorter events, 0.0 us)
Async XLA Ops:
  7.2 113.5 %all-gather.2.cloned.1.call-start = ((), (), s32[]{:S(2)}) async-start(), calls=%async_computation | async-start | bytes 33816576 | tf_op jit(solution)/shard_map/all_gather | solution.py:290
  10.5 1.6 %collective-permute-start = (f32[8,8]{1,0:T(8,128)S(1)}, f32[8,8]{1,0:T(8,128)S(1)}, u32[]{:S(2)}, u32[]{:S(2)}) collective-permute-start(f32[8,8]{1,0:T(8,128)S(1)} %convert_reduce_fusion), channel_id=1, source_target_pairs={{0,16},{16,0},{32,48},{48,32},{64,80},{80,64},{96,112},{112,96},{1... | collective-permute-start | bytes 776 | tf_op jit(solution)/shard_map/ppermute | solution.py:277
  12.0 4.0 %collective-permute-start.1 = (f32[8,8]{1,0:T(8,128)S(1)}, f32[8,8]{1,0:T(8,128)S(1)}, u32[]{:S(2)}, u32[]{:S(2)}) collective-permute-start(f32[8,8]{1,0:T(8,128)S(1)} %add.26), channel_id=1, source_target_pairs={{0,64},{16,80},{32,96},{48,112},{64,0},{80,16},{96,32},{112,48},{1... | collective-permute-start | bytes 776 | tf_op jit(solution)/shard_map/ppermute | solution.py:277
  16.0 2.5 %collective-permute-start.2 = (f32[8,8]{1,0:T(8,128)S(1)}, f32[8,8]{1,0:T(8,128)S(1)}, u32[]{:S(2)}, u32[]{:S(2)}) collective-permute-start(f32[8,8]{1,0:T(8,128)S(1)} %add.27), channel_id=1, source_target_pairs={{0,32},{16,48},{32,0},{48,16},{64,96},{80,112},{96,64},{112,80},{1... | collective-permute-start | bytes 776 | tf_op jit(solution)/shard_map/ppermute | solution.py:277
  18.5 4.0 %collective-permute-start.3 = (f32[8,8]{1,0:T(8,128)S(1)}, f32[8,8]{1,0:T(8,128)S(1)}, u32[]{:S(2)}, u32[]{:S(2)}) collective-permute-start(f32[8,8]{1,0:T(8,128)S(1)} %add.28), channel_id=1, source_target_pairs={{0,8},{1,9},{2,10},{3,11},{4,12},{5,13},{6,14},{7,15},{8,0},{9,1},... | collective-permute-start | bytes 776 | tf_op jit(solution)/shard_map/ppermute | solution.py:277
  22.4 2.8 %collective-permute-start.4 = (f32[8,8]{1,0:T(8,128)S(1)}, f32[8,8]{1,0:T(8,128)S(1)}, u32[]{:S(2)}, u32[]{:S(2)}) collective-permute-start(f32[8,8]{1,0:T(8,128)S(1)} %add.29), channel_id=1, source_target_pairs={{0,4},{1,5},{2,6},{3,7},{4,0},{5,1},{6,2},{7,3},{8,12},{9,13},{10,... | collective-permute-start | bytes 776 | tf_op jit(solution)/shard_map/ppermute | solution.py:277
  25.3 5.0 %collective-permute-start.5 = (f32[8,8]{1,0:T(8,128)S(1)}, f32[8,8]{1,0:T(8,128)S(1)}, u32[]{:S(2)}, u32[]{:S(2)}) collective-permute-start(f32[8,8]{1,0:T(8,128)S(1)} %add.30), channel_id=1, source_target_pairs={{0,2},{1,3},{2,0},{3,1},{4,6},{5,7},{6,4},{7,5},{8,10},{9,11},{10,... | collective-permute-start | bytes 776 | tf_op jit(solution)/shard_map/ppermute | solution.py:277
  30.3 3.5 %copy-start = (bf16[8,256,256]{2,1,0:T(8,128)(2,1)S(1)}, bf16[8,256,256]{2,1,0:T(8,128)(2,1)}, u32[]{:S(2)}) copy-start(bf16[8,256,256]{2,1,0:T(8,128)(2,1)} %near_ref.1) | copy-start | bytes 3145732
  30.3 3.5 %copy-start.2 = (f32[512]{0:T(512)S(1)}, f32[512]{0:T(512)}, u32[]{:S(2)}) copy-start(f32[512]{0:T(512)} %param.9) | copy-start | bytes 6148
  30.3 3.5 %collective-permute-start.6 = (f32[8,8]{1,0:T(8,128)S(1)}, f32[8,8]{1,0:T(8,128)S(1)}, u32[]{:S(2)}, u32[]{:S(2)}) collective-permute-start(f32[8,8]{1,0:T(8,128)S(1)} %add.31), channel_id=1, source_target_pairs={{0,1},{1,0},{2,3},{3,2},{4,5},{5,4},{6,7},{7,6},{8,9},{9,8},{10,11... | collective-permute-start | bytes 776 | tf_op jit(solution)/shard_map/ppermute | solution.py:277
  68.4 1.1 copy-start.1
Sparse Core Ops, SparseCore 0:
  11.5 109.0 all-gather.1

commit v6 on v2

--- a/solution.py
+++ b/solution.py
@@ -18,6 +18,14 @@
 
 def dot32(left, right):
     return jnp.dot(left, right, precision=HIGHEST, preferred_element_type=jnp.float32)
+
+
+def split3(value):
+    high = value.astype(jnp.bfloat16)
+    rest = value - high.astype(jnp.float32)
+    middle = rest.astype(jnp.bfloat16)
+    low = (rest - middle.astype(jnp.float32)).astype(jnp.bfloat16)
+    return high, middle, low
 
 
 def spread_rows(value, row):
@@ -108,14 +116,17 @@
     factor_steps(work, upper, 0, size // BLOCK)
 
 
-def lead_end_kernel(work_ref, upper_ref, factor_ref, inverse_ref, work, upper):
+def lead_end_kernel(work_ref, upper_ref, factor_ref, parts_ref, work, upper):
     whole = upper.shape[0]
     half = whole // 2
     work[...] = work_ref[...]
     upper[:half, :] = upper_ref[:half, :]
     factor_steps(work, upper, half // BLOCK, whole // BLOCK)
     factor_ref[...] = upper[...].T
-    inverse_ref[...] = work[:, whole:].T
+    for n, part in enumerate(split3(work[:, whole:].T)):
+        for i in range(2):
+            for j in range(2):
+                parts_ref[n, i, j] = part[i * half : (i + 1) * half, j * half : (j + 1) * half]
 
 
 VMEM = pl.BlockSpec(memory_space=pltpu.VMEM)
@@ -144,7 +155,7 @@
     square = jax.ShapeDtypeStruct((whole, whole), jnp.float32)
     return pl.pallas_call(
         lead_end_kernel,
-        out_shape=(square, square),
+        out_shape=(square, jax.ShapeDtypeStruct((3, 2, 2, whole // 2, whole // 2), jnp.bfloat16)),
         in_specs=[VMEM, VMEM],
         out_specs=(VMEM, VMEM),
         scratch_shapes=[
@@ -276,96 +287,147 @@
 
 
 def far_kernel(
-    slots, info_ref, own_hbm, other_hbm, blocks_ref, turned_hbm, inverse_hbm, out_hbm, held, total,
-    other_ref, turned_ref, inverse_ref, out_ref, items, arrived, loaded, stored,
+    slots, sums, info_ref, own_hbm, other_hbm, blocks_ref, turned_hbm, parts_hbm, out_hbm, held,
+    own_ref, other_ref, turned_ref, parts_ref, out_ref, items, counts, arrived, loaded, stored,
 ):
     tiles = info_ref.shape[0]
     size = turned_ref.shape[1]
-    span = GROUP * size
-
-    def fetch(t, q, place):
-        return pltpu.make_async_copy(
-            blocks_ref.at[place],
-            held.at[t, pl.ds(pl.multiple_of(q * size, size), size), :],
-            arrived.at[t, q],
-        )
+    empty = turned_ref.shape[0] - 1
+
+    def rounds_of(t):
+        return (counts[t] + GROUP - 1) // GROUP
+
+    def begin(t, r):
+        for i in range(GROUP):
+            s = r * GROUP + i
+            place = jnp.where(s < counts[t], items[0, t, s], 0)
+            pltpu.make_async_copy(
+                blocks_ref.at[place], held.at[t, s], arrived.at[t, r]
+            ).start()
+
+    def begin_rounds(t, first, past):
+        def begin_round(r, carry):
+            begin(t, r)
+            return carry
+
+        lax.fori_loop(first, past, begin_round, 0)
+
+    def finish(t, r):
+        pltpu.make_async_copy(
+            blocks_ref.at[pl.ds(0, GROUP)],
+            held.at[t, pl.ds(r * GROUP, GROUP)],
+            arrived.at[t, r],
+        ).wait()
 
     def store(t):
-        return pltpu.make_async_copy(
-            out_ref.at[t], out_hbm.at[pl.ds(t * size, size), :], stored.at[t]
-        )
-
-    load_turned = pltpu.make_async_copy(turned_hbm, turned_ref, loaded.at[0])
-    load_own = pltpu.make_async_copy(own_hbm, total, loaded.at[1])
-    load_inverse = pltpu.make_async_copy(inverse_hbm, inverse_ref, loaded.at[2])
-    load_other = pltpu.make_async_copy(other_hbm, other_ref, loaded.at[3])
-    load_turned.start()
-    load_own.start()
-    counts = []
-    for t in range(tiles):
-        count = list_slots(t, info_ref, items, slots)
-        counts.append(count)
-
-        def begin(q, carry):
-            fetch(t, q, jnp.where(q < count, items[0, t, q], 0)).start()
+        rows = pl.ds(pl.multiple_of(t * size, size), size)
+        return pltpu.make_async_copy(out_ref.at[t], out_hbm.at[rows, :], stored.at[t])
+
+    def multiply(total, unit, terms):
+        for n, (left, right) in enumerate(terms):
+            pltpu.matmul_push_rhs(right, n % 2, unit)
+            pltpu.matmul_acc_lhs(total, left, n % 2)
+
+    def main(first_sum, second_sum):
+        load_turned = pltpu.make_async_copy(turned_hbm, turned_ref, loaded.at[0])
+        load_parts = pltpu.make_async_copy(parts_hbm, parts_ref, loaded.at[1])
+        load_own = pltpu.make_async_copy(own_hbm, own_ref, loaded.at[2])
+        load_other = pltpu.make_async_copy(other_hbm, other_ref, loaded.at[3])
+        load_turned.start()
+        for t in range(tiles):
+            counts[t] = list_slots(t, info_ref, items, slots)
+            if t == 0:
+                begin_rounds(0, 0, rounds_of(0))
+        load_parts.start()
+        load_own.start()
+        load_other.start()
+        pltpu.matmul_pop(first_sum)
+        pltpu.matmul_pop(second_sum)
+        load_turned.wait()
+
+        def tile_step(t, carry):
+            rounds = rounds_of(t)
+            following = jnp.minimum(t + 1, tiles - 1)
+            next_rounds = jnp.where(t + 1 < tiles, rounds_of(following), 0)
+
+            def one_round(r, carry):
+                @pl.when(r < next_rounds)
+                def fetch():
+                    begin(following, r)
+
+                finish(t, r)
+                for i in range(GROUP):
+                    s = r * GROUP + i
+                    used = s < counts[t]
+                    block = held[t, s]
+                    pltpu.matmul_push_rhs(block, i % 2, 0)
+                    pltpu.matmul_push_rhs(block, i % 2, 1)
+                    first = jnp.where(used, items[1, t, s], empty)
+                    second = jnp.where(used, items[2, t, s], empty)
+                    pltpu.matmul_acc_lhs(first_sum, turned_ref[first], i % 2)
+                    pltpu.matmul_acc_lhs(second_sum, turned_ref[second], i % 2)
+                return carry
+
+            lax.fori_loop(0, rounds, one_round, 0)
+            begin_rounds(following, rounds, jnp.maximum(rounds, next_rounds))
+
+            @pl.when(t == 0)
+            def factors():
+                load_parts.wait()
+                load_own.wait()
+                load_other.wait()
+
+            before = own_ref[t] + other_ref[t]
+            rows = (
+                split3((pltpu.matmul_pop(first_sum) + before[:size]).T),
+                split3((pltpu.matmul_pop(second_sum) + before[size:]).T),
+            )
+            products = ((0, 0), (0, 1), (1, 0), (0, 2), (1, 1), (2, 0))
+
+            def terms(half, columns, chosen):
+                return [(rows[half][i], parts_ref[j, half, columns]) for i, j in chosen]
+
+            multiply(first_sum, 0, terms(0, 0, products))
+            multiply(second_sum, 1, terms(0, 1, products) + terms(1, 1, products[3:]))
+            out_ref[t, :, :size] = pltpu.matmul_pop(first_sum)
+            multiply(first_sum, 0, terms(1, 1, products[:3]))
+            out_ref[t, :, size:] = pltpu.matmul_pop(second_sum) + pltpu.matmul_pop(first_sum)
+            store(t).start()
             return carry
 
-        lax.fori_loop(0, (count + GROUP - 1) // GROUP * GROUP, begin, 0)
-    load_other.start()
-    load_inverse.start()
-    load_turned.wait()
-    load_own.wait()
-    for t in range(tiles):
-
-        def one_round(r, carry):
-            for i in range(GROUP):
-                fetch(t, r * GROUP + i, 0).wait()
-            right = held[t, pl.ds(pl.multiple_of(r * span, span), span), :]
-            total[t] += jnp.dot(
-                left_rows(t, r, counts[t], items, turned_ref),
-                right,
-                preferred_element_type=jnp.float32,
-            )
-            return carry
-
-        lax.fori_loop(0, (counts[t] + GROUP - 1) // GROUP, one_round, 0)
-        if t == 0:
-            load_other.wait()
-            load_inverse.wait()
-        turned = (total[t] + other_ref[t]).T
-        out_ref[t, :, :size] = dot32(turned[:, :size], inverse_ref[:size, :size])
-        out_ref[t, :, size:] = dot32(turned, inverse_ref[:, size:])
-        store(t).start()
-    for t in range(tiles):
-        store(t).wait()
-
-
-HBM = pl.BlockSpec(memory_space=pltpu.HBM)
-
-
-def far(info, slots, sums, other_sums, blocks, turned_near, inverse):
+        lax.fori_loop(0, tiles, tile_step, 0)
+        for t in range(tiles):
+            store(t).wait()
+
+    pl.run_scoped(main, *sums)
+
+
+def far(info, slots, own_sums, other_sums, blocks, turned_near, parts):
     tiles = info.shape[0]
     size = blocks.shape[1]
+    hbm = pl.BlockSpec(memory_space=pltpu.HBM)
+    sums = [pltpu.ACC(mxu_id=n)((size, size), jnp.float32) for n in range(2)]
     return pl.pallas_call(
-        functools.partial(far_kernel, slots),
+        functools.partial(far_kernel, slots, sums),
         out_shape=jax.ShapeDtypeStruct((tiles * size, 2 * size), jnp.float32),
-        in_specs=[pl.BlockSpec(memory_space=pltpu.SMEM)] + [HBM] * 5,
-        out_specs=HBM,
+        in_specs=[pl.BlockSpec(memory_space=pltpu.SMEM)] + [hbm] * 5,
+        out_specs=hbm,
         scratch_shapes=[
-            pltpu.VMEM((tiles, slots * size, size), jnp.bfloat16),
-            pltpu.VMEM(sums.shape, jnp.float32),
-            pltpu.VMEM(sums.shape, jnp.float32),
+            pltpu.VMEM((tiles, slots, size, size), jnp.bfloat16),
+            pltpu.VMEM(own_sums.shape, jnp.float32),
+            pltpu.VMEM(own_sums.shape, jnp.float32),
             pltpu.VMEM(turned_near.shape, jnp.bfloat16),
-            pltpu.VMEM(inverse.shape, jnp.float32),
+            pltpu.VMEM(parts.shape, jnp.bfloat16),
             pltpu.VMEM((tiles, size, 2 * size), jnp.float32),
-            pltpu.SMEM((3, tiles, slots), jnp.int32),
-            pltpu.SemaphoreType.DMA((tiles, slots)),
+            pltpu.SMEM((3, tiles, slots + 1), jnp.int32),
+            pltpu.SMEM((tiles,), jnp.int32),
+            pltpu.SemaphoreType.DMA((tiles, slots // GROUP)),
             pltpu.SemaphoreType.DMA((4,)),
             pltpu.SemaphoreType.DMA((tiles,)),
         ],
         compiler_params=pltpu.CompilerParams(vmem_limit_bytes=63 << 20),
         name="far",
-    )(info, sums, other_sums, blocks, turned_near, inverse)
+    )(info, own_sums, other_sums, blocks, turned_near, parts)
 
 
 def local_pairs(near_first, near_second, counts, near_total):
@@ -431,7 +493,7 @@
             pairs = pairs + swap(pairs, axis, bit)
         return lax.optimization_barrier((pairs, to_z, to_y))
 
-    for stages in ((("row", 1),), (("row", 4),), (("row", 2),)):
+    for stages in ((("col", 8),), (("col", 4), ("col", 2)), (("col", 1),)):
         pairs, step_y, step_z = advance(
             pairs, ((line_y[-1], True), (line_z[-1], False)), stages
         )
@@ -440,25 +502,25 @@
     by_z = [jnp.concatenate(line_y, axis=0)]
     by_y = [jnp.concatenate(line_z, axis=0)]
     pairs, step_z, step_y = advance(
-        pairs, ((by_z[-1], False), (by_y[-1], True)), (("col", 8), ("col", 4), ("col", 2))
+        pairs, ((by_z[-1], False), (by_y[-1], True)), (("row", 1), ("row", 4), ("row", 2))
     )
     by_z.append(step_z)
     by_y.append(step_y)
+    step_z, step_y = hop(by_z[-1], False), hop(by_y[-1], True)
     info_other = swap(info_other, "row", 1)
-    pairs = pairs + swap(pairs, "col", 1)
-    step_z, step_y = hop(by_z[-1], False), hop(by_y[-1], True)
+    pairs, info_other = lax.optimization_barrier((pairs, info_other))
     work, upper = lead_start(pairs, near_cache, turned, lead_diag)
     work, step_z, step_y = lax.optimization_barrier((work, step_z, step_y))
     by_z.append(step_z)
     by_y.append(step_y)
     step_z, step_y = hop(by_z[-1], False), hop(by_y[-1], True)
-    lead_factor, inverse = lead_end(work, upper)
-    inverse, step_z, step_y = lax.optimization_barrier((inverse, step_z, step_y))
+    lead_factor, parts = lead_end(work, upper)
+    parts, step_z, step_y = lax.optimization_barrier((parts, step_z, step_y))
     pieces = by_z + [step_z] + by_y + [step_y]
     sums_other = ring_sums(info_other, slots, padded, pieces)
     moved = swap(sums_other, "row", 1)
     sums = ring_sums(info_own, slots, padded, pieces)
-    far_factor = far(info, slots, sums, moved, blocks, padded, inverse)
+    far_factor = far(info, slots, sums, moved, blocks, padded, parts)
     return lead_factor, far_factor
 
 

time: 187 us -> 166 us (0.89)
  waiting for transfers between devices: 46.2 us -> 31.4 us
  starting transfers between devices: 47.9 us -> 41.8 us
    ppermute x9, waiting for transfers between devices: 44.9 us -> 21.8 us  [swap(): lax.ppermute(value, axis, [(i, i ^ bit) for i in range(lax.axis_size(axis...]
    ppermute x12, waiting for transfers between devices: 1.24 us -> 9.53 us  [hop(): return lax.ppermute(value, ('row', 'col'), moves)]
    ppermute x9, starting transfers between devices: 29.5 us -> 26.4 us  [swap(): lax.ppermute(value, axis, [(i, i ^ bit) for i in range(lax.axis_size(axis...]
    ppermute x12, starting transfers between devices: 18.4 us -> 15.4 us  [hop(): return lax.ppermute(value, ('row', 'col'), moves)]
  transfers between devices with their start and end apart: 22 -> 22, of which waited for: 10 -> 11; matrix products, arithmetic and copies ran while one was open for 3% -> 3% of each run, Pallas kernels for 29% -> 33%
where the time goes in v6:
time: 166 us; the launch traced here: 163 us
  Pallas kernels  66.5 us (40%)
  starting transfers between devices  41.8 us (25%)
  waiting for transfers between devices  31.4 us (19%)
  between operations  14.3 us (9%)
  local copies, waits for them, and re-layouts  6.78 us (4%)
  other arithmetic  2.57 us (2%)
    ppermute x9, starting transfers between devices, swap(): lax.ppermute(value, axis, [(i, i ^ bit) for i in range(lax.axis_size(axis...  26.4 us
    ppermute x9, waiting for transfers between devices, swap(): lax.ppermute(value, axis, [(i, i ^ bit) for i in range(lax.axis_size(axis...  21.8 us
    pallas_call x2, Pallas kernels, ring_sums(): pl.pallas_call(functools.partial(ring_kernel, slots), out_shape=jax.Shape...  19.7 us
    pallas_call x1, Pallas kernels, lead_start(): pl.pallas_call(lead_start_kernel, out_shape=(jax.ShapeDtypeStruct((whole,...  18.2 us
    pallas_call x1, Pallas kernels, lead_end(): pl.pallas_call(lead_end_kernel, out_shape=(square, jax.ShapeDtypeStruct((...  16.6 us
    ppermute x12, starting transfers between devices, hop(): return lax.ppermute(value, ('row', 'col'), moves)  15.4 us
    pallas_call x1, Pallas kernels, far(): pl.pallas_call(functools.partial(far_kernel, slots, sums), out_shape=jax....  12 us
    ppermute x12, waiting for transfers between devices, hop(): return lax.ppermute(value, ('row', 'col'), moves)  9.53 us
  transfers between devices with their start and end apart: 22, of which 11 were waited for; matrix products, arithmetic and copies ran while one was open for 3% of the time, Pallas kernels for 33%

profile of v6, /device:TPU:7, one launch (start us, length us, event | category | flops | bytes accessed | tf_op | source)
XLA Modules:
  0.0 163.3 jit_solution(5060182059339076479)
XLA Ops:
  7.2 0.0 all-gather.2.cloned.1.call-start
  7.2 1.6 constant_dynamic-slice_fusion
  8.8 0.0 all-gather.2.cloned.1.call-update
  8.8 1.1 constant_dynamic-slice_fusion.1
  9.9 2.8 %collective-permute-start.1 = (bf16[2,256,256]{2,1,0:T(8,128)(2,1)S(1)}, bf16[2,256,256]{2,1,0:T(8,128)(2,1)S(1)}, u32[]{:S(2)}, u32[]{:S(2)}) collective-permute-start(bf16[2,256,256]{2,1,0:T(8,128)(2,1)S(1)} %get-tuple-element.51), channel_id=1, source_target_pairs={{0,4},{1,5},{2,6},{3,7},{4,8},{5,9},{6,10},{7,11},{8,12},{9,13},{1... | collective-permute-start | bytes 786440 | tf_op jit(solution)/shard_map/ppermute | solution.py:452
  12.7 3.8 %collective-permute-start.2 = (bf16[2,256,256]{2,1,0:T(8,128)(2,1)S(1)}, bf16[2,256,256]{2,1,0:T(8,128)(2,1)S(1)}, u32[]{:S(2)}, u32[]{:S(2)}) collective-permute-start(bf16[2,256,256]{2,1,0:T(8,128)(2,1)S(1)} %get-tuple-element.50), channel_id=1, source_target_pairs={{0,1},{1,2},{2,3},{3,0},{4,5},{5,6},{6,7},{7,4},{8,9},{9,10},{10,1... | collective-permute-start | bytes 786440 | tf_op jit(solution)/shard_map/ppermute | solution.py:452
  16.5 0.7 iota_compare_fusion.2
  17.2 0.7 iota_compare_fusion
  17.9 0.1 convert_reduce_fusion
  18.0 0.4 collective-permute-start
  18.5 3.6 %collective-permute-done = f32[8,8]{1,0:T(8,128)S(1)} collective-permute-done((f32[8,8]{1,0:T(8,128)S(1)}, f32[8,8]{1,0:T(8,128)S(1)}, u32[]{:S(2)}, u32[]{:S(2)}) %collective-permute-start) | collective-permute-done | bytes 288 | tf_op jit(solution)/shard_map/ppermute | solution.py:456
  22.1 0.0 collective-permute-done.1
  22.1 0.0 collective-permute-done.2
  22.1 0.5 collective-permute-start.5
  22.6 1.1 collective-permute-start.6
  23.7 0.7 collective-permute-start.3
  24.4 3.9 %collective-permute-done.3 = f32[8,8]{1,0:T(8,128)S(1)} collective-permute-done((f32[8,8]{1,0:T(8,128)S(1)}, f32[8,8]{1,0:T(8,128)S(1)}, u32[]{:S(2)}, u32[]{:S(2)}) %collective-permute-start.3) | collective-permute-done | bytes 288 | tf_op jit(solution)/shard_map/ppermute | solution.py:456
  28.3 0.0 collective-permute-start.4
  28.3 4.0 %collective-permute-done.4 = f32[8,8]{1,0:T(8,128)S(1)} collective-permute-done((f32[8,8]{1,0:T(8,128)S(1)}, f32[8,8]{1,0:T(8,128)S(1)}, u32[]{:S(2)}, u32[]{:S(2)}) %collective-permute-start.4) | collective-permute-done | bytes 288 | tf_op jit(solution)/shard_map/ppermute | solution.py:456
  32.3 0.0 collective-permute-done.5
  32.3 0.0 collective-permute-done.6
  32.3 0.1 collective-permute-start.8
  32.4 0.3 collective-permute-start.9
  32.7 1.2 collective-permute-start.7
  33.9 4.3 %collective-permute-done.7 = f32[8,8]{1,0:T(8,128)S(1)} collective-permute-done((f32[8,8]{1,0:T(8,128)S(1)}, f32[8,8]{1,0:T(8,128)S(1)}, u32[]{:S(2)}, u32[]{:S(2)}) %collective-permute-start.7) | collective-permute-done | bytes 288 | tf_op jit(solution)/shard_map/ppermute | solution.py:456
  38.3 0.0 copy-start.8
  38.3 0.0 copy-start.1
  38.3 0.0 collective-permute-done.8
  38.3 0.0 collective-permute-done.9
  38.3 0.1 pad_maximum_fusion.refs_0_
  38.5 0.0 copy-start.2
  38.5 1.6 collective-permute-start.13
  40.1 0.1 pad_maximum_fusion.1.refs_4_
  40.2 0.3 collective-permute-start.14
  40.6 3.2 %collective-permute-start.10 = (f32[8,8]{1,0:T(8,128)S(1)}, f32[8,8]{1,0:T(8,128)S(1)}, u32[]{:S(2)}, u32[]{:S(2)}) collective-permute-start(f32[8,8]{1,0:T(8,128)S(1)} %add.117), channel_id=1, source_target_pairs={{0,16},{16,0},{32,48},{48,32},{64,80},{80,64},{96,112},{112,96},{1... | collective-permute-start | bytes 776 | tf_op jit(solution)/shard_map/ppermute | solution.py:456
  43.8 0.8 collective-permute-done.10
  44.6 1.1 collective-permute-start.11
  45.7 2.9 %collective-permute-done.11 = f32[8,8]{1,0:T(8,128)S(1)} collective-permute-done((f32[8,8]{1,0:T(8,128)S(1)}, f32[8,8]{1,0:T(8,128)S(1)}, u32[]{:S(2)}, u32[]{:S(2)}) %collective-permute-start.11) | collective-permute-done | bytes 288 | tf_op jit(solution)/shard_map/ppermute | solution.py:456
  48.6 0.9 collective-permute-start.12
  49.5 2.0 %collective-permute-done.12 = f32[8,8]{1,0:T(8,128)S(1)} collective-permute-done((f32[8,8]{1,0:T(8,128)S(1)}, f32[8,8]{1,0:T(8,128)S(1)}, u32[]{:S(2)}, u32[]{:S(2)}) %collective-permute-start.12) | collective-permute-done | bytes 288 | tf_op jit(solution)/shard_map/ppermute | solution.py:456
  51.5 6.6 %collective-permute-done.13.refs_1_ = bf16[8,256,256]{2,1,0:T(8,128)(2,1)} collective-permute-done((bf16[8,256,256]{2,1,0:T(8,128)(2,1)S(1)}, bf16[8,256,256]{2,1,0:T(8,128)(2,1)}, u32[]{:S(2)}, u32[]{:S(2)}) %collective-permute-start.13) | collective-permute-done | bytes 1048608 | tf_op jit(solution)/shard_map/ppermute | solution.py:452
  58.1 1.9 %collective-permute-done.14.refs_5_ = bf16[8,256,256]{2,1,0:T(8,128)(2,1)} collective-permute-done((bf16[8,256,256]{2,1,0:T(8,128)(2,1)S(1)}, bf16[8,256,256]{2,1,0:T(8,128)(2,1)}, u32[]{:S(2)}, u32[]{:S(2)}) %collective-permute-start.14) | collective-permute-done | bytes 1048608 | tf_op jit(solution)/shard_map/ppermute | solution.py:452
  60.0 0.7 collective-permute-start.16
  60.7 0.8 collective-permute-start.17
  61.5 0.1 select_select_fusion
  61.6 0.7 add_add_fusion.2
  62.2 5.0 %collective-permute-start.15 = (s32[4,72]{1,0:T(4,128)S(1)}, s32[4,72]{1,0:T(4,128)S(1)}, u32[]{:S(2)}, u32[]{:S(2)}) collective-permute-start(s32[4,72]{1,0:T(4,128)S(1)} %get-tuple-element.54), channel_id=1, source_target_pairs={{0,16},{16,0},{32,48},{48,32},{64,80},{80,64},{96,112},{112,96},{1... | collective-permute-start | bytes 3464 | tf_op jit(solution)/shard_map/ppermute | solution.py:456
  67.3 0.5 copy.11
  67.8 0.3 collective-permute-done.15.info_ref
  68.1 18.2 %lead_start.1 = (f32[512,1024]{1,0:T(8,128)S(1)}, f32[512,512]{1,0:T(8,128)S(1)}) custom-call(f32[8,8]{1,0:T(8,128)S(1)} %add.120.pairs_ref, bf16[8,256,256]{2,1,0:T(8,128)(2,1)S(1)} %copy-done.1, bf16[8,256,256]{2,1,0:T(8,128)(2,1)S(1)} %bitcast.2, f32[1,512]{1,0:T(1,128)S(1)} %bitcast.4), custom_call_target="tpu_custom_call" | custom-call | flops 8999999488 | bytes 6291456 | tf_op jit(solution)/shard_map/lead_start/pallas_call | solution.py:137
  86.3 1.0 collective-permute-done.17.refs_6_
  87.3 0.8 collective-permute-start.18
  88.1 2.7 %collective-permute-start.19 = (bf16[8,256,256]{2,1,0:T(8,128)(2,1)}, bf16[8,256,256]{2,1,0:T(8,128)(2,1)S(1)}, u32[]{:S(2)}, u32[]{:S(2)}) collective-permute-start(bf16[8,256,256]{2,1,0:T(8,128)(2,1)} %collective-permute-done.17.refs_6_), channel_id=1, source_target_pairs={{0,4},{1,5},{2,6},{3,7},{4,8},{5,9},{6,10},{7,11},{8,12},{9,13},{1... | collective-permute-start | bytes 3145736 | tf_op jit(solution)/shard_map/ppermute | solution.py:452
  90.8 1.1 concatenate.23.turned_ref.turned_hbm
  91.9 16.6 %lead_end.1 = (f32[512,512]{1,0:T(8,128)}, bf16[3,2,2,256,256]{4,3,2,1,0:T(8,128)(2,1)S(1)}) custom-call(f32[512,1024]{1,0:T(8,128)S(1)} %get-tuple-element.40.work_ref, f32[512,512]{1,0:T(8,128)S(1)} %get-tuple-element.41.upper_ref), custom_call_target="tpu_custom_call" | custom-call | flops 8999999488 | bytes 6291456 | tf_op jit(solution)/shard_map/lead_end/pallas_call | solution.py:156
  108.5 1.2 copy-done
  109.7 0.9 copy-done.5
  110.6 0.3 copy-done.6
  110.9 9.6 %ring_sums.3 = f32[4,512,256]{2,1,0:T(8,128)} custom-call(s32[4,72]{1,0:T(4,128)} %copy-done.9, bf16[9,256,256]{2,1,0:T(8,128)(2,1)} %concatenate.23.turned_ref.turned_hbm, bf16[8,256,256]{2,1,0:T(8,128)(2,1)} %copy-done.3, bf16[8,256,256]{2,1,0:T(8,128)(2,1)} %collective-permute-done.13.refs_1_, bf16[8,256,256]{2,1,0:T(8,128)(2,1)} %collective-permute-done.16.refs_2_, ...), custom_call_target="tpu_custom_call" | custom-call | flops 3000000000 | bytes 12582912 | tf_op jit(solution)/shard_map/ring_sums/pallas_call | solution.py:264
  120.6 13.7 %collective-permute-start.20 = (f32[4,512,256]{2,1,0:T(8,128)}, f32[4,512,256]{2,1,0:T(8,128)}, u32[]{:S(2)}, u32[]{:S(2)}) collective-permute-start(f32[4,512,256]{2,1,0:T(8,128)} %ring_sums.3), channel_id=1, source_target_pairs={{0,16},{16,0},{32,48},{48,32},{64,80},{80,64},{96,112},{112,96},{1... | collective-permute-start | bytes 6291464 | tf_op jit(solution)/shard_map/ppermute | solution.py:456
  134.3 10.1 %ring_sums.2.own_hbm = f32[4,512,256]{2,1,0:T(8,128)} custom-call(s32[4,72]{1,0:T(4,128)} %get-tuple-element.52.info_ref, bf16[9,256,256]{2,1,0:T(8,128)(2,1)} %concatenate.23.turned_ref.turned_hbm, bf16[8,256,256]{2,1,0:T(8,128)(2,1)} %copy-done.3, bf16[8,256,256]{2,1,0:T(8,128)(2,1)} %collective-permute-done.13.refs_1_, ...), custom_call_target="tpu_custom_call" | custom-call | flops 3000000000 | bytes 12582912 | tf_op jit(solution)/shard_map/ring_sums/pallas_call | solution.py:264
  144.4 0.0 collective-permute-done.20.other_hbm
  144.4 0.0 all-gather.2.cloned.1.call-done.blocks_ref
  144.5 12.0 %far.1 = f32[1024,512]{1,0:T(8,128)} custom-call(s32[4,72]{1,0:T(4,128)} %get-tuple-element.53.info_ref, f32[4,512,256]{2,1,0:T(8,128)} %ring_sums.2.own_hbm, f32[4,512,256]{2,1,0:T(8,128)} %collective-permute-done.20.other_hbm, bf16[128,256,256]{2,1,0:T(8,128)(2,1)} %all-gather.2.cloned.1.call-done.blocks_ref, ...), custom_call_target="tpu_custom_call" | custom-call | tf_op jit(solution)/shard_map/far/pallas_call | solution.py:410
  (28 shorter events, 0.1 us)
Async XLA Ops:
  7.2 137.3 %all-gather.2.cloned.1.call-start = ((), (), s32[]{:S(2)}) async-start(), calls=%async_computation | async-start | bytes 16908288 | tf_op jit(solution)/shard_map/all_gather | solution.py:472
  9.9 12.2 %collective-permute-start.1 = (bf16[2,256,256]{2,1,0:T(8,128)(2,1)S(1)}, bf16[2,256,256]{2,1,0:T(8,128)(2,1)S(1)}, u32[]{:S(2)}, u32[]{:S(2)}) collective-permute-start(bf16[2,256,256]{2,1,0:T(8,128)(2,1)S(1)} %get-tuple-element.51), channel_id=1, source_target_pairs={{0,4},{1,5},{2,6},{3,7},{4,8},{5,9},{6,10},{7,11},{8,12},{9,13},{1... | collective-permute-start | bytes 786440 | tf_op jit(solution)/shard_map/ppermute | solution.py:452
  12.7 9.4 %collective-permute-start.2 = (bf16[2,256,256]{2,1,0:T(8,128)(2,1)S(1)}, bf16[2,256,256]{2,1,0:T(8,128)(2,1)S(1)}, u32[]{:S(2)}, u32[]{:S(2)}) collective-permute-start(bf16[2,256,256]{2,1,0:T(8,128)(2,1)S(1)} %get-tuple-element.50), channel_id=1, source_target_pairs={{0,1},{1,2},{2,3},{3,0},{4,5},{5,6},{6,7},{7,4},{8,9},{9,10},{10,1... | collective-permute-start | bytes 786440 | tf_op jit(solution)/shard_map/ppermute | solution.py:452
  18.0 4.0 %collective-permute-start = (f32[8,8]{1,0:T(8,128)S(1)}, f32[8,8]{1,0:T(8,128)S(1)}, u32[]{:S(2)}, u32[]{:S(2)}) collective-permute-start(f32[8,8]{1,0:T(8,128)S(1)} %convert_reduce_fusion), channel_id=1, source_target_pairs={{0,8},{1,9},{2,10},{3,11},{4,12},{5,13},{6,14},{7,15},{8,0},{9,1},... | collective-permute-start | bytes 776 | tf_op jit(solution)/shard_map/ppermute | solution.py:456
  22.1 10.2 %collective-permute-start.5 = (bf16[2,256,256]{2,1,0:T(8,128)(2,1)S(1)}, bf16[2,256,256]{2,1,0:T(8,128)(2,1)S(1)}, u32[]{:S(2)}, u32[]{:S(2)}) collective-permute-start(bf16[2,256,256]{2,1,0:T(8,128)(2,1)S(1)} %collective-permute-done.1), channel_id=1, source_target_pairs={{0,4},{1,5},{2,6},{3,7},{4,8},{5,9},{6,10},{7,11},{8,12},{9,13},{1... | collective-permute-start | bytes 786440 | tf_op jit(solution)/shard_map/ppermute | solution.py:452
  22.6 9.7 %collective-permute-start.6 = (bf16[2,256,256]{2,1,0:T(8,128)(2,1)S(1)}, bf16[2,256,256]{2,1,0:T(8,128)(2,1)S(1)}, u32[]{:S(2)}, u32[]{:S(2)}) collective-permute-start(bf16[2,256,256]{2,1,0:T(8,128)(2,1)S(1)} %collective-permute-done.2), channel_id=1, source_target_pairs={{0,1},{1,2},{2,3},{3,0},{4,5},{5,6},{6,7},{7,4},{8,9},{9,10},{10,1... | collective-permute-start | bytes 786440 | tf_op jit(solution)/shard_map/ppermute | solution.py:452
  23.7 4.7 %collective-permute-start.3 = (f32[8,8]{1,0:T(8,128)S(1)}, f32[8,8]{1,0:T(8,128)S(1)}, u32[]{:S(2)}, u32[]{:S(2)}) collective-permute-start(f32[8,8]{1,0:T(8,128)S(1)} %add.110), channel_id=1, source_target_pairs={{0,4},{1,5},{2,6},{3,7},{4,0},{5,1},{6,2},{7,3},{8,12},{9,13},{10,... | collective-permute-start | bytes 776 | tf_op jit(solution)/shard_map/ppermute | solution.py:456
  28.3 4.0 %collective-permute-start.4 = (f32[8,8]{1,0:T(8,128)S(1)}, f32[8,8]{1,0:T(8,128)S(1)}, u32[]{:S(2)}, u32[]{:S(2)}) collective-permute-start(f32[8,8]{1,0:T(8,128)S(1)} %add.115), channel_id=1, source_target_pairs={{0,2},{1,3},{2,0},{3,1},{4,6},{5,7},{6,4},{7,5},{8,10},{9,11},{10,... | collective-permute-start | bytes 776 | tf_op jit(solution)/shard_map/ppermute | solution.py:456
  32.3 6.0 %collective-permute-start.8 = (bf16[2,256,256]{2,1,0:T(8,128)(2,1)S(1)}, bf16[2,256,256]{2,1,0:T(8,128)(2,1)S(1)}, u32[]{:S(2)}, u32[]{:S(2)}) collective-permute-start(bf16[2,256,256]{2,1,0:T(8,128)(2,1)S(1)} %collective-permute-done.5), channel_id=1, source_target_pairs={{0,4},{1,5},{2,6},{3,7},{4,8},{5,9},{6,10},{7,11},{8,12},{9,13},{1... | collective-permute-start | bytes 786440 | tf_op jit(solution)/shard_map/ppermute | solution.py:452
  32.4 5.9 %collective-permute-start.9 = (bf16[2,256,256]{2,1,0:T(8,128)(2,1)S(1)}, bf16[2,256,256]{2,1,0:T(8,128)(2,1)S(1)}, u32[]{:S(2)}, u32[]{:S(2)}) collective-permute-start(bf16[2,256,256]{2,1,0:T(8,128)(2,1)S(1)} %collective-permute-done.6), channel_id=1, source_target_pairs={{0,1},{1,2},{2,3},{3,0},{4,5},{5,6},{6,7},{7,4},{8,9},{9,10},{10,1... | collective-permute-start | bytes 786440 | tf_op jit(solution)/shard_map/ppermute | solution.py:452
  32.7 5.5 %collective-permute-start.7 = (f32[8,8]{1,0:T(8,128)S(1)}, f32[8,8]{1,0:T(8,128)S(1)}, u32[]{:S(2)}, u32[]{:S(2)}) collective-permute-start(f32[8,8]{1,0:T(8,128)S(1)} %add.116), channel_id=1, source_target_pairs={{0,1},{1,0},{2,3},{3,2},{4,5},{5,4},{6,7},{7,6},{8,9},{9,8},{10,11... | collective-permute-start | bytes 776 | tf_op jit(solution)/shard_map/ppermute | solution.py:456
  38.3 23.2 %copy-start.10 = (s32[4,24]{1,0:T(4,128)S(1)}, s32[4,24]{1,0:T(4,128)}, u32[]{:S(2)}) copy-start(s32[4,24]{1,0:T(4,128)} %param.10) | copy-start | bytes 1156
  38.3 23.2 %copy-start.11 = (s32[4]{0:T(128)S(1)}, s32[4]{0:T(128)}, u32[]{:S(2)}) copy-start(s32[4]{0:T(128)} %param.13) | copy-start | bytes 52
  38.3 23.3 %copy-start.7 = (s32[4,24]{1,0:T(4,128)S(1)}, s32[4,24]{1,0:T(4,128)}, u32[]{:S(2)}) copy-start(s32[4,24]{1,0:T(4,128)} %param.12) | copy-start | bytes 1156
  38.3 23.3 %copy-start.8 = (s32[4,24]{1,0:T(4,128)S(1)}, s32[4,24]{1,0:T(4,128)}, u32[]{:S(2)}) copy-start(s32[4,24]{1,0:T(4,128)} %param.11) | copy-start | bytes 1156
  38.3 29.0 %copy-start.1 = (bf16[8,256,256]{2,1,0:T(8,128)(2,1)S(1)}, bf16[8,256,256]{2,1,0:T(8,128)(2,1)}, u32[]{:S(2)}) copy-start(bf16[8,256,256]{2,1,0:T(8,128)(2,1)} %near_ref.1) | copy-start | bytes 3145732
  38.5 29.4 %copy-start.3 = (bf16[8,256,256]{2,1,0:T(8,128)(2,1)}, bf16[8,256,256]{2,1,0:T(8,128)(2,1)S(1)}, u32[]{:S(2)}) copy-start(bf16[8,256,256]{2,1,0:T(8,128)(2,1)S(1)} %pad_maximum_fusion.refs_0_) | copy-start | bytes 3145732
  38.5 29.6 %copy-start.2 = (f32[512]{0:T(512)S(1)}, f32[512]{0:T(512)}, u32[]{:S(2)}) copy-start(f32[512]{0:T(512)} %param.9) | copy-start | bytes 6148
  38.5 19.6 %collective-permute-start.13 = (bf16[8,256,256]{2,1,0:T(8,128)(2,1)S(1)}, bf16[8,256,256]{2,1,0:T(8,128)(2,1)}, u32[]{:S(2)}, u32[]{:S(2)}) collective-permute-start(bf16[8,256,256]{2,1,0:T(8,128)(2,1)S(1)} %pad_maximum_fusion.refs_0_), channel_id=1, source_target_pairs={{0,1},{1,2},{2,3},{3,0},{4,5},{5,6},{6,7},{7,4},{8,9},{9,10},{10,1... | collective-permute-start | bytes 3145736 | tf_op jit(solution)/shard_map/ppermute | solution.py:452
  40.2 22.0 %copy-start.4 = (bf16[8,256,256]{2,1,0:T(8,128)(2,1)}, bf16[8,256,256]{2,1,0:T(8,128)(2,1)S(1)}, u32[]{:S(2)}) copy-start(bf16[8,256,256]{2,1,0:T(8,128)(2,1)S(1)} %pad_maximum_fusion.1.refs_4_) | copy-start | bytes 3145732
  40.2 19.8 %collective-permute-start.14 = (bf16[8,256,256]{2,1,0:T(8,128)(2,1)S(1)}, bf16[8,256,256]{2,1,0:T(8,128)(2,1)}, u32[]{:S(2)}, u32[]{:S(2)}) collective-permute-start(bf16[8,256,256]{2,1,0:T(8,128)(2,1)S(1)} %pad_maximum_fusion.1.refs_4_), channel_id=1, source_target_pairs={{0,4},{1,5},{2,6},{3,7},{4,8},{5,9},{6,10},{7,11},{8,12},{9,13},{1... | collective-permute-start | bytes 3145736 | tf_op jit(solution)/shard_map/ppermute | solution.py:452
  40.6 4.0 %collective-permute-start.10 = (f32[8,8]{1,0:T(8,128)S(1)}, f32[8,8]{1,0:T(8,128)S(1)}, u32[]{:S(2)}, u32[]{:S(2)}) collective-permute-start(f32[8,8]{1,0:T(8,128)S(1)} %add.117), channel_id=1, source_target_pairs={{0,16},{16,0},{32,48},{48,32},{64,80},{80,64},{96,112},{112,96},{1... | collective-permute-start | bytes 776 | tf_op jit(solution)/shard_map/ppermute | solution.py:456
  44.6 4.0 %collective-permute-start.11 = (f32[8,8]{1,0:T(8,128)S(1)}, f32[8,8]{1,0:T(8,128)S(1)}, u32[]{:S(2)}, u32[]{:S(2)}) collective-permute-start(f32[8,8]{1,0:T(8,128)S(1)} %add.118), channel_id=1, source_target_pairs={{0,64},{16,80},{32,96},{48,112},{64,0},{80,16},{96,32},{112,48},{1... | collective-permute-start | bytes 776 | tf_op jit(solution)/shard_map/ppermute | solution.py:456
  48.6 2.9 %collective-permute-start.12 = (f32[8,8]{1,0:T(8,128)S(1)}, f32[8,8]{1,0:T(8,128)S(1)}, u32[]{:S(2)}, u32[]{:S(2)}) collective-permute-start(f32[8,8]{1,0:T(8,128)S(1)} %add.119), channel_id=1, source_target_pairs={{0,32},{16,48},{32,0},{48,16},{64,96},{80,112},{96,64},{112,80},{1... | collective-permute-start | bytes 776 | tf_op jit(solution)/shard_map/ppermute | solution.py:456
  60.0 26.3 %collective-permute-start.16 = (bf16[8,256,256]{2,1,0:T(8,128)(2,1)}, bf16[8,256,256]{2,1,0:T(8,128)(2,1)}, u32[]{:S(2)}, u32[]{:S(2)}) collective-permute-start(bf16[8,256,256]{2,1,0:T(8,128)(2,1)} %collective-permute-done.13.refs_1_), channel_id=1, source_target_pairs={{0,1},{1,2},{2,3},{3,0},{4,5},{5,6},{6,7},{7,4},{8,9},{9,10},{10,1... | collective-permute-start | bytes 3145736 | tf_op jit(solution)/shard_map/ppermute | solution.py:452
  60.7 26.6 %collective-permute-start.17 = (bf16[8,256,256]{2,1,0:T(8,128)(2,1)}, bf16[8,256,256]{2,1,0:T(8,128)(2,1)}, u32[]{:S(2)}, u32[]{:S(2)}) collective-permute-start(bf16[8,256,256]{2,1,0:T(8,128)(2,1)} %collective-permute-done.14.refs_5_), channel_id=1, source_target_pairs={{0,4},{1,5},{2,6},{3,7},{4,8},{5,9},{6,10},{7,11},{8,12},{9,13},{1... | collective-permute-start | bytes 3145736 | tf_op jit(solution)/shard_map/ppermute | solution.py:452
  62.2 5.9 %collective-permute-start.15 = (s32[4,72]{1,0:T(4,128)S(1)}, s32[4,72]{1,0:T(4,128)S(1)}, u32[]{:S(2)}, u32[]{:S(2)}) collective-permute-start(s32[4,72]{1,0:T(4,128)S(1)} %get-tuple-element.54), channel_id=1, source_target_pairs={{0,16},{16,0},{32,48},{48,32},{64,80},{80,64},{96,112},{112,96},{1... | collective-permute-start | bytes 3464 | tf_op jit(solution)/shard_map/ppermute | solution.py:456
  68.1 18.2 %copy-start.9 = (s32[4,72]{1,0:T(4,128)}, s32[4,72]{1,0:T(4,128)S(1)}, u32[]{:S(2)}) copy-start(s32[4,72]{1,0:T(4,128)S(1)} %collective-permute-done.15.info_ref) | copy-start | bytes 3460
  87.3 22.3 %collective-permute-start.18 = (bf16[8,256,256]{2,1,0:T(8,128)(2,1)}, bf16[8,256,256]{2,1,0:T(8,128)(2,1)S(1)}, u32[]{:S(2)}, u32[]{:S(2)}) collective-permute-start(bf16[8,256,256]{2,1,0:T(8,128)(2,1)} %collective-permute-done.16.refs_2_), channel_id=1, source_target_pairs={{0,1},{1,2},{2,3},{3,0},{4,5},{5,6},{6,7},{7,4},{8,9},{9,10},{10,1... | collective-permute-start | bytes 3145736 | tf_op jit(solution)/shard_map/ppermute | solution.py:452
  88.1 21.6 %collective-permute-start.19 = (bf16[8,256,256]{2,1,0:T(8,128)(2,1)}, bf16[8,256,256]{2,1,0:T(8,128)(2,1)S(1)}, u32[]{:S(2)}, u32[]{:S(2)}) collective-permute-start(bf16[8,256,256]{2,1,0:T(8,128)(2,1)} %collective-permute-done.17.refs_6_), channel_id=1, source_target_pairs={{0,4},{1,5},{2,6},{3,7},{4,8},{5,9},{6,10},{7,11},{8,12},{9,13},{1... | collective-permute-start | bytes 3145736 | tf_op jit(solution)/shard_map/ppermute | solution.py:452
  108.5 1.2 copy-start
  109.6 1.0 copy-start.5
  109.6 1.3 copy-start.6
  120.6 23.8 %collective-permute-start.20 = (f32[4,512,256]{2,1,0:T(8,128)}, f32[4,512,256]{2,1,0:T(8,128)}, u32[]{:S(2)}, u32[]{:S(2)}) collective-permute-start(f32[4,512,256]{2,1,0:T(8,128)} %ring_sums.3), channel_id=1, source_target_pairs={{0,16},{16,0},{32,48},{48,32},{64,80},{80,64},{96,112},{112,96},{1... | collective-permute-start | bytes 6291464 | tf_op jit(solution)/shard_map/ppermute | solution.py:456
Sparse Core Ops, SparseCore 0:
  11.1 94.6 all-gather.1

commit v7 on v5

--- a/solution.py
+++ b/solution.py
@@ -282,20 +282,18 @@
     response_cache, near_cache, lead_diag, far_offsets, near_first, near_second, tile_counts
 ):
     near_total = near_cache.shape[0]
-    cached, size = response_cache.shape[:2]
-    share = cached * size // lax.axis_size("row")
-    own = lax.dynamic_slice_in_dim(
-        response_cache.reshape(cached * size, size), lax.axis_index("row") * share, share, 0
-    )
-    blocks = lax.all_gather(own, ("col", "row"), axis=0, tiled=True).reshape(-1, size, size)
-    pairs = total_pairs(local_pairs(near_first, near_second, tile_counts, near_total))
+    share = response_cache.shape[0] // lax.axis_size("row")
+    own = lax.dynamic_slice_in_dim(response_cache, lax.axis_index("row") * share, share, 0)
+    blocks = lax.all_gather(own, ("col", "row"), axis=0, tiled=True)
     turned = jnp.transpose(near_cache, (0, 2, 1))
     padded = jnp.concatenate([turned, jnp.zeros_like(turned[:1])], axis=0)
+    labels, turned, padded = lax.optimization_barrier((near_first, turned, padded))
+    pairs = total_pairs(local_pairs(labels, near_second, tile_counts, near_total))
     lead_factor, parts = lead(pairs, near_cache, turned, lead_diag)
     usable = jnp.arange(far_offsets.shape[1], dtype=jnp.int32)[None, :] < tile_counts[:, None]
     info = jnp.concatenate(
         [far_offsets]
-        + [jnp.where(usable, labels, near_total) for labels in (near_first, near_second)]
+        + [jnp.where(usable, chosen, near_total) for chosen in (near_first, near_second)]
         + [tile_counts[:, None]],
         axis=1,
     )

time: 142 us -> 142 us (level)
  waiting for transfers between devices: 57.8 us -> 61 us
  other arithmetic: 3.68 us -> 0.94 us
    ppermute x7, waiting for transfers between devices: 6.62 us -> 10.2 us  [total_pairs(): lax.ppermute(value, axis, [(i, i ^ bit) for i in range(size)])]
  transfers between devices with their start and end apart: 8 -> 8, of which waited for: 5 -> 8; matrix products, arithmetic and copies ran while one was open for 5% -> 3% of each run, Pallas kernels for 25% -> 25%
where the time goes in v7:
time: 142 us; the launch traced here: 141 us
  waiting for transfers between devices  61 us (43%)
  Pallas kernels  47.6 us (34%)
  between operations  14.1 us (10%)
  starting transfers between devices  11.3 us (8%)
  local copies, waits for them, and re-layouts  5.59 us (4%)
    all_gather x1, waiting for transfers between devices, shards(): blocks = lax.all_gather(own, ('col', 'row'), axis=0, tiled=True)  50.8 us
    pallas_call x1, Pallas kernels, lead(): pl.pallas_call(lead_kernel, out_shape=(jax.ShapeDtypeStruct((whole, whole...  34.6 us
    pallas_call x1, Pallas kernels, far(): pl.pallas_call(functools.partial(far_kernel, slots, sums), out_shape=jax....  13 us
    ppermute x7, starting transfers between devices, total_pairs(): lax.ppermute(value, axis, [(i, i ^ bit) for i in range(size)])  11.2 us
    ppermute x7, waiting for transfers between devices, total_pairs(): lax.ppermute(value, axis, [(i, i ^ bit) for i in range(size)])  10.2 us
  transfers between devices with their start and end apart: 8, of which 8 were waited for; matrix products, arithmetic and copies ran while one was open for 3% of the time, Pallas kernels for 25%

profile of v7, /device:TPU:7, one launch (start us, length us, event | category | flops | bytes accessed | tf_op | source)
XLA Modules:
  0.0 140.6 jit_solution(12034973672650697697)
XLA Ops:
  7.2 0.0 all-gather.2.cloned.1.call-start
  7.2 1.7 %constant_dynamic-slice_fusion = bf16[2,256,256]{2,1,0:T(8,128)(2,1)} fusion(bf16[16,256,256]{2,1,0:T(8,128)(2,1)} %param.7, s32[]{:T(128)S(6)} %select_n.12), kind=kLoop, calls=%fused_computation.8 | loop fusion | bytes 524292 | tf_op jit(solution)/shard_map/dynamic_slice | solution.py:286
  8.9 0.0 all-gather.2.cloned.1.call-update
  8.9 0.0 copy-start.6
  8.9 0.0 copy-start.3
  8.9 0.0 copy-start.4
  8.9 0.0 copy-start.5
  9.0 0.0 copy-start
  9.0 0.0 copy-start.2
  9.0 1.6 %copy.13 = bf16[8,256,256]{1,2,0:T(8,128)(2,1)S(1)} copy(bf16[8,256,256]{2,1,0:T(8,128)(2,1)} %near_ref.1) | data formatting | bytes 2097152 | tf_op args[1]
  10.6 1.1 concatenate.6.turned_hbm
  11.6 0.0 copy-done.6
  11.6 0.1 iota_compare_fusion.2
  11.7 0.0 copy-done.3
  11.7 0.0 copy-done.4
  11.7 0.1 convert_reduce_fusion
  11.8 0.8 collective-permute-start
  12.6 0.8 collective-permute-done
  13.4 1.1 collective-permute-start.1
  14.6 2.8 %collective-permute-done.1 = f32[8,8]{1,0:T(8,128)S(1)} collective-permute-done((f32[8,8]{1,0:T(8,128)S(1)}, f32[8,8]{1,0:T(8,128)S(1)}, u32[]{:S(2)}, u32[]{:S(2)}) %collective-permute-start.1) | collective-permute-done | bytes 288 | tf_op jit(solution)/shard_map/ppermute | solution.py:277
  17.4 0.5 collective-permute-start.2
  17.9 1.9 %collective-permute-done.2 = f32[8,8]{1,0:T(8,128)S(1)} collective-permute-done((f32[8,8]{1,0:T(8,128)S(1)}, f32[8,8]{1,0:T(8,128)S(1)}, u32[]{:S(2)}, u32[]{:S(2)}) %collective-permute-start.2) | collective-permute-done | bytes 288 | tf_op jit(solution)/shard_map/ppermute | solution.py:277
  19.9 2.9 %collective-permute-start.3 = (f32[8,8]{1,0:T(8,128)S(1)}, f32[8,8]{1,0:T(8,128)S(1)}, u32[]{:S(2)}, u32[]{:S(2)}) collective-permute-start(f32[8,8]{1,0:T(8,128)S(1)} %add.28), channel_id=1, source_target_pairs={{0,8},{1,9},{2,10},{3,11},{4,12},{5,13},{6,14},{7,15},{8,0},{9,1},... | collective-permute-start | bytes 776 | tf_op jit(solution)/shard_map/ppermute | solution.py:277
  22.8 1.0 collective-permute-done.3
  23.8 1.3 collective-permute-start.4
  25.1 1.6 %collective-permute-done.4 = f32[8,8]{1,0:T(8,128)S(1)} collective-permute-done((f32[8,8]{1,0:T(8,128)S(1)}, f32[8,8]{1,0:T(8,128)S(1)}, u32[]{:S(2)}, u32[]{:S(2)}) %collective-permute-start.4) | collective-permute-done | bytes 288 | tf_op jit(solution)/shard_map/ppermute | solution.py:277
  26.7 3.6 %collective-permute-start.5 = (f32[8,8]{1,0:T(8,128)S(1)}, f32[8,8]{1,0:T(8,128)S(1)}, u32[]{:S(2)}, u32[]{:S(2)}) collective-permute-start(f32[8,8]{1,0:T(8,128)S(1)} %add.30), channel_id=1, source_target_pairs={{0,2},{1,3},{2,0},{3,1},{4,6},{5,7},{6,4},{7,5},{8,10},{9,11},{10,... | collective-permute-start | bytes 776 | tf_op jit(solution)/shard_map/ppermute | solution.py:277
  30.3 0.1 broadcast_select_fusion.1
  30.4 0.1 copy.14
  30.4 0.8 collective-permute-done.5
  31.3 1.0 collective-permute-start.6
  32.3 0.0 copy-done.5
  32.3 0.7 pad_add_fusion.info_ref
  32.9 1.2 collective-permute-done.6
  34.1 0.0 copy-done
  34.1 0.0 copy-done.2
  34.2 34.6 %lead.1 = (f32[512,512]{1,0:T(8,128)}, bf16[3,2,2,256,256]{4,3,2,1,0:T(8,128)(2,1)S(1)}) custom-call(f32[8,8]{1,0:T(8,128)S(1)} %add.32.pairs_ref, bf16[8,256,256]{2,1,0:T(8,128)(2,1)S(1)} %copy-done, bf16[8,256,256]{2,1,0:T(8,128)(2,1)S(1)} %bitcast.4, f32[1,512]{1,0:T(1,128)S(1)} %bitcast.5), custom_call_target="tpu_custom_call" | custom-call | tf_op jit(solution)/shard_map/lead/pallas_call | solution.py:120
  68.7 0.0 copy-start.1
  68.8 1.1 copy-done.1
  69.9 50.8 %all-gather.2.cloned.1.call-done.blocks_ref = bf16[256,256,256]{2,1,0:T(8,128)(2,1)} async-done(((bf16[2,256,256]{2,1,0:T(8,128)(2,1)}), bf16[256,256,256]{2,1,0:T(8,128)(2,1)}) %all-gather.2.cloned.1.call-update) | async-done | bytes 33554448 | tf_op jit(solution)/shard_map/all_gather | solution.py:287
  120.7 13.0 %far.1 = f32[1024,512]{1,0:T(8,128)} custom-call(s32[4,73]{1,0:T(4,128)} %pad_add_fusion.info_ref, bf16[256,256,256]{2,1,0:T(8,128)(2,1)} %all-gather.2.cloned.1.call-done.blocks_ref, bf16[9,256,256]{2,1,0:T(8,128)(2,1)} %concatenate.6.turned_hbm, bf16[3,2,2,256,256]{4,3,2,1,0:T(8,128)(2,1)} %copy-done.1), custom_call_target="tpu_custom_call" | custom-call | tf_op jit(solution)/shard_map/far/pallas_call | solution.py:244
  (8 shorter events, 0.0 us)
Async XLA Ops:
  7.2 113.6 %all-gather.2.cloned.1.call-start = ((), (), s32[]{:S(2)}) async-start(), calls=%async_computation | async-start | bytes 33816576 | tf_op jit(solution)/shard_map/all_gather | solution.py:287
  8.9 2.7 %copy-start.6 = (s32[4]{0:T(128)S(1)}, s32[4]{0:T(128)}, u32[]{:S(2)}) copy-start(s32[4]{0:T(128)} %param.13) | copy-start | bytes 52
  8.9 2.8 %copy-start.3 = (s32[4,24]{1,0:T(4,128)S(1)}, s32[4,24]{1,0:T(4,128)}, u32[]{:S(2)}) copy-start(s32[4,24]{1,0:T(4,128)} %param.12) | copy-start | bytes 1156
  8.9 2.8 %copy-start.4 = (s32[4,24]{1,0:T(4,128)S(1)}, s32[4,24]{1,0:T(4,128)}, u32[]{:S(2)}) copy-start(s32[4,24]{1,0:T(4,128)} %param.11) | copy-start | bytes 1156
  8.9 23.3 %copy-start.5 = (s32[4,24]{1,0:T(4,128)S(1)}, s32[4,24]{1,0:T(4,128)}, u32[]{:S(2)}) copy-start(s32[4,24]{1,0:T(4,128)} %param.10) | copy-start | bytes 1156
  9.0 25.2 %copy-start = (bf16[8,256,256]{2,1,0:T(8,128)(2,1)S(1)}, bf16[8,256,256]{2,1,0:T(8,128)(2,1)}, u32[]{:S(2)}) copy-start(bf16[8,256,256]{2,1,0:T(8,128)(2,1)} %near_ref.1) | copy-start | bytes 3145732
  9.0 25.2 %copy-start.2 = (f32[512]{0:T(512)S(1)}, f32[512]{0:T(512)}, u32[]{:S(2)}) copy-start(f32[512]{0:T(512)} %param.9) | copy-start | bytes 6148
  11.8 1.6 %collective-permute-start = (f32[8,8]{1,0:T(8,128)S(1)}, f32[8,8]{1,0:T(8,128)S(1)}, u32[]{:S(2)}, u32[]{:S(2)}) collective-permute-start(f32[8,8]{1,0:T(8,128)S(1)} %convert_reduce_fusion), channel_id=1, source_target_pairs={{0,16},{16,0},{32,48},{48,32},{64,80},{80,64},{96,112},{112,96},{1... | collective-permute-start | bytes 776 | tf_op jit(solution)/shard_map/ppermute | solution.py:277
  13.4 4.0 %collective-permute-start.1 = (f32[8,8]{1,0:T(8,128)S(1)}, f32[8,8]{1,0:T(8,128)S(1)}, u32[]{:S(2)}, u32[]{:S(2)}) collective-permute-start(f32[8,8]{1,0:T(8,128)S(1)} %add.26), channel_id=1, source_target_pairs={{0,64},{16,80},{32,96},{48,112},{64,0},{80,16},{96,32},{112,48},{1... | collective-permute-start | bytes 776 | tf_op jit(solution)/shard_map/ppermute | solution.py:277
  17.4 2.5 %collective-permute-start.2 = (f32[8,8]{1,0:T(8,128)S(1)}, f32[8,8]{1,0:T(8,128)S(1)}, u32[]{:S(2)}, u32[]{:S(2)}) collective-permute-start(f32[8,8]{1,0:T(8,128)S(1)} %add.27), channel_id=1, source_target_pairs={{0,32},{16,48},{32,0},{48,16},{64,96},{80,112},{96,64},{112,80},{1... | collective-permute-start | bytes 776 | tf_op jit(solution)/shard_map/ppermute | solution.py:277
  19.9 4.0 %collective-permute-start.3 = (f32[8,8]{1,0:T(8,128)S(1)}, f32[8,8]{1,0:T(8,128)S(1)}, u32[]{:S(2)}, u32[]{:S(2)}) collective-permute-start(f32[8,8]{1,0:T(8,128)S(1)} %add.28), channel_id=1, source_target_pairs={{0,8},{1,9},{2,10},{3,11},{4,12},{5,13},{6,14},{7,15},{8,0},{9,1},... | collective-permute-start | bytes 776 | tf_op jit(solution)/shard_map/ppermute | solution.py:277
  23.8 2.9 %collective-permute-start.4 = (f32[8,8]{1,0:T(8,128)S(1)}, f32[8,8]{1,0:T(8,128)S(1)}, u32[]{:S(2)}, u32[]{:S(2)}) collective-permute-start(f32[8,8]{1,0:T(8,128)S(1)} %add.29), channel_id=1, source_target_pairs={{0,4},{1,5},{2,6},{3,7},{4,0},{5,1},{6,2},{7,3},{8,12},{9,13},{10,... | collective-permute-start | bytes 776 | tf_op jit(solution)/shard_map/ppermute | solution.py:277
  26.7 4.6 %collective-permute-start.5 = (f32[8,8]{1,0:T(8,128)S(1)}, f32[8,8]{1,0:T(8,128)S(1)}, u32[]{:S(2)}, u32[]{:S(2)}) collective-permute-start(f32[8,8]{1,0:T(8,128)S(1)} %add.30), channel_id=1, source_target_pairs={{0,2},{1,3},{2,0},{3,1},{4,6},{5,7},{6,4},{7,5},{8,10},{9,11},{10,... | collective-permute-start | bytes 776 | tf_op jit(solution)/shard_map/ppermute | solution.py:277
  31.3 2.9 %collective-permute-start.6 = (f32[8,8]{1,0:T(8,128)S(1)}, f32[8,8]{1,0:T(8,128)S(1)}, u32[]{:S(2)}, u32[]{:S(2)}) collective-permute-start(f32[8,8]{1,0:T(8,128)S(1)} %add.31), channel_id=1, source_target_pairs={{0,1},{1,0},{2,3},{3,2},{4,5},{5,4},{6,7},{7,6},{8,9},{9,8},{10,11... | collective-permute-start | bytes 776 | tf_op jit(solution)/shard_map/ppermute | solution.py:277
  68.7 1.1 copy-start.1
Sparse Core Ops, SparseCore 0:
  11.5 109.1 all-gather.1

commit v8 on v5

--- a/solution.py
+++ b/solution.py
@@ -165,9 +165,12 @@
             arrived.at[t, r],
         ).wait()
 
-    def store(t):
+    def store(t, half):
         rows = pl.ds(pl.multiple_of(t * size, size), size)
-        return pltpu.make_async_copy(out_ref.at[t], out_hbm.at[rows, :], stored.at[t])
+        columns = pl.ds(half * size, size)
+        return pltpu.make_async_copy(
+            out_ref.at[t, half], out_hbm.at[rows, columns], stored.at[t, half]
+        )
 
     def multiply(total, unit, terms):
         for n, (left, right) in enumerate(terms):
@@ -222,15 +225,17 @@
 
             multiply(first_sum, 0, terms(0, 0, products))
             multiply(second_sum, 1, terms(0, 1, products) + terms(1, 1, products[3:]))
-            out_ref[t, :, :size] = pltpu.matmul_pop(first_sum)
+            out_ref[t, 0] = pltpu.matmul_pop(first_sum)
+            store(t, 0).start()
             multiply(first_sum, 0, terms(1, 1, products[:3]))
-            out_ref[t, :, size:] = pltpu.matmul_pop(second_sum) + pltpu.matmul_pop(first_sum)
-            store(t).start()
+            out_ref[t, 1] = pltpu.matmul_pop(second_sum) + pltpu.matmul_pop(first_sum)
+            store(t, 1).start()
             return carry
 
         lax.fori_loop(0, tiles, tile_step, 0)
         for t in range(tiles):
-            store(t).wait()
+            for half in range(2):
+                store(t, half).wait()
 
     pl.run_scoped(main, *sums)
 
@@ -250,10 +255,10 @@
             pltpu.VMEM((tiles, slots, size, size), jnp.bfloat16),
             pltpu.VMEM(turned_near.shape, jnp.bfloat16),
             pltpu.VMEM(parts.shape, jnp.bfloat16),
-            pltpu.VMEM((tiles, size, 2 * size), jnp.float32),
+            pltpu.VMEM((tiles, 2, size, size), jnp.float32),
             pltpu.SemaphoreType.DMA((tiles, slots // GROUP)),
             pltpu.SemaphoreType.DMA((2,)),
-            pltpu.SemaphoreType.DMA((tiles,)),
+            pltpu.SemaphoreType.DMA((tiles, 2)),
         ],
         compiler_params=pltpu.CompilerParams(vmem_limit_bytes=63 << 20),
         name="far",

time: 142 us -> 141 us (level)
  no operation moved by 1% of the time
where the time goes in v8:
time: 141 us; the launch traced here: 140 us
  waiting for transfers between devices  57.8 us (41%)
  Pallas kernels  47 us (33%)
  between operations  14.1 us (10%)
  starting transfers between devices  11.3 us (8%)
  local copies, waits for them, and re-layouts  6.11 us (4%)
  other arithmetic  3.68 us (3%)
    all_gather x1, waiting for transfers between devices, shards(): lax.all_gather(own, ('col', 'row'), axis=0, tiled=True)  51.1 us
    pallas_call x1, Pallas kernels, lead(): pl.pallas_call(lead_kernel, out_shape=(jax.ShapeDtypeStruct((whole, whole...  34.6 us
    pallas_call x1, Pallas kernels, far(): pl.pallas_call(functools.partial(far_kernel, slots, sums), out_shape=jax....  12.4 us
    ppermute x7, starting transfers between devices, total_pairs(): lax.ppermute(value, axis, [(i, i ^ bit) for i in range(size)])  11.3 us
    ppermute x7, waiting for transfers between devices, total_pairs(): lax.ppermute(value, axis, [(i, i ^ bit) for i in range(size)])  6.62 us
  transfers between devices with their start and end apart: 8, of which 5 were waited for; matrix products, arithmetic and copies ran while one was open for 5% of the time, Pallas kernels for 25%

profile of v8, /device:TPU:7, one launch (start us, length us, event | category | flops | bytes accessed | tf_op | source)
XLA Modules:
  0.0 139.9 jit_solution(17832989291164093555)
XLA Ops:
  7.2 0.0 all-gather.2.cloned.1.call-start
  7.2 1.7 %constant_dynamic-slice_fusion = bf16[512,256]{1,0:T(8,128)(2,1)} fusion(bf16[4096,256]{1,0:T(8,128)(2,1)} %bitcast.9, s32[]{:T(128)S(6)} %select_n.12), kind=kLoop, calls=%fused_computation.8 | loop fusion | bytes 524292 | tf_op jit(solution)/shard_map/dynamic_slice | solution.py:292
  8.9 0.0 all-gather.2.cloned.1.call-update
  8.9 0.7 iota_compare_fusion.2
  9.6 0.7 iota_compare_fusion
  10.4 0.1 convert_reduce_fusion
  10.5 0.8 collective-permute-start
  11.2 0.8 collective-permute-done
  12.0 1.1 collective-permute-start.1
  13.2 2.8 %collective-permute-done.1 = f32[8,8]{1,0:T(8,128)S(1)} collective-permute-done((f32[8,8]{1,0:T(8,128)S(1)}, f32[8,8]{1,0:T(8,128)S(1)}, u32[]{:S(2)}, u32[]{:S(2)}) %collective-permute-start.1) | collective-permute-done | bytes 288 | tf_op jit(solution)/shard_map/ppermute | solution.py:282
  16.0 0.5 collective-permute-start.2
  16.6 1.9 %collective-permute-done.2 = f32[8,8]{1,0:T(8,128)S(1)} collective-permute-done((f32[8,8]{1,0:T(8,128)S(1)}, f32[8,8]{1,0:T(8,128)S(1)}, u32[]{:S(2)}, u32[]{:S(2)}) %collective-permute-start.2) | collective-permute-done | bytes 288 | tf_op jit(solution)/shard_map/ppermute | solution.py:282
  18.5 2.9 %collective-permute-start.3 = (f32[8,8]{1,0:T(8,128)S(1)}, f32[8,8]{1,0:T(8,128)S(1)}, u32[]{:S(2)}, u32[]{:S(2)}) collective-permute-start(f32[8,8]{1,0:T(8,128)S(1)} %add.28), channel_id=1, source_target_pairs={{0,8},{1,9},{2,10},{3,11},{4,12},{5,13},{6,14},{7,15},{8,0},{9,1},... | collective-permute-start | bytes 776 | tf_op jit(solution)/shard_map/ppermute | solution.py:282
  21.4 1.0 collective-permute-done.3
  22.4 1.3 collective-permute-start.4
  23.7 0.8 broadcast_select_fusion.1
  24.5 0.7 copy.12
  25.3 0.0 collective-permute-done.4
  25.3 3.7 %collective-permute-start.5 = (f32[8,8]{1,0:T(8,128)S(1)}, f32[8,8]{1,0:T(8,128)S(1)}, u32[]{:S(2)}, u32[]{:S(2)}) collective-permute-start(f32[8,8]{1,0:T(8,128)S(1)} %add.30), channel_id=1, source_target_pairs={{0,2},{1,3},{2,0},{3,1},{4,6},{5,7},{6,4},{7,5},{8,10},{9,11},{10,... | collective-permute-start | bytes 776 | tf_op jit(solution)/shard_map/ppermute | solution.py:282
  28.9 1.3 pad_add_fusion.info_ref
  30.3 0.0 collective-permute-done.5
  30.3 0.0 copy-start
  30.3 0.0 copy-start.2
  30.3 0.9 collective-permute-start.6
  31.2 1.5 %copy.11 = bf16[8,256,256]{1,2,0:T(8,128)(2,1)S(1)} copy(bf16[8,256,256]{2,1,0:T(8,128)(2,1)} %near_ref.1) | data formatting | bytes 2097152 | tf_op args[1]
  32.7 1.1 concatenate.7.turned_hbm
  33.8 0.0 collective-permute-done.6
  33.8 0.0 copy-done
  33.8 0.0 copy-done.2
  33.8 34.6 %lead.1 = (f32[512,512]{1,0:T(8,128)}, bf16[3,2,2,256,256]{4,3,2,1,0:T(8,128)(2,1)S(1)}) custom-call(f32[8,8]{1,0:T(8,128)S(1)} %add.32.pairs_ref, bf16[8,256,256]{2,1,0:T(8,128)(2,1)S(1)} %copy-done, bf16[8,256,256]{2,1,0:T(8,128)(2,1)S(1)} %bitcast.6, f32[1,512]{1,0:T(1,128)S(1)} %bitcast.7), custom_call_target="tpu_custom_call" | custom-call | tf_op jit(solution)/shard_map/lead/pallas_call | solution.py:120
  68.4 0.0 copy-start.1
  68.4 1.1 copy-done.1
  69.6 51.1 %all-gather.2.cloned.1.call-done = bf16[65536,256]{1,0:T(8,128)(2,1)} async-done(((bf16[512,256]{1,0:T(8,128)(2,1)}), bf16[65536,256]{1,0:T(8,128)(2,1)}) %all-gather.2.cloned.1.call-update) | async-done | bytes 33554448 | tf_op jit(solution)/shard_map/all_gather | solution.py:295
  120.7 12.4 %far.1 = f32[1024,512]{1,0:T(8,128)} custom-call(s32[4,73]{1,0:T(4,128)} %pad_add_fusion.info_ref, bf16[256,256,256]{2,1,0:T(8,128)(2,1)} %bitcast.8, bf16[9,256,256]{2,1,0:T(8,128)(2,1)} %concatenate.7.turned_hbm, bf16[3,2,2,256,256]{4,3,2,1,0:T(8,128)(2,1)} %copy-done.1), custom_call_target="tpu_custom_call" | custom-call | tf_op jit(solution)/shard_map/far/pallas_call | solution.py:249
  (7 shorter events, 0.0 us)
Async XLA Ops:
  7.2 113.5 %all-gather.2.cloned.1.call-start = ((), (), s32[]{:S(2)}) async-start(), calls=%async_computation | async-start | bytes 33816576 | tf_op jit(solution)/shard_map/all_gather | solution.py:295
  10.5 1.6 %collective-permute-start = (f32[8,8]{1,0:T(8,128)S(1)}, f32[8,8]{1,0:T(8,128)S(1)}, u32[]{:S(2)}, u32[]{:S(2)}) collective-permute-start(f32[8,8]{1,0:T(8,128)S(1)} %convert_reduce_fusion), channel_id=1, source_target_pairs={{0,16},{16,0},{32,48},{48,32},{64,80},{80,64},{96,112},{112,96},{1... | collective-permute-start | bytes 776 | tf_op jit(solution)/shard_map/ppermute | solution.py:282
  12.0 4.0 %collective-permute-start.1 = (f32[8,8]{1,0:T(8,128)S(1)}, f32[8,8]{1,0:T(8,128)S(1)}, u32[]{:S(2)}, u32[]{:S(2)}) collective-permute-start(f32[8,8]{1,0:T(8,128)S(1)} %add.26), channel_id=1, source_target_pairs={{0,64},{16,80},{32,96},{48,112},{64,0},{80,16},{96,32},{112,48},{1... | collective-permute-start | bytes 776 | tf_op jit(solution)/shard_map/ppermute | solution.py:282
  16.0 2.5 %collective-permute-start.2 = (f32[8,8]{1,0:T(8,128)S(1)}, f32[8,8]{1,0:T(8,128)S(1)}, u32[]{:S(2)}, u32[]{:S(2)}) collective-permute-start(f32[8,8]{1,0:T(8,128)S(1)} %add.27), channel_id=1, source_target_pairs={{0,32},{16,48},{32,0},{48,16},{64,96},{80,112},{96,64},{112,80},{1... | collective-permute-start | bytes 776 | tf_op jit(solution)/shard_map/ppermute | solution.py:282
  18.5 4.0 %collective-permute-start.3 = (f32[8,8]{1,0:T(8,128)S(1)}, f32[8,8]{1,0:T(8,128)S(1)}, u32[]{:S(2)}, u32[]{:S(2)}) collective-permute-start(f32[8,8]{1,0:T(8,128)S(1)} %add.28), channel_id=1, source_target_pairs={{0,8},{1,9},{2,10},{3,11},{4,12},{5,13},{6,14},{7,15},{8,0},{9,1},... | collective-permute-start | bytes 776 | tf_op jit(solution)/shard_map/ppermute | solution.py:282
  22.4 2.8 %collective-permute-start.4 = (f32[8,8]{1,0:T(8,128)S(1)}, f32[8,8]{1,0:T(8,128)S(1)}, u32[]{:S(2)}, u32[]{:S(2)}) collective-permute-start(f32[8,8]{1,0:T(8,128)S(1)} %add.29), channel_id=1, source_target_pairs={{0,4},{1,5},{2,6},{3,7},{4,0},{5,1},{6,2},{7,3},{8,12},{9,13},{10,... | collective-permute-start | bytes 776 | tf_op jit(solution)/shard_map/ppermute | solution.py:282
  25.3 5.0 %collective-permute-start.5 = (f32[8,8]{1,0:T(8,128)S(1)}, f32[8,8]{1,0:T(8,128)S(1)}, u32[]{:S(2)}, u32[]{:S(2)}) collective-permute-start(f32[8,8]{1,0:T(8,128)S(1)} %add.30), channel_id=1, source_target_pairs={{0,2},{1,3},{2,0},{3,1},{4,6},{5,7},{6,4},{7,5},{8,10},{9,11},{10,... | collective-permute-start | bytes 776 | tf_op jit(solution)/shard_map/ppermute | solution.py:282
  30.3 3.5 %copy-start = (bf16[8,256,256]{2,1,0:T(8,128)(2,1)S(1)}, bf16[8,256,256]{2,1,0:T(8,128)(2,1)}, u32[]{:S(2)}) copy-start(bf16[8,256,256]{2,1,0:T(8,128)(2,1)} %near_ref.1) | copy-start | bytes 3145732
  30.3 3.5 %copy-start.2 = (f32[512]{0:T(512)S(1)}, f32[512]{0:T(512)}, u32[]{:S(2)}) copy-start(f32[512]{0:T(512)} %param.9) | copy-start | bytes 6148
  30.3 3.5 %collective-permute-start.6 = (f32[8,8]{1,0:T(8,128)S(1)}, f32[8,8]{1,0:T(8,128)S(1)}, u32[]{:S(2)}, u32[]{:S(2)}) collective-permute-start(f32[8,8]{1,0:T(8,128)S(1)} %add.31), channel_id=1, source_target_pairs={{0,1},{1,0},{2,3},{3,2},{4,5},{5,4},{6,7},{7,6},{8,9},{9,8},{10,11... | collective-permute-start | bytes 776 | tf_op jit(solution)/shard_map/ppermute | solution.py:282
  68.4 1.1 copy-start.1
Sparse Core Ops, SparseCore 0:
  11.5 109.0 all-gather.1
